TPU v7x, 32 devices: a whole 2x2x4 slice. The times are simulated.
32 devices in a mesh: groups: 2 (over y), dp: 2 (over x), expert: 8 (over z, core).
Axes of the slice: x: 2, y: 2, z: 4, core: 2. Of those that a mesh axis runs over, the one named last changes fastest.
Arguments:
- tokens: bfloat16 [4096, 2048], P(('groups', 'dp', 'expert')), parts along dimension 0, may hold values from -6 to 6
- routes: int32 [4096, 4], P(('groups', 'dp', 'expert')), parts along dimension 0, may hold values from 0 to 7, all different within a row; in each aligned block of 128 rows (0 to 127, 128 to 255, ...) at most 128 rows name the same one
- w_gate: bfloat16 [16, 2048, 512], P(('groups', 'expert')), parts along dimension 0, may hold values from -0.125 to 0.125
- w_up: bfloat16 [16, 2048, 512], P(('groups', 'expert')), parts along dimension 0, may hold values from -0.125 to 0.125
Outputs:
- r_factor: float32 [16, 512, 512], P(('groups', 'expert'), 'dp'), parts along dimension 0
There are 2 independent parts, one for each index of `groups`. A program takes and returns all parts, laid end to end along the dimension named above; each array names one. Nothing has to cross between parts.
Inputs may be any that keep to these rules, and one draw needn't show every extreme that they name: `routes`: each row names 4 different experts. In each aligned block of 128 rows (the tokens of one device) no expert is named by more than 128 rows, and in some block some expert is named by exactly 128 rows.
All inputs are finite; a program needn't handle non-finite values.
Results may differ from a plain program's by a relative error of at most 0.0027.
Values may be sent and summed in bfloat16 or wider, within the bound.
No kernel may reach another device: no remote copies, remote signals or barrier semaphores. Data moves between devices by JAX's collectives and lax.ppermute only.
A program may use at most 64 MiB of HBM per device.

v0:
```python
import jax
import jax.numpy as jnp
from jax import lax
from jax.sharding import PartitionSpec as P

RIDGE = 0.05


def body(tokens, routes, w_gate, w_up):
    owners = lax.axis_size("expert")
    data_ranks = lax.axis_size("dp")
    experts = w_gate.shape[0] * owners
    factor_width = w_gate.shape[2]
    model_width = tokens.shape[1]
    tok_rows, top_count = routes.shape
    capacity = min(tok_rows, 2 * tok_rows * top_count // experts)
    assigned = routes.reshape(-1)
    onehot = (assigned[:, None] == jnp.arange(experts, dtype=jnp.int32)[None, :]).astype(jnp.int32)
    position = jnp.sum(jnp.cumsum(onehot, axis=0) * onehot, axis=1) - 1
    target = assigned * capacity + position
    anchor = jnp.arange(tok_rows * top_count, dtype=jnp.int32) // top_count
    source_row = jnp.zeros((experts * capacity,), jnp.int32).at[target].set(anchor)
    filled = jnp.zeros((experts * capacity,), jnp.int32).at[target].set(1)
    outbox = jnp.where(filled[:, None] > 0, tokens[source_row], jnp.zeros((), tokens.dtype))
    outbox = outbox.reshape(experts, capacity, model_width)
    gate_matrix = w_gate[0]
    up_matrix = w_up[0]
    arrived = lax.all_to_all(outbox, "expert", split_axis=0, concat_axis=0, tiled=True)
    flattened = arrived.reshape(-1, model_width)
    gate_proj = jnp.dot(flattened, gate_matrix, preferred_element_type=jnp.float32)
    up_proj = jnp.dot(flattened, up_matrix, preferred_element_type=jnp.float32)
    hidden = (jax.nn.silu(gate_proj) * up_proj).astype(jnp.bfloat16)
    hidden = hidden.reshape(arrived.shape[0], arrived.shape[1], factor_width)
    hidden = hidden.reshape(-1, factor_width)
    gram_local = lax.dot_general(
        hidden, hidden, (((0,), (0,)), ((), ())), preferred_element_type=jnp.float32
    )
    rows_mean = data_ranks * tok_rows * top_count
    block_rows = factor_width // data_ranks
    my_rank = lax.axis_index("dp")
    summed = lax.psum(gram_local, "dp")
    regular = summed / rows_mean + RIDGE * jnp.eye(factor_width, dtype=jnp.float32)
    factor = jnp.linalg.cholesky(regular).T
    my_rows = lax.dynamic_slice_in_dim(factor, my_rank * block_rows, block_rows, 0)
    return my_rows.reshape(1, block_rows, factor_width)


def solution(mesh):
    in_specs = (
        P(("groups", "dp", "expert"), None),
        P(("groups", "dp", "expert"), None),
        P(("groups", "expert"), None, None),
        P(("groups", "expert"), None, None),
    )
    out_specs = P(("groups", "expert"), "dp", None)
    return jax.shard_map(body, mesh=mesh, in_specs=in_specs, out_specs=out_specs, check_vma=False)
```

profile of v0, /device:TPU:0, one launch (start us, length us, event | category | flops | bytes accessed | tf_op | source)
XLA Modules:
  0.0 292.4 jit_solution(2657920740436624957)
XLA Ops:
  10.1 2.4 scatter_custom_fusion.1
  12.6 2.4 scatter_custom_fusion
  15.1 9.9 %gather_fusion = bf16[1024,2048]{1,0:T(8,128)(2,1)} fusion(bf16[128,2048]{1,0:T(8,128)(2,1)} %param.4, s32[1024]{0:T(1024)S(1)} %fusion.26), kind=kCustom, calls=%fused_computation | custom fusion | bytes 8392704 | tf_op jit(solution)/shard_map/gather | solution.py:24
  25.0 2.5 broadcast_select_fusion
  27.6 100.1 %all_to_all.5 = bf16[8,128,2048]{2,1,0:T(8,128)(2,1)S(1)} all-to-all(bf16[8,128,2048]{2,1,0:T(8,128)(2,1)S(1)} %broadcast_select_fusion), channel_id=1, replica_groups=mesh['groups'=2,'dp'=2,'expert'=8] {'expert'}, dimensions={0} | all-to-all | bytes 8388608 | tf_op jit(solution)/shard_map/all_to_all | solution.py:28
  127.7 1.9 copy-done.2
  129.6 3.7 %fusion = f32[1024,512]{1,0:T(8,128)} fusion(bf16[1024,2048]{1,0:T(8,128)(2,1)S(1)} %bitcast.49, bf16[1,2048,512]{2,1,0:T(8,128)(2,1)S(1)} %copy-done), kind=kOutput, calls=%fused_computation.4 | convolution fusion | flops 2147483648 | bytes 8388608 | tf_op jit(solution)/shard_map/dot_general | solution.py:31
  133.3 12.2 %fusion.7 = f32[512,512]{0,1:T(8,128)} fusion(f32[1024,512]{1,0:T(8,128)} %fusion, bf16[1024,2048]{1,0:T(8,128)(2,1)} %bitcast.50, bf16[1,2048,512]{2,1,0:T(8,128)(2,1)} %param.6), kind=kOutput, calls=%fused_computation.14 | convolution fusion | flops 2687500288 | bytes 9437184 | tf_op jit(solution)/shard_map/dot_general | solution.py:35
  145.6 39.2 %all-reduce.3.cloned.1.call-done = f32[512,512]{0,1:T(8,128)} async-done(((f32[512,512]{0,1:T(8,128)}), f32[512,512]{0,1:T(8,128)}) %all-reduce.3.cloned.1.call-update) | async-done | bytes 1048592 | tf_op jit(solution)/shard_map/psum | solution.py:41
  184.7 2.4 select_add_fusion
  187.1 2.6 copy.18
  189.7 1.5 fusion.9
  192.2 11.7 %cholesky.103 = f32[128,128]{1,0:T(8,128)S(1)} custom-call(f32[128,128]{1,0:T(8,128)S(1)} %cholesky.263), custom_call_target="Cholesky" | custom-call | tf_op jit(solution)/shard_map/jit(cholesky)/cholesky | solution.py:43
  203.9 10.0 %custom-call.27 = f32[1,128,128]{1,2,0:T(8,128)S(1)} custom-call(f32[1,128,128]{2,1,0:T(8,128)S(1)} %get-tuple-element.10), custom_call_target="InvertDiagBlocksLowerTriangular" | custom-call | tf_op jit(solution)/shard_map/jit(cholesky)/cholesky | solution.py:43
  214.0 1.2 fusion.15
  215.2 1.3 convolution_subtract_fusion
  216.5 11.7 %cholesky.215 = f32[128,128]{1,0:T(8,128)S(1)} custom-call(f32[128,128]{1,0:T(8,128)S(1)} %cholesky.267), custom_call_target="Cholesky" | custom-call | tf_op jit(solution)/shard_map/jit(cholesky)/cholesky | solution.py:43
  229.8 10.4 %custom-call.28 = f32[1,128,128]{1,2,0:T(8,128)} custom-call(f32[1,128,128]{2,1,0:T(8,128)S(1)} %get-tuple-element.8), custom_call_target="InvertDiagBlocksLowerTriangular" | custom-call | tf_op jit(solution)/shard_map/jit(cholesky)/cholesky | solution.py:43
  242.1 1.2 convolution_dynamic-update-slice_fusion
  243.2 1.5 convolution_subtract_fusion.1
  244.8 11.7 %cholesky.236 = f32[128,128]{1,0:T(8,128)S(1)} custom-call(f32[128,128]{1,0:T(8,128)S(1)} %cholesky.272), custom_call_target="Cholesky" | custom-call | tf_op jit(solution)/shard_map/jit(cholesky)/cholesky | solution.py:43
  256.6 10.0 %custom-call.29 = f32[1,128,128]{1,2,0:T(8,128)S(1)} custom-call(f32[1,128,128]{2,1,0:T(8,128)S(1)} %get-tuple-element.6), custom_call_target="InvertDiagBlocksLowerTriangular" | custom-call | tf_op jit(solution)/shard_map/jit(cholesky)/cholesky | solution.py:43
  266.9 1.3 convolution_subtract_fusion.2
  268.3 11.7 %cholesky.253 = f32[128,128]{1,0:T(8,128)S(1)} custom-call(f32[128,128]{1,0:T(8,128)S(1)} %convolution_subtract_fusion.2), custom_call_target="Cholesky" | custom-call | tf_op jit(solution)/shard_map/jit(cholesky)/cholesky | solution.py:43
  (49 shorter events, 11.5 us)
Async XLA Ops:
  6.5 123.1 %copy-start = (bf16[1,2048,512]{2,1,0:T(8,128)(2,1)S(1)}, bf16[1,2048,512]{2,1,0:T(8,128)(2,1)}, u32[]{:S(2)}) copy-start(bf16[1,2048,512]{2,1,0:T(8,128)(2,1)} %param.7) | copy-start | bytes 6291460
  6.5 178.2 %all-reduce.3.cloned.1.call-start = ((), (), s32[]{:S(2)}) async-start(), calls=%async_computation.1 | async-start | bytes 2097152 | tf_op jit(solution)/shard_map/psum | solution.py:41
  127.7 1.9 copy-start.2
  184.7 5.0 %copy-start.1 = (f32[512,512]{0,1:T(8,128)S(1)}, f32[512,512]{0,1:T(8,128)}, u32[]{:S(2)}) copy-start(f32[512,512]{0,1:T(8,128)} %all-reduce.3.cloned.1.call-done) | copy-start | bytes 3145732
  191.2 1.0 copy-start.3
Sparse Core Ops, SparseCore 0:
  145.7 38.9 all-reduce.2
where the time goes:
time: 293 us; the launch traced here: 292 us
  blocking collectives  100 us (34%)
  other arithmetic  88.8 us (30%)
  waiting for transfers between devices  39.2 us (13%)
  local copies, waits for them, and re-layouts  25.6 us (9%)
  matrix products  22.7 us (8%)
  between operations  16.1 us (5%)
    all_to_all x1, blocking collectives, body(): lax.all_to_all(outbox, 'expert', split_axis=0, concat_axis=0, tiled=True)  100 us
    another operation x14, other arithmetic, body(): factor = jnp.linalg.cholesky(regular).T  79.4 us
    psum x1, waiting for transfers between devices, body(): summed = lax.psum(gram_local, 'dp')  39.2 us
    dot_general x1, matrix products, body(): lax.dot_general(hidden, hidden, (((0,), (0,)), ((), ())), preferred_eleme...  12.2 us
    gather x1, local copies, waits for them, and re-layouts, body(): tokens[source_row]  9.94 us
    another operation x6, matrix products, body(): factor = jnp.linalg.cholesky(regular).T  6.75 us
  transfers between devices with their start and end apart: 1, of which 1 were waited for; matrix products, arithmetic and copies ran while one was open for 0% of the time, Pallas kernels for 0%

commit v1 on v0

v1 whole, which is shorter than its diff:
```python
import functools

import jax
import jax.numpy as jnp
from jax import lax
from jax.experimental import pallas as pl
from jax.experimental.pallas import tpu as pltpu
from jax.sharding import PartitionSpec as P

RIDGE = 0.05
CORES = 2


def hidden_gram_kernel(own_ref, other_ref, member_ref, gate_ref, up_ref, *rest):
    first = len(rest) == 2
    gram_in_ref = None if first else rest[0]
    gram_ref, hidden_ref = rest[-2:]
    step = pl.program_id(0)
    rows = own_ref.shape[0]
    width = gate_ref.shape[1]
    gate_block = gate_ref[...]
    up_block = up_ref[...]
    x = jnp.concatenate([own_ref[...], other_ref[...]], axis=0)
    gate = jnp.dot(x, gate_block, preferred_element_type=jnp.float32)
    up = jnp.dot(x, up_block, preferred_element_type=jnp.float32)
    value = gate / (1.0 + jnp.exp(-gate)) * up
    value = jnp.where(member_ref[...] > 0, value, 0.0)
    hidden_ref[:, pl.ds(pl.multiple_of(step * width, width), width)] = value.astype(jnp.bfloat16)

    @pl.when(step == pl.num_programs(0) - 1)
    def _():
        h = hidden_ref[...]
        gram = lax.dot_general(h, h, (((0,), (0,)), ((), ())), preferred_element_type=jnp.float32)
        if first:
            gram_ref[...] = gram
        else:
            gram_ref[...] = gram_in_ref[...] + gram


def hidden_gram(own, other, member, slot, gate_w, up_w, gram=None, width=256):
    rows, model = own.shape
    hw = gate_w.shape[1]
    whole = lambda i: (0, 0)
    in_specs = [
        pl.BlockSpec((rows, model), whole),
        pl.BlockSpec((rows, model), whole),
        pl.BlockSpec((2 * rows, 1), lambda i: (slot, 0)),
        pl.BlockSpec((model, width), lambda i: (0, i)),
        pl.BlockSpec((model, width), lambda i: (0, i)),
    ]
    args = [own, other, member, gate_w, up_w]
    aliases = {}
    if gram is not None:
        in_specs.append(pl.BlockSpec((hw, hw), whole))
        args.append(gram)
        aliases = {5: 0}
    return pl.pallas_call(
        hidden_gram_kernel,
        grid=(hw // width,),
        in_specs=in_specs,
        out_specs=pl.BlockSpec((hw, hw), whole),
        out_shape=jax.ShapeDtypeStruct((hw, hw), jnp.float32),
        scratch_shapes=[pltpu.VMEM((2 * rows, hw), jnp.bfloat16)],
        input_output_aliases=aliases,
        compiler_params=pltpu.CompilerParams(dimension_semantics=("arbitrary",)),
        cost_estimate=pl.CostEstimate(
            flops=2 * 2 * rows * model * 2 * hw + 2 * 2 * rows * hw * hw,
            bytes_accessed=2 * (2 * rows * model + 2 * model * hw) + 4 * hw * hw,
            transcendentals=2 * rows * hw,
        ),
        name=f"hidden_gram_{slot}",
    )(*args)


def shifted(pairs):
    return [(s * CORES + c, d * CORES + c) for s, d in pairs for c in range(CORES)]


def gather_grams(tokens, routes, gate_w, up_w):
    owners = lax.axis_size("expert")
    chips = owners // CORES
    me = lax.axis_index("expert")
    move = lambda x, pairs: lax.ppermute(x, "expert", pairs)
    swap = [(e, e ^ 1) for e in range(owners)]
    ring = lambda s: shifted([(z, (z + s) % chips) for z in range(chips)])

    direct = {}
    if chips == 4:
        direct[1] = move(tokens, ring(1))
        direct[3] = move(tokens, ring(-1))
        far = move(tokens, shifted([(0, 2), (3, 1)]))
        on_up = move(direct[1], shifted([(2, 3)]))
        on_down = move(direct[3], shifted([(1, 0)]))
        direct[2] = far + on_up + on_down
    else:
        for s in range(1, chips):
            direct[s] = move(tokens, ring(s))

    names = routes.T
    pair = jnp.concatenate([names, move(names, swap)], axis=0)
    named = [pair] + [move(pair, ring(s)) for s in range(1, chips)]
    named = jnp.stack(named).reshape(chips, CORES, routes.shape[1], routes.shape[0])
    member = jnp.any(named == me, axis=2).astype(jnp.float32).reshape(-1, 1)

    gram = hidden_gram(tokens, move(tokens, swap), member, 0, gate_w, up_w)
    order = [1, 3, 2] if chips == 4 else list(range(1, chips))
    for s in order:
        gram = hidden_gram(direct[s], move(direct[s], swap), member, s, gate_w, up_w, gram)
    return gram


def packed_grams(tokens, routes, gate_w, up_w, capacity):
    owners = lax.axis_size("expert")
    experts = owners
    model_width = tokens.shape[1]
    tok_rows, top_count = routes.shape
    assigned = routes.reshape(-1)
    onehot = (assigned[:, None] == jnp.arange(experts, dtype=jnp.int32)[None, :]).astype(jnp.int32)
    position = jnp.sum(jnp.cumsum(onehot, axis=0) * onehot, axis=1) - 1
    target = assigned * capacity + position
    anchor = jnp.arange(tok_rows * top_count, dtype=jnp.int32) // top_count
    source_row = jnp.zeros((experts * capacity,), jnp.int32).at[target].set(anchor)
    filled = jnp.zeros((experts * capacity,), jnp.int32).at[target].set(1)
    outbox = jnp.where(filled[:, None] > 0, tokens[source_row], jnp.zeros((), tokens.dtype))
    outbox = outbox.reshape(experts, capacity, model_width)
    arrived = lax.all_to_all(outbox, "expert", split_axis=0, concat_axis=0, tiled=True)
    flattened = arrived.reshape(-1, model_width)
    gate_proj = jnp.dot(flattened, gate_w, preferred_element_type=jnp.float32)
    up_proj = jnp.dot(flattened, up_w, preferred_element_type=jnp.float32)
    hidden = (jax.nn.silu(gate_proj) * up_proj).astype(jnp.bfloat16)
    return lax.dot_general(hidden, hidden, (((0,), (0,)), ((), ())), preferred_element_type=jnp.float32)


def body(tokens, routes, w_gate, w_up):
    owners = lax.axis_size("expert")
    data_ranks = lax.axis_size("dp")
    experts = w_gate.shape[0] * owners
    factor_width = w_gate.shape[2]
    tok_rows, top_count = routes.shape
    capacity = min(tok_rows, 2 * tok_rows * top_count // experts)
    gate_w, up_w = w_gate[0], w_up[0]
    if tok_rows * owners <= experts * capacity and owners % CORES == 0:
        gram_local = gather_grams(tokens, routes, gate_w, up_w)
    else:
        gram_local = packed_grams(tokens, routes, gate_w, up_w, capacity)
    rows_mean = data_ranks * tok_rows * top_count
    return finish(gram_local, rows_mean, data_ranks, factor_width)


def finish(gram_local, rows_mean, data_ranks, factor_width):
    block_rows = factor_width // data_ranks
    my_rank = lax.axis_index("dp")
    summed = gram_local
    for s in range(1, data_ranks):
        summed = summed + lax.ppermute(gram_local, "dp", [(r, (r + s) % data_ranks) for r in range(data_ranks)])
    regular = summed / rows_mean + RIDGE * jnp.eye(factor_width, dtype=jnp.float32)
    factor = jnp.linalg.cholesky(regular).T
    my_rows = lax.dynamic_slice_in_dim(factor, my_rank * block_rows, block_rows, 0)
    return my_rows.reshape(1, block_rows, factor_width)


def solution(mesh):
    in_specs = (
        P(("groups", "dp", "expert"), None),
        P(("groups", "dp", "expert"), None),
        P(("groups", "expert"), None, None),
        P(("groups", "expert"), None, None),
    )
    out_specs = P(("groups", "expert"), "dp", None)
    return jax.shard_map(body, mesh=mesh, in_specs=in_specs, out_specs=out_specs, check_vma=False)
```

time: 293 us -> 195 us (0.67)
  blocking collectives: 100 us -> 0 us
  waiting for transfers between devices: 39.2 us -> 69.2 us
  matrix products: 22.7 us -> 2.33 us
  Pallas kernels: 0 us -> 19.8 us
  local copies, waits for them, and re-layouts: 25.6 us -> 6 us
  starting transfers between devices: 0.01 us -> 15 us
  between operations: 16.1 us -> 2.84 us
  other arithmetic: 88.8 us -> 80 us
    all_to_all x1 -> x0, blocking collectives: 100 us -> none  [body(): lax.all_to_all(outbox, 'expert', split_axis=0, concat_axis=0, tiled=True)]
    ppermute x0 -> x14, waiting for transfers between devices: none -> 69.2 us  [the longest x13 48.6 us: gather_grams(): move = lambda x, pairs: lax.ppermute(x, 'expert', pairs)]
    psum x1 -> x0, waiting for transfers between devices: 39.2 us -> none  [body(): summed = lax.psum(gram_local, 'dp')]
    pallas_call x0 -> x4, Pallas kernels: none -> 19.8 us  [hidden_gram(): pl.pallas_call(hidden_gram_kernel, grid=(hw // width,), in_specs=in_specs...]
    dot_general x2 -> x0, matrix products: 15.9 us -> none  [the longest x1 12.2 us: body(): lax.dot_general(hidden, hidden, (((0,), (0,)), ((), ())), preferred_eleme...]
    ppermute x0 -> x14, starting transfers between devices: none -> 15 us  [the longest x13 13.4 us: gather_grams(): move = lambda x, pairs: lax.ppermute(x, 'expert', pairs)]
    gather x1 -> x0, local copies, waits for them, and re-layouts: 9.94 us -> none  [body(): tokens[source_row]]
    scatter x2 -> x0, local copies, waits for them, and re-layouts: 4.89 us -> none  [the longest x1 2.45 us: body(): jnp.zeros((experts * capacity,), jnp.int32).at[target].set(anchor)]
  transfers between devices with their start and end apart: 1 -> 14, of which waited for: 1 -> 9; matrix products, arithmetic and copies ran while one was open for 0% -> 1% of each run, Pallas kernels for 0% -> 8%
where the time goes in v1:
time: 195 us
  other arithmetic  80 us (41%)
  waiting for transfers between devices  69.2 us (35%)
  Pallas kernels  19.8 us (10%)
  starting transfers between devices  15 us (8%)
  local copies, waits for them, and re-layouts  6 us (3%)
  between operations  2.84 us (1%)
  matrix products  2.33 us (1%)
    another operation x14, other arithmetic, finish(): factor = jnp.linalg.cholesky(regular).T  78.6 us
    ppermute x13, waiting for transfers between devices, gather_grams(): move = lambda x, pairs: lax.ppermute(x, 'expert', pairs)  48.6 us
    ppermute x1, waiting for transfers between devices, finish(): lax.ppermute(gram_local, 'dp', [(r, (r + s) % data_ranks) for r in range(...  20.5 us
    pallas_call x4, Pallas kernels, hidden_gram(): pl.pallas_call(hidden_gram_kernel, grid=(hw // width,), in_specs=in_specs...  19.8 us
    ppermute x13, starting transfers between devices, gather_grams(): move = lambda x, pairs: lax.ppermute(x, 'expert', pairs)  13.4 us
  transfers between devices with their start and end apart: 14, of which 9 were waited for; matrix products, arithmetic and copies ran while one was open for 1% of the time, Pallas kernels for 8%

profile of v1, /device:TPU:0, one launch (start us, length us, event | category | flops | bytes accessed | tf_op | source)
XLA Modules:
  0.0 195.2 jit_solution(11947892593787962412)
XLA Ops:
  0.0 3.1 %collective-permute-start.1 = (bf16[128,2048]{1,0:T(8,128)(2,1)}, bf16[128,2048]{1,0:T(8,128)(2,1)S(1)}, u32[]{:S(2)}, u32[]{:S(2)}) collective-permute-start(bf16[128,2048]{1,0:T(8,128)(2,1)} %own_ref.1), channel_id=1, source_target_pairs={{0,2},{1,3},{2,4},{3,5},{4,6},{5,7},{6,0},{7,1},{8,10},{9,11},{10,... | collective-permute-start | bytes 1572872 | tf_op jit(solution)/shard_map/ppermute | solution.py:83
  3.1 2.1 %collective-permute-start.3 = (bf16[128,2048]{1,0:T(8,128)(2,1)}, bf16[128,2048]{1,0:T(8,128)(2,1)S(1)}, u32[]{:S(2)}, u32[]{:S(2)}) collective-permute-start(bf16[128,2048]{1,0:T(8,128)(2,1)} %own_ref.1), channel_id=1, source_target_pairs={{0,6},{1,7},{2,0},{3,1},{4,2},{5,3},{6,4},{7,5},{8,14},{9,15},{10,... | collective-permute-start | bytes 1572872 | tf_op jit(solution)/shard_map/ppermute | solution.py:83
  5.1 2.9 %collective-permute-start = (bf16[128,2048]{1,0:T(8,128)(2,1)}, bf16[128,2048]{1,0:T(8,128)(2,1)S(1)}, u32[]{:S(2)}, u32[]{:S(2)}) collective-permute-start(bf16[128,2048]{1,0:T(8,128)(2,1)} %own_ref.1), channel_id=1, source_target_pairs={{0,4},{1,5},{6,2},{7,3},{8,12},{9,13},{14,10},{15,11},{16,20},{17,... | collective-permute-start | bytes 1572872 | tf_op jit(solution)/shard_map/ppermute | solution.py:83
  8.0 10.1 %collective-permute-done.1.own_ref = bf16[128,2048]{1,0:T(8,128)(2,1)S(1)} collective-permute-done((bf16[128,2048]{1,0:T(8,128)(2,1)}, bf16[128,2048]{1,0:T(8,128)(2,1)S(1)}, u32[]{:S(2)}, u32[]{:S(2)}) %collective-permute-start.1) | collective-permute-done | bytes 524320 | tf_op jit(solution)/shard_map/ppermute | solution.py:83
  18.8 9.1 %collective-permute-done.3.own_ref = bf16[128,2048]{1,0:T(8,128)(2,1)S(1)} collective-permute-done((bf16[128,2048]{1,0:T(8,128)(2,1)}, bf16[128,2048]{1,0:T(8,128)(2,1)S(1)}, u32[]{:S(2)}, u32[]{:S(2)}) %collective-permute-start.3) | collective-permute-done | bytes 524320 | tf_op jit(solution)/shard_map/ppermute | solution.py:83
  29.8 7.3 %collective-permute-done = bf16[128,2048]{1,0:T(8,128)(2,1)S(1)} collective-permute-done((bf16[128,2048]{1,0:T(8,128)(2,1)}, bf16[128,2048]{1,0:T(8,128)(2,1)S(1)}, u32[]{:S(2)}, u32[]{:S(2)}) %collective-permute-start) | collective-permute-done | bytes 524320 | tf_op jit(solution)/shard_map/ppermute | solution.py:83
  37.1 6.0 %collective-permute-done.4 = bf16[128,2048]{1,0:T(8,128)(2,1)S(1)} collective-permute-done((bf16[128,2048]{1,0:T(8,128)(2,1)S(1)}, bf16[128,2048]{1,0:T(8,128)(2,1)S(1)}, u32[]{:S(2)}, u32[]{:S(2)}) %collective-permute-start.4) | collective-permute-done | bytes 524320 | tf_op jit(solution)/shard_map/ppermute | solution.py:83
  45.3 8.8 %collective-permute-done.7 = s32[8,128]{1,0:T(8,128)S(1)} collective-permute-done((s32[8,128]{1,0:T(8,128)S(1)}, s32[8,128]{1,0:T(8,128)S(1)}, u32[]{:S(2)}, u32[]{:S(2)}) %collective-permute-start.7) | collective-permute-done | bytes 4128 | tf_op jit(solution)/shard_map/ppermute | solution.py:83
  54.4 4.2 %collective-permute-done.8 = s32[8,128]{1,0:T(8,128)S(1)} collective-permute-done((s32[8,128]{1,0:T(8,128)S(1)}, s32[8,128]{1,0:T(8,128)S(1)}, u32[]{:S(2)}, u32[]{:S(2)}) %collective-permute-start.8) | collective-permute-done | bytes 4128 | tf_op jit(solution)/shard_map/ppermute | solution.py:83
  58.6 2.0 %collective-permute-start.9 = (s32[8,128]{1,0:T(8,128)S(1)}, s32[8,128]{1,0:T(8,128)S(1)}, u32[]{:S(2)}, u32[]{:S(2)}) collective-permute-start(s32[8,128]{1,0:T(8,128)S(1)} %pad_add_fusion), channel_id=1, source_target_pairs={{0,6},{1,7},{2,0},{3,1},{4,2},{5,3},{6,4},{7,5},{8,14},{9,15},{10,... | collective-permute-start | bytes 12296 | tf_op jit(solution)/shard_map/ppermute | solution.py:83
  60.6 1.6 collective-permute-done.9
  64.1 4.7 %hidden_gram_0.1.rest_0_ = f32[512,512]{1,0:T(8,128)} custom-call(bf16[128,2048]{1,0:T(8,128)(2,1)} %own_ref.1, bf16[128,2048]{1,0:T(8,128)(2,1)} %copy-done.1, f32[1024,1]{1,0:T(8,128)} %copy.21.member_ref, bf16[2048,512]{1,0:T(8,128)(2,1)} %bitcast.32, bf16[2048,512]{1,0:T(8,128)(2,1)} %bitcast.36), custom_call_target="tpu_custom_call" | custom-call | flops 1207959552 | bytes 6291456 | tf_op jit(solution)/shard_map/hidden_gram_0/pallas_call | solution.py:57
  69.6 5.0 %hidden_gram_1.1.rest_0_ = f32[512,512]{1,0:T(8,128)} custom-call(bf16[128,2048]{1,0:T(8,128)(2,1)} %copy-done.3, bf16[128,2048]{1,0:T(8,128)(2,1)} %copy-done.4, f32[1024,1]{1,0:T(8,128)} %copy.21.member_ref, bf16[2048,512]{1,0:T(8,128)(2,1)} %bitcast.33, bf16[2048,512]{1,0:T(8,128)(2,1)} %bitcast.37, ...), custom_call_target="tpu_custom_call", output_to_operand_aliasing={{}: (5, {})} | custom-call | flops 1207959552 | bytes 6291456 | tf_op jit(solution)/shard_map/hidden_gram_1/pallas_call | solution.py:57
  75.4 5.0 %hidden_gram_3.1.rest_0_ = f32[512,512]{1,0:T(8,128)} custom-call(bf16[128,2048]{1,0:T(8,128)(2,1)} %copy-done.2, bf16[128,2048]{1,0:T(8,128)(2,1)} %copy-done.5, f32[1024,1]{1,0:T(8,128)} %copy.21.member_ref, bf16[2048,512]{1,0:T(8,128)(2,1)} %bitcast.34, bf16[2048,512]{1,0:T(8,128)(2,1)} %bitcast.38, ...), custom_call_target="tpu_custom_call", output_to_operand_aliasing={{}: (5, {})} | custom-call | flops 1207959552 | bytes 6291456 | tf_op jit(solution)/shard_map/hidden_gram_3/pallas_call | solution.py:57
  80.5 5.0 %hidden_gram_2.1 = f32[512,512]{1,0:T(8,128)} custom-call(bf16[128,2048]{1,0:T(8,128)(2,1)} %copy-done, bf16[128,2048]{1,0:T(8,128)(2,1)} %collective-permute-done.5.other_ref, f32[1024,1]{1,0:T(8,128)} %copy.21.member_ref, bf16[2048,512]{1,0:T(8,128)(2,1)} %bitcast.35, bf16[2048,512]{1,0:T(8,128)(2,1)} %bitcast.39, ...), custom_call_target="tpu_custom_call", output_to_operand_aliasing={{}: (5, {})} | custom-call | flops 1207959552 | bytes 6291456 | tf_op jit(solution)/shard_map/hidden_gram_2/pallas_call | solution.py:57
  87.1 1.6 collective-permute-start.13
  88.6 20.5 %collective-permute-done.13 = f32[512,512]{0,1:T(8,128)S(1)} collective-permute-done((f32[512,512]{0,1:T(8,128)S(1)}, f32[512,512]{0,1:T(8,128)S(1)}, u32[]{:S(2)}, u32[]{:S(2)}) %collective-permute-start.13) | collective-permute-done | bytes 1048608 | tf_op jit(solution)/shard_map/ppermute | solution.py:155
  110.0 11.7 %cholesky.103 = f32[128,128]{1,0:T(8,128)S(1)} custom-call(f32[128,128]{1,0:T(8,128)S(1)} %cholesky.263), custom_call_target="Cholesky" | custom-call | tf_op jit(solution)/shard_map/jit(cholesky)/cholesky | solution.py:157
  121.7 9.8 %custom-call.27 = f32[1,128,128]{1,2,0:T(8,128)S(1)} custom-call(f32[1,128,128]{2,1,0:T(8,128)S(1)} %get-tuple-element.10), custom_call_target="InvertDiagBlocksLowerTriangular" | custom-call | tf_op jit(solution)/shard_map/jit(cholesky)/cholesky | solution.py:157
  132.2 11.7 %cholesky.215 = f32[128,128]{1,0:T(8,128)S(1)} custom-call(f32[128,128]{1,0:T(8,128)S(1)} %cholesky.267), custom_call_target="Cholesky" | custom-call | tf_op jit(solution)/shard_map/jit(cholesky)/cholesky | solution.py:157
  144.3 10.0 %custom-call.28 = f32[1,128,128]{1,2,0:T(8,128)S(1)} custom-call(f32[1,128,128]{2,1,0:T(8,128)S(1)} %get-tuple-element.8), custom_call_target="InvertDiagBlocksLowerTriangular" | custom-call | tf_op jit(solution)/shard_map/jit(cholesky)/cholesky | solution.py:157
  155.4 11.7 %cholesky.236 = f32[128,128]{1,0:T(8,128)S(1)} custom-call(f32[128,128]{1,0:T(8,128)S(1)} %cholesky.272), custom_call_target="Cholesky" | custom-call | tf_op jit(solution)/shard_map/jit(cholesky)/cholesky | solution.py:157
  167.3 9.8 %custom-call.29 = f32[1,128,128]{1,2,0:T(8,128)S(1)} custom-call(f32[1,128,128]{2,1,0:T(8,128)S(1)} %get-tuple-element.6), custom_call_target="InvertDiagBlocksLowerTriangular" | custom-call | tf_op jit(solution)/shard_map/jit(cholesky)/cholesky | solution.py:157
  177.9 11.7 %cholesky.253 = f32[128,128]{1,0:T(8,128)S(1)} custom-call(f32[128,128]{1,0:T(8,128)S(1)} %convolution_subtract_fusion.2), custom_call_target="Cholesky" | custom-call | tf_op jit(solution)/shard_map/jit(cholesky)/cholesky | solution.py:157
  (65 shorter events, 16.9 us)
Async XLA Ops:
  0.0 43.3 %copy-start.6 = (s32[128,4]{0,1:T(4,128)S(1)}, s32[128,4]{0,1:T(4,128)}, u32[]{:S(2)}) copy-start(s32[128,4]{0,1:T(4,128)} %param.5) | copy-start | bytes 6148
  0.0 18.1 %collective-permute-start.1 = (bf16[128,2048]{1,0:T(8,128)(2,1)}, bf16[128,2048]{1,0:T(8,128)(2,1)S(1)}, u32[]{:S(2)}, u32[]{:S(2)}) collective-permute-start(bf16[128,2048]{1,0:T(8,128)(2,1)} %own_ref.1), channel_id=1, source_target_pairs={{0,2},{1,3},{2,4},{3,5},{4,6},{5,7},{6,0},{7,1},{8,10},{9,11},{10,... | collective-permute-start | bytes 1572872 | tf_op jit(solution)/shard_map/ppermute | solution.py:83
  3.1 24.8 %collective-permute-start.3 = (bf16[128,2048]{1,0:T(8,128)(2,1)}, bf16[128,2048]{1,0:T(8,128)(2,1)S(1)}, u32[]{:S(2)}, u32[]{:S(2)}) collective-permute-start(bf16[128,2048]{1,0:T(8,128)(2,1)} %own_ref.1), channel_id=1, source_target_pairs={{0,6},{1,7},{2,0},{3,1},{4,2},{5,3},{6,4},{7,5},{8,14},{9,15},{10,... | collective-permute-start | bytes 1572872 | tf_op jit(solution)/shard_map/ppermute | solution.py:83
  5.1 31.9 %collective-permute-start = (bf16[128,2048]{1,0:T(8,128)(2,1)}, bf16[128,2048]{1,0:T(8,128)(2,1)S(1)}, u32[]{:S(2)}, u32[]{:S(2)}) collective-permute-start(bf16[128,2048]{1,0:T(8,128)(2,1)} %own_ref.1), channel_id=1, source_target_pairs={{0,4},{1,5},{6,2},{7,3},{8,12},{9,13},{14,10},{15,11},{16,20},{17,... | collective-permute-start | bytes 1572872 | tf_op jit(solution)/shard_map/ppermute | solution.py:83
  18.1 50.7 %copy-start.3 = (bf16[128,2048]{1,0:T(8,128)(2,1)}, bf16[128,2048]{1,0:T(8,128)(2,1)S(1)}, u32[]{:S(2)}) copy-start(bf16[128,2048]{1,0:T(8,128)(2,1)S(1)} %collective-permute-done.1.own_ref) | copy-start | bytes 1572868
  18.1 19.0 %collective-permute-start.2 = (bf16[128,2048]{1,0:T(8,128)(2,1)S(1)}, bf16[128,2048]{1,0:T(8,128)(2,1)S(1)}, u32[]{:S(2)}, u32[]{:S(2)}) collective-permute-start(bf16[128,2048]{1,0:T(8,128)(2,1)S(1)} %collective-permute-done.1.own_ref), channel_id=1, source_target_pairs={{4,6},{5,7},{12,14},{13,15},{20,22},{21,23},{28,30},{29,31}} | collective-permute-start | bytes 1572872 | tf_op jit(solution)/shard_map/ppermute | solution.py:83
  27.9 40.9 %copy-start.2 = (bf16[128,2048]{1,0:T(8,128)(2,1)}, bf16[128,2048]{1,0:T(8,128)(2,1)S(1)}, u32[]{:S(2)}) copy-start(bf16[128,2048]{1,0:T(8,128)(2,1)S(1)} %collective-permute-done.3.own_ref) | copy-start | bytes 1572868
  27.9 15.2 %collective-permute-start.4 = (bf16[128,2048]{1,0:T(8,128)(2,1)S(1)}, bf16[128,2048]{1,0:T(8,128)(2,1)S(1)}, u32[]{:S(2)}, u32[]{:S(2)}) collective-permute-start(bf16[128,2048]{1,0:T(8,128)(2,1)S(1)} %collective-permute-done.3.own_ref), channel_id=1, source_target_pairs={{2,0},{3,1},{10,8},{11,9},{18,16},{19,17},{26,24},{27,25}} | collective-permute-start | bytes 1572872 | tf_op jit(solution)/shard_map/ppermute | solution.py:83
  29.2 34.1 %collective-permute-start.12 = (bf16[128,2048]{1,0:T(8,128)(2,1)}, bf16[128,2048]{1,0:T(8,128)(2,1)S(1)}, u32[]{:S(2)}, u32[]{:S(2)}) collective-permute-start(bf16[128,2048]{1,0:T(8,128)(2,1)} %own_ref.1), channel_id=1, source_target_pairs={{0,1},{1,0},{2,3},{3,2},{4,5},{5,4},{6,7},{7,6},{8,9},{9,8},{10,11... | collective-permute-start | bytes 1572872 | tf_op jit(solution)/shard_map/ppermute | solution.py:83
  29.3 39.5 %collective-permute-start.11 = (bf16[128,2048]{1,0:T(8,128)(2,1)S(1)}, bf16[128,2048]{1,0:T(8,128)(2,1)S(1)}, u32[]{:S(2)}, u32[]{:S(2)}) collective-permute-start(bf16[128,2048]{1,0:T(8,128)(2,1)S(1)} %collective-permute-done.1.own_ref), channel_id=1, source_target_pairs={{0,1},{1,0},{2,3},{3,2},{4,5},{5,4},{6,7},{7,6},{8,9},{9,8},{10,11... | collective-permute-start | bytes 1572872 | tf_op jit(solution)/shard_map/ppermute | solution.py:83
  37.1 37.5 %collective-permute-start.10 = (bf16[128,2048]{1,0:T(8,128)(2,1)S(1)}, bf16[128,2048]{1,0:T(8,128)(2,1)S(1)}, u32[]{:S(2)}, u32[]{:S(2)}) collective-permute-start(bf16[128,2048]{1,0:T(8,128)(2,1)S(1)} %collective-permute-done.3.own_ref), channel_id=1, source_target_pairs={{0,1},{1,0},{2,3},{3,2},{4,5},{5,4},{6,7},{7,6},{8,9},{9,8},{10,11... | collective-permute-start | bytes 1572872 | tf_op jit(solution)/shard_map/ppermute | solution.py:83
  43.2 25.6 %copy-start = (bf16[128,2048]{1,0:T(8,128)(2,1)}, bf16[128,2048]{1,0:T(8,128)(2,1)S(1)}, u32[]{:S(2)}) copy-start(bf16[128,2048]{1,0:T(8,128)(2,1)S(1)} %add_add_fusion.own_ref) | copy-start | bytes 1572868
  43.2 37.3 %collective-permute-start.5 = (bf16[128,2048]{1,0:T(8,128)(2,1)S(1)}, bf16[128,2048]{1,0:T(8,128)(2,1)}, u32[]{:S(2)}, u32[]{:S(2)}) collective-permute-start(bf16[128,2048]{1,0:T(8,128)(2,1)S(1)} %add_add_fusion.own_ref), channel_id=1, source_target_pairs={{0,1},{1,0},{2,3},{3,2},{4,5},{5,4},{6,7},{7,6},{8,9},{9,8},{10,11... | collective-permute-start | bytes 1572872 | tf_op jit(solution)/shard_map/ppermute | solution.py:83
  43.3 2.0 %collective-permute-start.6 = (s32[4,128]{1,0:T(4,128)S(1)}, s32[4,128]{1,0:T(4,128)S(1)}, u32[]{:S(2)}, u32[]{:S(2)}) collective-permute-start(s32[4,128]{1,0:T(4,128)S(1)} %bitcast.45), channel_id=1, source_target_pairs={{0,1},{1,0},{2,3},{3,2},{4,5},{5,4},{6,7},{7,6},{8,9},{9,8},{10,11... | collective-permute-start | bytes 6152 | tf_op jit(solution)/shard_map/ppermute | solution.py:83
  45.3 8.8 %collective-permute-start.7 = (s32[8,128]{1,0:T(8,128)S(1)}, s32[8,128]{1,0:T(8,128)S(1)}, u32[]{:S(2)}, u32[]{:S(2)}) collective-permute-start(s32[8,128]{1,0:T(8,128)S(1)} %pad_add_fusion), channel_id=1, source_target_pairs={{0,2},{1,3},{2,4},{3,5},{4,6},{5,7},{6,0},{7,1},{8,10},{9,11},{10,... | collective-permute-start | bytes 12296 | tf_op jit(solution)/shard_map/ppermute | solution.py:83
  54.1 4.5 %collective-permute-start.8 = (s32[8,128]{1,0:T(8,128)S(1)}, s32[8,128]{1,0:T(8,128)S(1)}, u32[]{:S(2)}, u32[]{:S(2)}) collective-permute-start(s32[8,128]{1,0:T(8,128)S(1)} %pad_add_fusion), channel_id=1, source_target_pairs={{0,4},{1,5},{2,6},{3,7},{4,0},{5,1},{6,2},{7,3},{8,12},{9,13},{10,... | collective-permute-start | bytes 12296 | tf_op jit(solution)/shard_map/ppermute | solution.py:83
  58.6 3.6 %collective-permute-start.9 = (s32[8,128]{1,0:T(8,128)S(1)}, s32[8,128]{1,0:T(8,128)S(1)}, u32[]{:S(2)}, u32[]{:S(2)}) collective-permute-start(s32[8,128]{1,0:T(8,128)S(1)} %pad_add_fusion), channel_id=1, source_target_pairs={{0,6},{1,7},{2,0},{3,1},{4,2},{5,3},{6,4},{7,5},{8,14},{9,15},{10,... | collective-permute-start | bytes 12296 | tf_op jit(solution)/shard_map/ppermute | solution.py:83
  63.3 0.8 copy-start.1
  68.8 0.8 copy-start.4
  74.6 0.8 copy-start.5
  87.1 22.1 %collective-permute-start.13 = (f32[512,512]{0,1:T(8,128)S(1)}, f32[512,512]{0,1:T(8,128)S(1)}, u32[]{:S(2)}, u32[]{:S(2)}) collective-permute-start(f32[512,512]{0,1:T(8,128)S(1)} %copy.23), channel_id=1, source_target_pairs={{0,8},{8,0},{1,9},{9,1},{2,10},{10,2},{3,11},{11,3},{4,12},{12,4},... | collective-permute-start | bytes 3145736 | tf_op jit(solution)/shard_map/ppermute | solution.py:155

commit v2 on v1

--- a/solution.py
+++ b/solution.py
@@ -147,14 +147,88 @@
     return finish(gram_local, rows_mean, data_ranks, factor_width)
 
 
+def over_lanes(column, width):
+    return jnp.concatenate([column] * (width // column.shape[1]), axis=1)
+
+
+def factor_panel(x, columns, sublane):
+    rows, width = x.shape
+    factor = jnp.zeros_like(x)
+    for k in range(rows):
+        scale = lax.rsqrt(jnp.broadcast_to(columns[k][k : k + 1, :], columns[k].shape))
+        lower = columns[k] * scale
+        upper = jnp.broadcast_to(x[k : k + 1, :], x.shape) * over_lanes(scale, width)
+        factor = jnp.where(sublane == k, upper, factor)
+        for j in range(k + 1, rows):
+            columns[j] = columns[j] - lower * jnp.broadcast_to(lower[j : j + 1, :], lower.shape)
+        if k + 1 < rows:
+            x = x - over_lanes(lower, width) * upper
+    return factor
+
+
+def outer_sum(a, b):
+    return lax.dot_general(
+        a, b, (((0,), (0,)), ((), ())), precision=lax.Precision.HIGHEST, preferred_element_type=jnp.float32
+    )
+
+
+def factor_kernel(mine_ref, theirs_ref, out_ref, rest_ref, *, rows_mean):
+    size = mine_ref.shape[0]
+    block, panel = 128, 8
+    row = lax.broadcasted_iota(jnp.int32, (size, size), 0)
+    col = lax.broadcasted_iota(jnp.int32, (size, size), 1)
+    rest_ref[...] = (mine_ref[...] + theirs_ref[...]) / rows_mean + jnp.where(row == col, RIDGE, 0.0)
+    for base in range(0, size, block):
+        width = size - base
+        end = base + block
+        if base:
+            out_ref[base:end, :base] = jnp.zeros((block, base), jnp.float32)
+        sublane = lax.broadcasted_iota(jnp.int32, (panel, width), 0)
+        lane = lax.broadcasted_iota(jnp.int32, (panel, width), 1)
+
+        def step(p, carry):
+            first = panel * p
+            rows = pl.ds(pl.multiple_of(base + first, panel), panel)
+            x = rest_ref[rows, base:]
+            corner = x[:, :block]
+            columns = [
+                jnp.take_along_axis(
+                    corner, jnp.full(corner.shape, first + j, jnp.int32), axis=1, mode="promise_in_bounds"
+                )
+                for j in range(panel)
+            ]
+            factor = factor_panel(x, columns, sublane)
+            out_ref[rows, base:] = jnp.where(lane >= sublane + first, factor, 0.0)
+            below = jnp.where(lane[:, :block] >= first + panel, factor[:, :block], 0.0)
+            rest_ref[base:end, base:] -= outer_sum(below, factor)
+            return carry
+
+        lax.fori_loop(0, block // panel, step, 0)
+        if end < size:
+            done = out_ref[base:end, end:]
+            rest_ref[end:, end:] -= outer_sum(done, done)
+
+
+def factor_of(mine, theirs, rows_mean):
+    size = mine.shape[0]
+    return pl.pallas_call(
+        functools.partial(factor_kernel, rows_mean=rows_mean),
+        in_specs=[pl.BlockSpec(memory_space=pltpu.VMEM)] * 2,
+        out_specs=pl.BlockSpec(memory_space=pltpu.VMEM),
+        out_shape=jax.ShapeDtypeStruct((size, size), jnp.float32),
+        scratch_shapes=[pltpu.VMEM((size, size), jnp.float32)],
+        name="factor",
+    )(mine, theirs)
+
+
 def finish(gram_local, rows_mean, data_ranks, factor_width):
     block_rows = factor_width // data_ranks
     my_rank = lax.axis_index("dp")
-    summed = gram_local
+    theirs = jnp.zeros_like(gram_local)
     for s in range(1, data_ranks):
-        summed = summed + lax.ppermute(gram_local, "dp", [(r, (r + s) % data_ranks) for r in range(data_ranks)])
-    regular = summed / rows_mean + RIDGE * jnp.eye(factor_width, dtype=jnp.float32)
-    factor = jnp.linalg.cholesky(regular).T
+        moved = lax.ppermute(gram_local, "dp", [(r, (r + s) % data_ranks) for r in range(data_ranks)])
+        theirs = moved if s == 1 else theirs + moved
+    factor = factor_of(gram_local, theirs, rows_mean)
     my_rows = lax.dynamic_slice_in_dim(factor, my_rank * block_rows, block_rows, 0)
     return my_rows.reshape(1, block_rows, factor_width)
 

time: 195 us -> 146 us (0.75)
  other arithmetic: 80 us -> 0.12 us
  Pallas kernels: 19.8 us -> 55 us
  between operations: 2.84 us -> 0.12 us
  matrix products: 2.33 us -> 0 us
    another operation x14 -> x0, other arithmetic: 78.6 us -> none  [finish(): factor = jnp.linalg.cholesky(regular).T]
    pallas_call x0 -> x1, Pallas kernels: none -> 35.3 us  [factor_of(): pl.pallas_call(functools.partial(factor_kernel, rows_mean=rows_mean), in_...]
    another operation x6 -> x0, matrix products: 2.33 us -> none  [finish(): factor = jnp.linalg.cholesky(regular).T]
  transfers between devices with their start and end apart: 14 -> 14, of which waited for: 9 -> 9; matrix products, arithmetic and copies ran while one was open for 1% -> 1% of each run, Pallas kernels for 8% -> 10%
where the time goes in v2:
time: 146 us
  waiting for transfers between devices  69.4 us (48%)
  Pallas kernels  55 us (38%)
  starting transfers between devices  14.9 us (10%)
  local copies, waits for them, and re-layouts  6.3 us (4%)
    ppermute x13, waiting for transfers between devices, gather_grams(): move = lambda x, pairs: lax.ppermute(x, 'expert', pairs)  48.6 us
    pallas_call x1, Pallas kernels, factor_of(): pl.pallas_call(functools.partial(factor_kernel, rows_mean=rows_mean), in_...  35.3 us
    ppermute x1, waiting for transfers between devices, finish(): lax.ppermute(gram_local, 'dp', [(r, (r + s) % data_ranks) for r in range(...  20.8 us
    pallas_call x4, Pallas kernels, hidden_gram(): pl.pallas_call(hidden_gram_kernel, grid=(hw // width,), in_specs=in_specs...  19.7 us
    ppermute x13, starting transfers between devices, gather_grams(): move = lambda x, pairs: lax.ppermute(x, 'expert', pairs)  13.4 us
    unnamed x16, local copies, waits for them, and re-layouts  3.37 us
  transfers between devices with their start and end apart: 14, of which 9 were waited for; matrix products, arithmetic and copies ran while one was open for 1% of the time, Pallas kernels for 10%

profile of v2, /device:TPU:0, one launch (start us, length us, event | category | flops | bytes accessed | tf_op | source)
XLA Modules:
  0.0 145.8 jit_solution(12281073625224378231)
XLA Ops:
  0.0 3.1 %collective-permute-start.1 = (bf16[128,2048]{1,0:T(8,128)(2,1)}, bf16[128,2048]{1,0:T(8,128)(2,1)S(1)}, u32[]{:S(2)}, u32[]{:S(2)}) collective-permute-start(bf16[128,2048]{1,0:T(8,128)(2,1)} %own_ref.1), channel_id=1, source_target_pairs={{0,2},{1,3},{2,4},{3,5},{4,6},{5,7},{6,0},{7,1},{8,10},{9,11},{10,... | collective-permute-start | bytes 1572872 | tf_op jit(solution)/shard_map/ppermute | solution.py:83
  3.1 2.1 %collective-permute-start.3 = (bf16[128,2048]{1,0:T(8,128)(2,1)}, bf16[128,2048]{1,0:T(8,128)(2,1)S(1)}, u32[]{:S(2)}, u32[]{:S(2)}) collective-permute-start(bf16[128,2048]{1,0:T(8,128)(2,1)} %own_ref.1), channel_id=1, source_target_pairs={{0,6},{1,7},{2,0},{3,1},{4,2},{5,3},{6,4},{7,5},{8,14},{9,15},{10,... | collective-permute-start | bytes 1572872 | tf_op jit(solution)/shard_map/ppermute | solution.py:83
  5.1 2.9 %collective-permute-start = (bf16[128,2048]{1,0:T(8,128)(2,1)}, bf16[128,2048]{1,0:T(8,128)(2,1)S(1)}, u32[]{:S(2)}, u32[]{:S(2)}) collective-permute-start(bf16[128,2048]{1,0:T(8,128)(2,1)} %own_ref.1), channel_id=1, source_target_pairs={{0,4},{1,5},{6,2},{7,3},{8,12},{9,13},{14,10},{15,11},{16,20},{17,... | collective-permute-start | bytes 1572872 | tf_op jit(solution)/shard_map/ppermute | solution.py:83
  8.0 10.1 %collective-permute-done.1.own_ref = bf16[128,2048]{1,0:T(8,128)(2,1)S(1)} collective-permute-done((bf16[128,2048]{1,0:T(8,128)(2,1)}, bf16[128,2048]{1,0:T(8,128)(2,1)S(1)}, u32[]{:S(2)}, u32[]{:S(2)}) %collective-permute-start.1) | collective-permute-done | bytes 524320 | tf_op jit(solution)/shard_map/ppermute | solution.py:83
  18.8 9.1 %collective-permute-done.3.own_ref = bf16[128,2048]{1,0:T(8,128)(2,1)S(1)} collective-permute-done((bf16[128,2048]{1,0:T(8,128)(2,1)}, bf16[128,2048]{1,0:T(8,128)(2,1)S(1)}, u32[]{:S(2)}, u32[]{:S(2)}) %collective-permute-start.3) | collective-permute-done | bytes 524320 | tf_op jit(solution)/shard_map/ppermute | solution.py:83
  27.9 1.3 collective-permute-start.4
  29.8 7.3 %collective-permute-done = bf16[128,2048]{1,0:T(8,128)(2,1)S(1)} collective-permute-done((bf16[128,2048]{1,0:T(8,128)(2,1)}, bf16[128,2048]{1,0:T(8,128)(2,1)S(1)}, u32[]{:S(2)}, u32[]{:S(2)}) %collective-permute-start) | collective-permute-done | bytes 524320 | tf_op jit(solution)/shard_map/ppermute | solution.py:83
  37.1 6.0 %collective-permute-done.4 = bf16[128,2048]{1,0:T(8,128)(2,1)S(1)} collective-permute-done((bf16[128,2048]{1,0:T(8,128)(2,1)S(1)}, bf16[128,2048]{1,0:T(8,128)(2,1)S(1)}, u32[]{:S(2)}, u32[]{:S(2)}) %collective-permute-start.4) | collective-permute-done | bytes 524320 | tf_op jit(solution)/shard_map/ppermute | solution.py:83
  43.8 1.5 %collective-permute-done.6 = s32[4,128]{1,0:T(4,128)S(1)} collective-permute-done((s32[4,128]{1,0:T(4,128)S(1)}, s32[4,128]{1,0:T(4,128)S(1)}, u32[]{:S(2)}, u32[]{:S(2)}) %collective-permute-start.6) | collective-permute-done | bytes 2080 | tf_op jit(solution)/shard_map/ppermute | solution.py:83
  45.3 8.8 %collective-permute-done.7 = s32[8,128]{1,0:T(8,128)S(1)} collective-permute-done((s32[8,128]{1,0:T(8,128)S(1)}, s32[8,128]{1,0:T(8,128)S(1)}, u32[]{:S(2)}, u32[]{:S(2)}) %collective-permute-start.7) | collective-permute-done | bytes 4128 | tf_op jit(solution)/shard_map/ppermute | solution.py:83
  54.4 4.2 %collective-permute-done.8 = s32[8,128]{1,0:T(8,128)S(1)} collective-permute-done((s32[8,128]{1,0:T(8,128)S(1)}, s32[8,128]{1,0:T(8,128)S(1)}, u32[]{:S(2)}, u32[]{:S(2)}) %collective-permute-start.8) | collective-permute-done | bytes 4128 | tf_op jit(solution)/shard_map/ppermute | solution.py:83
  58.6 2.0 %collective-permute-start.9 = (s32[8,128]{1,0:T(8,128)S(1)}, s32[8,128]{1,0:T(8,128)S(1)}, u32[]{:S(2)}, u32[]{:S(2)}) collective-permute-start(s32[8,128]{1,0:T(8,128)S(1)} %pad_add_fusion), channel_id=1, source_target_pairs={{0,6},{1,7},{2,0},{3,1},{4,2},{5,3},{6,4},{7,5},{8,14},{9,15},{10,... | collective-permute-start | bytes 12296 | tf_op jit(solution)/shard_map/ppermute | solution.py:83
  60.6 1.6 %collective-permute-done.9 = s32[8,128]{1,0:T(8,128)S(1)} collective-permute-done((s32[8,128]{1,0:T(8,128)S(1)}, s32[8,128]{1,0:T(8,128)S(1)}, u32[]{:S(2)}, u32[]{:S(2)}) %collective-permute-start.9) | collective-permute-done | bytes 4128 | tf_op jit(solution)/shard_map/ppermute | solution.py:83
  62.3 1.1 copy.11.member_ref
  63.3 0.8 copy-done.2
  64.1 4.7 %hidden_gram_0.1.rest_0_ = f32[512,512]{1,0:T(8,128)} custom-call(bf16[128,2048]{1,0:T(8,128)(2,1)} %own_ref.1, bf16[128,2048]{1,0:T(8,128)(2,1)} %copy-done.2, f32[1024,1]{1,0:T(8,128)} %copy.11.member_ref, bf16[2048,512]{1,0:T(8,128)(2,1)} %bitcast.10, bf16[2048,512]{1,0:T(8,128)(2,1)} %bitcast.14), custom_call_target="tpu_custom_call" | custom-call | flops 1207959552 | bytes 6291456 | tf_op jit(solution)/shard_map/hidden_gram_0/pallas_call | solution.py:57
  69.6 5.0 %hidden_gram_1.1.rest_0_ = f32[512,512]{1,0:T(8,128)} custom-call(bf16[128,2048]{1,0:T(8,128)(2,1)} %copy-done.4, bf16[128,2048]{1,0:T(8,128)(2,1)} %copy-done.5, f32[1024,1]{1,0:T(8,128)} %copy.11.member_ref, bf16[2048,512]{1,0:T(8,128)(2,1)} %bitcast.11, bf16[2048,512]{1,0:T(8,128)(2,1)} %bitcast.15, ...), custom_call_target="tpu_custom_call", output_to_operand_aliasing={{}: (5, {})} | custom-call | flops 1207959552 | bytes 6291456 | tf_op jit(solution)/shard_map/hidden_gram_1/pallas_call | solution.py:57
  75.4 5.0 %hidden_gram_3.1.rest_0_ = f32[512,512]{1,0:T(8,128)} custom-call(bf16[128,2048]{1,0:T(8,128)(2,1)} %copy-done.3, bf16[128,2048]{1,0:T(8,128)(2,1)} %copy-done.6, f32[1024,1]{1,0:T(8,128)} %copy.11.member_ref, bf16[2048,512]{1,0:T(8,128)(2,1)} %bitcast.12, bf16[2048,512]{1,0:T(8,128)(2,1)} %bitcast.16, ...), custom_call_target="tpu_custom_call", output_to_operand_aliasing={{}: (5, {})} | custom-call | flops 1207959552 | bytes 6291456 | tf_op jit(solution)/shard_map/hidden_gram_3/pallas_call | solution.py:57
  80.4 5.0 %hidden_gram_2.1.mine_ref = f32[512,512]{1,0:T(8,128)} custom-call(bf16[128,2048]{1,0:T(8,128)(2,1)} %copy-done, bf16[128,2048]{1,0:T(8,128)(2,1)} %collective-permute-done.5.other_ref, f32[1024,1]{1,0:T(8,128)} %copy.11.member_ref, bf16[2048,512]{1,0:T(8,128)(2,1)} %bitcast.13, bf16[2048,512]{1,0:T(8,128)(2,1)} %bitcast.17, ...), custom_call_target="tpu_custom_call", output_to_operand_aliasing={{}: (5, {})} | custom-call | flops 1207959552 | bytes 6291456 | tf_op jit(solution)/shard_map/hidden_gram_2/pallas_call | solution.py:57
  85.5 1.5 %collective-permute-start.13 = (f32[512,512]{1,0:T(8,128)}, f32[512,512]{1,0:T(8,128)S(1)}, u32[]{:S(2)}, u32[]{:S(2)}) collective-permute-start(f32[512,512]{1,0:T(8,128)} %hidden_gram_2.1.mine_ref), channel_id=1, source_target_pairs={{0,8},{8,0},{1,9},{9,1},{2,10},{10,2},{3,11},{11,3},{4,12},{12,4},... | collective-permute-start | bytes 3145736 | tf_op jit(solution)/shard_map/ppermute | solution.py:229
  87.0 20.8 %collective-permute-done.13.theirs_ref = f32[512,512]{1,0:T(8,128)S(1)} collective-permute-done((f32[512,512]{1,0:T(8,128)}, f32[512,512]{1,0:T(8,128)S(1)}, u32[]{:S(2)}, u32[]{:S(2)}) %collective-permute-start.13) | collective-permute-done | bytes 1048608 | tf_op jit(solution)/shard_map/ppermute | solution.py:229
  107.7 1.0 copy-done.1
  108.7 35.3 %factor.1 = f32[512,512]{1,0:T(8,128)} custom-call(f32[512,512]{1,0:T(8,128)} %hidden_gram_2.1.mine_ref, f32[512,512]{1,0:T(8,128)} %copy-done.1), custom_call_target="tpu_custom_call" | custom-call | tf_op jit(solution)/shard_map/factor/pallas_call | solution.py:214
  144.0 1.9 %dynamic-slice_bitcast_fusion = f32[1,256,512]{2,1,0:T(8,128)} fusion(f32[512,512]{1,0:T(8,128)} %factor.1, s32[]{:T(128)S(6)} %select_n.3), kind=kLoop, calls=%fused_computation | loop fusion | bytes 1048580 | tf_op jit(solution)/shard_map/reshape | solution.py:233
  (31 shorter events, 3.9 us)
Async XLA Ops:
  0.0 43.3 %copy-start.7 = (s32[128,4]{0,1:T(4,128)S(1)}, s32[128,4]{0,1:T(4,128)}, u32[]{:S(2)}) copy-start(s32[128,4]{0,1:T(4,128)} %param.5) | copy-start | bytes 6148
  0.0 18.1 %collective-permute-start.1 = (bf16[128,2048]{1,0:T(8,128)(2,1)}, bf16[128,2048]{1,0:T(8,128)(2,1)S(1)}, u32[]{:S(2)}, u32[]{:S(2)}) collective-permute-start(bf16[128,2048]{1,0:T(8,128)(2,1)} %own_ref.1), channel_id=1, source_target_pairs={{0,2},{1,3},{2,4},{3,5},{4,6},{5,7},{6,0},{7,1},{8,10},{9,11},{10,... | collective-permute-start | bytes 1572872 | tf_op jit(solution)/shard_map/ppermute | solution.py:83
  3.1 24.8 %collective-permute-start.3 = (bf16[128,2048]{1,0:T(8,128)(2,1)}, bf16[128,2048]{1,0:T(8,128)(2,1)S(1)}, u32[]{:S(2)}, u32[]{:S(2)}) collective-permute-start(bf16[128,2048]{1,0:T(8,128)(2,1)} %own_ref.1), channel_id=1, source_target_pairs={{0,6},{1,7},{2,0},{3,1},{4,2},{5,3},{6,4},{7,5},{8,14},{9,15},{10,... | collective-permute-start | bytes 1572872 | tf_op jit(solution)/shard_map/ppermute | solution.py:83
  5.1 31.9 %collective-permute-start = (bf16[128,2048]{1,0:T(8,128)(2,1)}, bf16[128,2048]{1,0:T(8,128)(2,1)S(1)}, u32[]{:S(2)}, u32[]{:S(2)}) collective-permute-start(bf16[128,2048]{1,0:T(8,128)(2,1)} %own_ref.1), channel_id=1, source_target_pairs={{0,4},{1,5},{6,2},{7,3},{8,12},{9,13},{14,10},{15,11},{16,20},{17,... | collective-permute-start | bytes 1572872 | tf_op jit(solution)/shard_map/ppermute | solution.py:83
  18.1 50.7 %copy-start.4 = (bf16[128,2048]{1,0:T(8,128)(2,1)}, bf16[128,2048]{1,0:T(8,128)(2,1)S(1)}, u32[]{:S(2)}) copy-start(bf16[128,2048]{1,0:T(8,128)(2,1)S(1)} %collective-permute-done.1.own_ref) | copy-start | bytes 1572868
  18.1 19.0 %collective-permute-start.2 = (bf16[128,2048]{1,0:T(8,128)(2,1)S(1)}, bf16[128,2048]{1,0:T(8,128)(2,1)S(1)}, u32[]{:S(2)}, u32[]{:S(2)}) collective-permute-start(bf16[128,2048]{1,0:T(8,128)(2,1)S(1)} %collective-permute-done.1.own_ref), channel_id=1, source_target_pairs={{4,6},{5,7},{12,14},{13,15},{20,22},{21,23},{28,30},{29,31}} | collective-permute-start | bytes 1572872 | tf_op jit(solution)/shard_map/ppermute | solution.py:83
  27.9 40.9 %copy-start.3 = (bf16[128,2048]{1,0:T(8,128)(2,1)}, bf16[128,2048]{1,0:T(8,128)(2,1)S(1)}, u32[]{:S(2)}) copy-start(bf16[128,2048]{1,0:T(8,128)(2,1)S(1)} %collective-permute-done.3.own_ref) | copy-start | bytes 1572868
  27.9 15.2 %collective-permute-start.4 = (bf16[128,2048]{1,0:T(8,128)(2,1)S(1)}, bf16[128,2048]{1,0:T(8,128)(2,1)S(1)}, u32[]{:S(2)}, u32[]{:S(2)}) collective-permute-start(bf16[128,2048]{1,0:T(8,128)(2,1)S(1)} %collective-permute-done.3.own_ref), channel_id=1, source_target_pairs={{2,0},{3,1},{10,8},{11,9},{18,16},{19,17},{26,24},{27,25}} | collective-permute-start | bytes 1572872 | tf_op jit(solution)/shard_map/ppermute | solution.py:83
  29.2 34.1 %collective-permute-start.12 = (bf16[128,2048]{1,0:T(8,128)(2,1)}, bf16[128,2048]{1,0:T(8,128)(2,1)S(1)}, u32[]{:S(2)}, u32[]{:S(2)}) collective-permute-start(bf16[128,2048]{1,0:T(8,128)(2,1)} %own_ref.1), channel_id=1, source_target_pairs={{0,1},{1,0},{2,3},{3,2},{4,5},{5,4},{6,7},{7,6},{8,9},{9,8},{10,11... | collective-permute-start | bytes 1572872 | tf_op jit(solution)/shard_map/ppermute | solution.py:83
  29.3 39.5 %collective-permute-start.11 = (bf16[128,2048]{1,0:T(8,128)(2,1)S(1)}, bf16[128,2048]{1,0:T(8,128)(2,1)S(1)}, u32[]{:S(2)}, u32[]{:S(2)}) collective-permute-start(bf16[128,2048]{1,0:T(8,128)(2,1)S(1)} %collective-permute-done.1.own_ref), channel_id=1, source_target_pairs={{0,1},{1,0},{2,3},{3,2},{4,5},{5,4},{6,7},{7,6},{8,9},{9,8},{10,11... | collective-permute-start | bytes 1572872 | tf_op jit(solution)/shard_map/ppermute | solution.py:83
  37.1 37.5 %collective-permute-start.10 = (bf16[128,2048]{1,0:T(8,128)(2,1)S(1)}, bf16[128,2048]{1,0:T(8,128)(2,1)S(1)}, u32[]{:S(2)}, u32[]{:S(2)}) collective-permute-start(bf16[128,2048]{1,0:T(8,128)(2,1)S(1)} %collective-permute-done.3.own_ref), channel_id=1, source_target_pairs={{0,1},{1,0},{2,3},{3,2},{4,5},{5,4},{6,7},{7,6},{8,9},{9,8},{10,11... | collective-permute-start | bytes 1572872 | tf_op jit(solution)/shard_map/ppermute | solution.py:83
  43.2 25.6 %copy-start = (bf16[128,2048]{1,0:T(8,128)(2,1)}, bf16[128,2048]{1,0:T(8,128)(2,1)S(1)}, u32[]{:S(2)}) copy-start(bf16[128,2048]{1,0:T(8,128)(2,1)S(1)} %add_add_fusion.own_ref) | copy-start | bytes 1572868
  43.2 37.3 %collective-permute-start.5 = (bf16[128,2048]{1,0:T(8,128)(2,1)S(1)}, bf16[128,2048]{1,0:T(8,128)(2,1)}, u32[]{:S(2)}, u32[]{:S(2)}) collective-permute-start(bf16[128,2048]{1,0:T(8,128)(2,1)S(1)} %add_add_fusion.own_ref), channel_id=1, source_target_pairs={{0,1},{1,0},{2,3},{3,2},{4,5},{5,4},{6,7},{7,6},{8,9},{9,8},{10,11... | collective-permute-start | bytes 1572872 | tf_op jit(solution)/shard_map/ppermute | solution.py:83
  43.3 2.0 %collective-permute-start.6 = (s32[4,128]{1,0:T(4,128)S(1)}, s32[4,128]{1,0:T(4,128)S(1)}, u32[]{:S(2)}, u32[]{:S(2)}) collective-permute-start(s32[4,128]{1,0:T(4,128)S(1)} %bitcast.23), channel_id=1, source_target_pairs={{0,1},{1,0},{2,3},{3,2},{4,5},{5,4},{6,7},{7,6},{8,9},{9,8},{10,11... | collective-permute-start | bytes 6152 | tf_op jit(solution)/shard_map/ppermute | solution.py:83
  45.3 8.8 %collective-permute-start.7 = (s32[8,128]{1,0:T(8,128)S(1)}, s32[8,128]{1,0:T(8,128)S(1)}, u32[]{:S(2)}, u32[]{:S(2)}) collective-permute-start(s32[8,128]{1,0:T(8,128)S(1)} %pad_add_fusion), channel_id=1, source_target_pairs={{0,2},{1,3},{2,4},{3,5},{4,6},{5,7},{6,0},{7,1},{8,10},{9,11},{10,... | collective-permute-start | bytes 12296 | tf_op jit(solution)/shard_map/ppermute | solution.py:83
  54.1 4.5 %collective-permute-start.8 = (s32[8,128]{1,0:T(8,128)S(1)}, s32[8,128]{1,0:T(8,128)S(1)}, u32[]{:S(2)}, u32[]{:S(2)}) collective-permute-start(s32[8,128]{1,0:T(8,128)S(1)} %pad_add_fusion), channel_id=1, source_target_pairs={{0,4},{1,5},{2,6},{3,7},{4,0},{5,1},{6,2},{7,3},{8,12},{9,13},{10,... | collective-permute-start | bytes 12296 | tf_op jit(solution)/shard_map/ppermute | solution.py:83
  58.6 3.6 %collective-permute-start.9 = (s32[8,128]{1,0:T(8,128)S(1)}, s32[8,128]{1,0:T(8,128)S(1)}, u32[]{:S(2)}, u32[]{:S(2)}) collective-permute-start(s32[8,128]{1,0:T(8,128)S(1)} %pad_add_fusion), channel_id=1, source_target_pairs={{0,6},{1,7},{2,0},{3,1},{4,2},{5,3},{6,4},{7,5},{8,14},{9,15},{10,... | collective-permute-start | bytes 12296 | tf_op jit(solution)/shard_map/ppermute | solution.py:83
  63.3 0.8 copy-start.2
  68.8 0.8 copy-start.5
  74.6 0.8 copy-start.6
  85.5 22.2 %collective-permute-start.13 = (f32[512,512]{1,0:T(8,128)}, f32[512,512]{1,0:T(8,128)S(1)}, u32[]{:S(2)}, u32[]{:S(2)}) collective-permute-start(f32[512,512]{1,0:T(8,128)} %hidden_gram_2.1.mine_ref), channel_id=1, source_target_pairs={{0,8},{8,0},{1,9},{9,1},{2,10},{10,2},{3,11},{11,3},{4,12},{12,4},... | collective-permute-start | bytes 3145736 | tf_op jit(solution)/shard_map/ppermute | solution.py:229
  107.7 1.0 copy-start.1

commit v3 on v2

--- a/solution.py
+++ b/solution.py
@@ -7,105 +7,94 @@
 from jax.experimental.pallas import tpu as pltpu
 from jax.sharding import PartitionSpec as P
 
+
 RIDGE = 0.05
 CORES = 2
-
-
-def hidden_gram_kernel(own_ref, other_ref, member_ref, gate_ref, up_ref, *rest):
-    first = len(rest) == 2
-    gram_in_ref = None if first else rest[0]
+CHIPS_DENSE = 4
+
+
+def hidden_gram_kernel(me_ref, own_ref, other_ref, own_names_ref, other_names_ref, gate_ref, up_ref, *rest, slot):
     gram_ref, hidden_ref = rest[-2:]
-    step = pl.program_id(0)
-    rows = own_ref.shape[0]
-    width = gate_ref.shape[1]
-    gate_block = gate_ref[...]
-    up_block = up_ref[...]
+    hw = gate_ref.shape[1]
+    width = 256
+    top = own_names_ref.shape[0] // CHIPS_DENSE
+    mine = slice(slot * top, (slot + 1) * top)
+    named = jnp.concatenate([own_names_ref[mine, :], other_names_ref[mine, :]], axis=0) == me_ref[0]
+    named = named.astype(jnp.float32).T
+    member = jnp.concatenate(
+        [jnp.max(named[:, c * top : (c + 1) * top], axis=1, keepdims=True) for c in range(CORES)], axis=0
+    )
     x = jnp.concatenate([own_ref[...], other_ref[...]], axis=0)
-    gate = jnp.dot(x, gate_block, preferred_element_type=jnp.float32)
-    up = jnp.dot(x, up_block, preferred_element_type=jnp.float32)
-    value = gate / (1.0 + jnp.exp(-gate)) * up
-    value = jnp.where(member_ref[...] > 0, value, 0.0)
-    hidden_ref[:, pl.ds(pl.multiple_of(step * width, width), width)] = value.astype(jnp.bfloat16)
-
-    @pl.when(step == pl.num_programs(0) - 1)
-    def _():
-        h = hidden_ref[...]
-        gram = lax.dot_general(h, h, (((0,), (0,)), ((), ())), preferred_element_type=jnp.float32)
-        if first:
-            gram_ref[...] = gram
-        else:
-            gram_ref[...] = gram_in_ref[...] + gram
-
-
-def hidden_gram(own, other, member, slot, gate_w, up_w, gram=None, width=256):
+
+    def step(i, carry):
+        at = pl.ds(pl.multiple_of(i * width, width), width)
+        gate = jnp.dot(x, gate_ref[:, at], preferred_element_type=jnp.float32)
+        up = jnp.dot(x, up_ref[:, at], preferred_element_type=jnp.float32)
+        value = gate / (1.0 + jnp.exp(-gate)) * up
+        hidden_ref[:, at] = jnp.where(member > 0, value, 0.0).astype(jnp.bfloat16)
+        return carry
+
+    lax.fori_loop(0, hw // width, step, 0)
+    h = hidden_ref[...]
+    gram = lax.dot_general(h, h, (((0,), (0,)), ((), ())), preferred_element_type=jnp.float32)
+    gram_ref[...] = gram if len(rest) == 2 else rest[0][...] + gram
+
+
+def hidden_gram(me, own, other, own_names, other_names, slot, gate_w, up_w, gram=None):
     rows, model = own.shape
     hw = gate_w.shape[1]
-    whole = lambda i: (0, 0)
-    in_specs = [
-        pl.BlockSpec((rows, model), whole),
-        pl.BlockSpec((rows, model), whole),
-        pl.BlockSpec((2 * rows, 1), lambda i: (slot, 0)),
-        pl.BlockSpec((model, width), lambda i: (0, i)),
-        pl.BlockSpec((model, width), lambda i: (0, i)),
-    ]
-    args = [own, other, member, gate_w, up_w]
+    args = [me, own, other, own_names, other_names, gate_w, up_w]
+    in_specs = [pl.BlockSpec(memory_space=pltpu.SMEM)] + [pl.BlockSpec(memory_space=pltpu.VMEM)] * 6
     aliases = {}
     if gram is not None:
-        in_specs.append(pl.BlockSpec((hw, hw), whole))
+        in_specs.append(pl.BlockSpec(memory_space=pltpu.VMEM))
         args.append(gram)
-        aliases = {5: 0}
+        aliases = {7: 0}
     return pl.pallas_call(
-        hidden_gram_kernel,
-        grid=(hw // width,),
+        functools.partial(hidden_gram_kernel, slot=slot),
         in_specs=in_specs,
-        out_specs=pl.BlockSpec((hw, hw), whole),
+        out_specs=pl.BlockSpec(memory_space=pltpu.VMEM),
         out_shape=jax.ShapeDtypeStruct((hw, hw), jnp.float32),
-        scratch_shapes=[pltpu.VMEM((2 * rows, hw), jnp.bfloat16)],
+        scratch_shapes=[pltpu.VMEM((CORES * rows, hw), jnp.bfloat16)],
         input_output_aliases=aliases,
-        compiler_params=pltpu.CompilerParams(dimension_semantics=("arbitrary",)),
+        compiler_params=pltpu.CompilerParams(vmem_limit_bytes=24 << 20),
         cost_estimate=pl.CostEstimate(
-            flops=2 * 2 * rows * model * 2 * hw + 2 * 2 * rows * hw * hw,
-            bytes_accessed=2 * (2 * rows * model + 2 * model * hw) + 4 * hw * hw,
-            transcendentals=2 * rows * hw,
+            flops=2 * CORES * rows * model * 2 * hw + 2 * CORES * rows * hw * hw,
+            bytes_accessed=2 * (CORES * rows * model + 2 * model * hw) + 4 * hw * hw,
+            transcendentals=CORES * rows * hw,
         ),
-        name=f"hidden_gram_{slot}",
     )(*args)
 
 
-def shifted(pairs):
+def between_chips(pairs):
     return [(s * CORES + c, d * CORES + c) for s, d in pairs for c in range(CORES)]
 
 
 def gather_grams(tokens, routes, gate_w, up_w):
-    owners = lax.axis_size("expert")
-    chips = owners // CORES
     me = lax.axis_index("expert")
-    move = lambda x, pairs: lax.ppermute(x, "expert", pairs)
-    swap = [(e, e ^ 1) for e in range(owners)]
-    ring = lambda s: shifted([(z, (z + s) % chips) for z in range(chips)])
-
-    direct = {}
-    if chips == 4:
-        direct[1] = move(tokens, ring(1))
-        direct[3] = move(tokens, ring(-1))
-        far = move(tokens, shifted([(0, 2), (3, 1)]))
-        on_up = move(direct[1], shifted([(2, 3)]))
-        on_down = move(direct[3], shifted([(1, 0)]))
-        direct[2] = far + on_up + on_down
-    else:
-        for s in range(1, chips):
-            direct[s] = move(tokens, ring(s))
+    move = lambda x, pairs: lax.ppermute(x, "expert", between_chips(pairs))
+    swap = lambda x: lax.ppermute(x, "expert", [(e, e ^ 1) for e in range(CHIPS_DENSE * CORES)])
+    near = [(z, z ^ 1) for z in range(CHIPS_DENSE)]
+    cross = [(z, z ^ 3) for z in range(CHIPS_DENSE)]
+    two = [(z, z ^ 2) for z in range(CHIPS_DENSE)]
 
     names = routes.T
-    pair = jnp.concatenate([names, move(names, swap)], axis=0)
-    named = [pair] + [move(pair, ring(s)) for s in range(1, chips)]
-    named = jnp.stack(named).reshape(chips, CORES, routes.shape[1], routes.shape[0])
-    member = jnp.any(named == me, axis=2).astype(jnp.float32).reshape(-1, 1)
-
-    gram = hidden_gram(tokens, move(tokens, swap), member, 0, gate_w, up_w)
-    order = [1, 3, 2] if chips == 4 else list(range(1, chips))
-    for s in order:
-        gram = hidden_gram(direct[s], move(direct[s], swap), member, s, gate_w, up_w, gram)
+    first = move(tokens, near)
+    named = [names]
+    for pairs in [near, cross, two]:
+        named.append(move(names, pairs))
+    own_names = jnp.concatenate(named, axis=0)
+    other_names = swap(own_names)
+    second = move(tokens, cross)
+    far = move(tokens, [(0, 2), (3, 1)])
+    onward = move(second, [(1, 0), (2, 3)])
+    third = far + onward
+
+    me = me.astype(jnp.int32).reshape(1)
+    gram = None
+    for slot, own in enumerate([tokens, first, second, third]):
+        other = swap(own)
+        gram = hidden_gram(me, own, other, own_names, other_names, slot, gate_w, up_w, gram)
     return gram
 
 
@@ -139,7 +128,7 @@
     tok_rows, top_count = routes.shape
     capacity = min(tok_rows, 2 * tok_rows * top_count // experts)
     gate_w, up_w = w_gate[0], w_up[0]
-    if tok_rows * owners <= experts * capacity and owners % CORES == 0:
+    if tok_rows * owners <= experts * capacity and owners == CHIPS_DENSE * CORES:
         gram_local = gather_grams(tokens, routes, gate_w, up_w)
     else:
         gram_local = packed_grams(tokens, routes, gate_w, up_w, capacity)

time: 146 us -> 137 us (0.938)
  Pallas kernels: 55 us -> 46.7 us
  starting transfers between devices: 14.9 us -> 13.4 us
  waiting for transfers between devices: 69.4 us -> 67.9 us
    pallas_call x4, Pallas kernels: 19.7 us -> 11.5 us  [hidden_gram(): pl.pallas_call(functools.partial(hidden_gram_kernel, slot=slot), in_specs...]
    ppermute x13 -> x12, waiting for transfers between devices: 48.6 us -> 44.2 us  [the longest x7 43 us: gather_grams(): move = lambda x, pairs: lax.ppermute(x, 'expert', between_chips(pairs))]
    ppermute x1, waiting for transfers between devices: 20.8 us -> 23.7 us  [finish(): lax.ppermute(gram_local, 'dp', [(r, (r + s) % data_ranks) for r in range(...]
    unnamed x16 -> x14, local copies, waits for them, and re-layouts: 3.37 us -> 5.37 us
    ppermute x13 -> x12, starting transfers between devices: 13.4 us -> 11.9 us  [the longest x7 11.2 us: gather_grams(): move = lambda x, pairs: lax.ppermute(x, 'expert', between_chips(pairs))]
  transfers between devices with their start and end apart: 14 -> 13, of which waited for: 9 -> 9; matrix products, arithmetic and copies ran while one was open for 1% -> 1% of each run, Pallas kernels for 10% -> 6%
where the time goes in v3:
time: 137 us; the launch traced here: 136 us
  waiting for transfers between devices  67.9 us (50%)
  Pallas kernels  46.7 us (34%)
  starting transfers between devices  13.4 us (10%)
  local copies, waits for them, and re-layouts  7.23 us (5%)
    ppermute x7, waiting for transfers between devices, gather_grams(): move = lambda x, pairs: lax.ppermute(x, 'expert', between_chips(pairs))  43 us
    pallas_call x1, Pallas kernels, factor_of(): pl.pallas_call(functools.partial(factor_kernel, rows_mean=rows_mean), in_...  35.3 us
    ppermute x1, waiting for transfers between devices, finish(): lax.ppermute(gram_local, 'dp', [(r, (r + s) % data_ranks) for r in range(...  23.7 us
    pallas_call x4, Pallas kernels, hidden_gram(): pl.pallas_call(functools.partial(hidden_gram_kernel, slot=slot), in_specs...  11.5 us
    ppermute x7, starting transfers between devices, gather_grams(): move = lambda x, pairs: lax.ppermute(x, 'expert', between_chips(pairs))  11.2 us
    unnamed x14, local copies, waits for them, and re-layouts  5.37 us
  transfers between devices with their start and end apart: 13, of which 9 were waited for; matrix products, arithmetic and copies ran while one was open for 1% of the time, Pallas kernels for 6%

profile of v3, /device:TPU:0, one launch (start us, length us, event | category | flops | bytes accessed | tf_op | source)
XLA Modules:
  0.0 136.2 jit_solution(6939815293101038221)
XLA Ops:
  0.0 5.1 %collective-permute-start.1 = (bf16[128,2048]{1,0:T(8,128)(2,1)}, bf16[128,2048]{1,0:T(8,128)(2,1)S(1)}, u32[]{:S(2)}, u32[]{:S(2)}) collective-permute-start(bf16[128,2048]{1,0:T(8,128)(2,1)} %own_ref.1), channel_id=1, source_target_pairs={{0,6},{1,7},{2,4},{3,5},{4,2},{5,3},{6,0},{7,1},{8,14},{9,15},{10,... | collective-permute-start | bytes 1572872 | tf_op jit(solution)/shard_map/ppermute | solution.py:75
  5.1 2.5 %collective-permute-start = (bf16[128,2048]{1,0:T(8,128)(2,1)}, bf16[128,2048]{1,0:T(8,128)(2,1)S(1)}, u32[]{:S(2)}, u32[]{:S(2)}) collective-permute-start(bf16[128,2048]{1,0:T(8,128)(2,1)} %own_ref.1), channel_id=1, source_target_pairs={{0,4},{1,5},{6,2},{7,3},{8,12},{9,13},{14,10},{15,11},{16,20},{17,... | collective-permute-start | bytes 1572872 | tf_op jit(solution)/shard_map/ppermute | solution.py:75
  7.6 10.6 %collective-permute-done.1.own_ref = bf16[128,2048]{1,0:T(8,128)(2,1)S(1)} collective-permute-done((bf16[128,2048]{1,0:T(8,128)(2,1)}, bf16[128,2048]{1,0:T(8,128)(2,1)S(1)}, u32[]{:S(2)}, u32[]{:S(2)}) %collective-permute-start.1) | collective-permute-done | bytes 524320 | tf_op jit(solution)/shard_map/ppermute | solution.py:75
  18.2 1.3 collective-permute-start.2
  19.5 9.4 %collective-permute-done.9.own_ref = bf16[128,2048]{1,0:T(8,128)(2,1)S(1)} collective-permute-done((bf16[128,2048]{1,0:T(8,128)(2,1)}, bf16[128,2048]{1,0:T(8,128)(2,1)S(1)}, u32[]{:S(2)}, u32[]{:S(2)}) %collective-permute-start.9) | collective-permute-done | bytes 524320 | tf_op jit(solution)/shard_map/ppermute | solution.py:75
  29.5 9.6 %collective-permute-done = bf16[128,2048]{1,0:T(8,128)(2,1)S(1)} collective-permute-done((bf16[128,2048]{1,0:T(8,128)(2,1)}, bf16[128,2048]{1,0:T(8,128)(2,1)S(1)}, u32[]{:S(2)}, u32[]{:S(2)}) %collective-permute-start) | collective-permute-done | bytes 524320 | tf_op jit(solution)/shard_map/ppermute | solution.py:75
  39.1 1.6 %collective-permute-done.2 = bf16[128,2048]{1,0:T(8,128)(2,1)S(1)} collective-permute-done((bf16[128,2048]{1,0:T(8,128)(2,1)S(1)}, bf16[128,2048]{1,0:T(8,128)(2,1)S(1)}, u32[]{:S(2)}, u32[]{:S(2)}) %collective-permute-start.2) | collective-permute-done | bytes 524320 | tf_op jit(solution)/shard_map/ppermute | solution.py:75
  41.0 3.8 %collective-permute-done.4 = s32[4,128]{1,0:T(4,128)S(1)} collective-permute-done((s32[4,128]{1,0:T(4,128)}, s32[4,128]{1,0:T(4,128)S(1)}, u32[]{:S(2)}, u32[]{:S(2)}) %collective-permute-start.4) | collective-permute-done | bytes 2080 | tf_op jit(solution)/shard_map/ppermute | solution.py:75
  44.8 2.3 %collective-permute-start.5 = (s32[4,128]{1,0:T(4,128)}, s32[4,128]{1,0:T(4,128)S(1)}, u32[]{:S(2)}, u32[]{:S(2)}) collective-permute-start(s32[4,128]{1,0:T(4,128)} %bitcast.15), channel_id=1, source_target_pairs={{0,6},{1,7},{2,4},{3,5},{4,2},{5,3},{6,0},{7,1},{8,14},{9,15},{10,... | collective-permute-start | bytes 6152 | tf_op jit(solution)/shard_map/ppermute | solution.py:75
  47.0 3.3 %collective-permute-done.5 = s32[4,128]{1,0:T(4,128)S(1)} collective-permute-done((s32[4,128]{1,0:T(4,128)}, s32[4,128]{1,0:T(4,128)S(1)}, u32[]{:S(2)}, u32[]{:S(2)}) %collective-permute-start.5) | collective-permute-done | bytes 2080 | tf_op jit(solution)/shard_map/ppermute | solution.py:75
  50.4 4.7 %collective-permute-done.6 = s32[4,128]{1,0:T(4,128)S(1)} collective-permute-done((s32[4,128]{1,0:T(4,128)}, s32[4,128]{1,0:T(4,128)S(1)}, u32[]{:S(2)}, u32[]{:S(2)}) %collective-permute-start.6) | collective-permute-done | bytes 2080 | tf_op jit(solution)/shard_map/ppermute | solution.py:75
  55.7 1.2 collective-permute-done.7.other_names_ref
  56.9 1.6 %copy-done = bf16[1,2048,512]{2,1,0:T(8,128)(2,1)S(1)} copy-done((bf16[1,2048,512]{2,1,0:T(8,128)(2,1)S(1)}, bf16[1,2048,512]{2,1,0:T(8,128)(2,1)}, u32[]{:S(2)}) %copy-start) | copy-done | bytes 2097176
  58.5 1.6 %copy-done.2 = bf16[1,2048,512]{2,1,0:T(8,128)(2,1)S(1)} copy-done((bf16[1,2048,512]{2,1,0:T(8,128)(2,1)S(1)}, bf16[1,2048,512]{2,1,0:T(8,128)(2,1)}, u32[]{:S(2)}) %copy-start.2) | copy-done | bytes 2097176
  60.1 1.0 copy-done.5
  61.1 2.0 %shard_map.46.rest_0_ = f32[512,512]{1,0:T(8,128)S(1)} custom-call(s32[1]{0:T(128)} %bitcast.me_ref, bf16[128,2048]{1,0:T(8,128)(2,1)S(1)} %copy-done.5, bf16[128,2048]{1,0:T(8,128)(2,1)S(1)} %collective-permute-done.11.other_ref, s32[16,128]{1,0:T(8,128)S(1)} %pad_add_fusion.own_names_ref, s32[16,128]{1,0:T(8,128)S(1)} %collective-permute-done.7.other_names_ref, ...), custom_call_target="tpu_custom_call" | custom-call | flops 1207959552 | bytes 6291456 | tf_op jit(solution)/shard_map/pallas_call | solution.py:53
  63.4 3.1 %shard_map.47.rest_0_ = f32[512,512]{1,0:T(8,128)S(1)} custom-call(s32[1]{0:T(128)} %bitcast.me_ref, bf16[128,2048]{1,0:T(8,128)(2,1)S(1)} %collective-permute-done.9.own_ref, bf16[128,2048]{1,0:T(8,128)(2,1)} %collective-permute-done.10.other_ref, s32[16,128]{1,0:T(8,128)S(1)} %pad_add_fusion.own_names_ref, ...), custom_call_target="tpu_custom_call", output_to_operand_aliasing={{}: (7, {})} | custom-call | flops 1207959552 | bytes 6291456 | tf_op jit(solution)/shard_map/pallas_call | solution.py:53
  66.5 3.1 %shard_map.48.rest_0_ = f32[512,512]{1,0:T(8,128)S(1)} custom-call(s32[1]{0:T(128)} %bitcast.me_ref, bf16[128,2048]{1,0:T(8,128)(2,1)S(1)} %collective-permute-done.1.own_ref, bf16[128,2048]{1,0:T(8,128)(2,1)} %collective-permute-done.8.other_ref, s32[16,128]{1,0:T(8,128)S(1)} %pad_add_fusion.own_names_ref, ...), custom_call_target="tpu_custom_call", output_to_operand_aliasing={{}: (7, {})} | custom-call | flops 1207959552 | bytes 6291456 | tf_op jit(solution)/shard_map/pallas_call | solution.py:53
  69.7 3.1 %shard_map.49.mine_ref = f32[512,512]{1,0:T(8,128)S(1)} custom-call(s32[1]{0:T(128)} %bitcast.me_ref, bf16[128,2048]{1,0:T(8,128)(2,1)S(1)} %add.6.own_ref, bf16[128,2048]{1,0:T(8,128)(2,1)} %collective-permute-done.3.other_ref, s32[16,128]{1,0:T(8,128)S(1)} %pad_add_fusion.own_names_ref, ...), custom_call_target="tpu_custom_call", output_to_operand_aliasing={{}: (7, {})} | custom-call | flops 1207959552 | bytes 6291456 | tf_op jit(solution)/shard_map/pallas_call | solution.py:53
  72.8 1.6 %collective-permute-start.12 = (f32[512,512]{1,0:T(8,128)S(1)}, f32[512,512]{1,0:T(8,128)S(1)}, u32[]{:S(2)}, u32[]{:S(2)}) collective-permute-start(f32[512,512]{1,0:T(8,128)S(1)} %shard_map.49.mine_ref), channel_id=1, source_target_pairs={{0,8},{8,0},{1,9},{9,1},{2,10},{10,2},{3,11},{11,3},{4,12},{12,4},... | collective-permute-start | bytes 3145736 | tf_op jit(solution)/shard_map/ppermute | solution.py:218
  74.4 23.7 %collective-permute-done.12.theirs_ref = f32[512,512]{1,0:T(8,128)S(1)} collective-permute-done((f32[512,512]{1,0:T(8,128)S(1)}, f32[512,512]{1,0:T(8,128)S(1)}, u32[]{:S(2)}, u32[]{:S(2)}) %collective-permute-start.12) | collective-permute-done | bytes 1048608 | tf_op jit(solution)/shard_map/ppermute | solution.py:218
  98.1 1.0 copy-done.6
  99.1 35.3 %factor.1 = f32[512,512]{1,0:T(8,128)} custom-call(f32[512,512]{1,0:T(8,128)} %copy-done.4, f32[512,512]{1,0:T(8,128)} %copy-done.6), custom_call_target="tpu_custom_call" | custom-call | tf_op jit(solution)/shard_map/factor/pallas_call | solution.py:203
  134.4 1.9 %dynamic-slice_bitcast_fusion = f32[1,256,512]{2,1,0:T(8,128)} fusion(f32[512,512]{1,0:T(8,128)} %factor.1, s32[]{:T(128)S(6)} %select_n.3), kind=kLoop, calls=%fused_computation | loop fusion | bytes 1048580 | tf_op jit(solution)/shard_map/reshape | solution.py:222
  (24 shorter events, 1.7 us)
Async XLA Ops:
  0.0 18.2 %collective-permute-start.1 = (bf16[128,2048]{1,0:T(8,128)(2,1)}, bf16[128,2048]{1,0:T(8,128)(2,1)S(1)}, u32[]{:S(2)}, u32[]{:S(2)}) collective-permute-start(bf16[128,2048]{1,0:T(8,128)(2,1)} %own_ref.1), channel_id=1, source_target_pairs={{0,6},{1,7},{2,4},{3,5},{4,2},{5,3},{6,0},{7,1},{8,14},{9,15},{10,... | collective-permute-start | bytes 1572872 | tf_op jit(solution)/shard_map/ppermute | solution.py:75
  5.1 23.9 %collective-permute-start.9 = (bf16[128,2048]{1,0:T(8,128)(2,1)}, bf16[128,2048]{1,0:T(8,128)(2,1)S(1)}, u32[]{:S(2)}, u32[]{:S(2)}) collective-permute-start(bf16[128,2048]{1,0:T(8,128)(2,1)} %own_ref.1), channel_id=1, source_target_pairs={{0,2},{1,3},{2,0},{3,1},{4,6},{5,7},{6,4},{7,5},{8,10},{9,11},{10,... | collective-permute-start | bytes 1572872 | tf_op jit(solution)/shard_map/ppermute | solution.py:75
  5.1 34.0 %collective-permute-start = (bf16[128,2048]{1,0:T(8,128)(2,1)}, bf16[128,2048]{1,0:T(8,128)(2,1)S(1)}, u32[]{:S(2)}, u32[]{:S(2)}) collective-permute-start(bf16[128,2048]{1,0:T(8,128)(2,1)} %own_ref.1), channel_id=1, source_target_pairs={{0,4},{1,5},{6,2},{7,3},{8,12},{9,13},{14,10},{15,11},{16,20},{17,... | collective-permute-start | bytes 1572872 | tf_op jit(solution)/shard_map/ppermute | solution.py:75
  18.2 22.5 %collective-permute-start.2 = (bf16[128,2048]{1,0:T(8,128)(2,1)S(1)}, bf16[128,2048]{1,0:T(8,128)(2,1)S(1)}, u32[]{:S(2)}, u32[]{:S(2)}) collective-permute-start(bf16[128,2048]{1,0:T(8,128)(2,1)S(1)} %collective-permute-done.1.own_ref), channel_id=1, source_target_pairs={{2,0},{3,1},{4,6},{5,7},{10,8},{11,9},{12,14},{13,15},{18,16},{19,... | collective-permute-start | bytes 1572872 | tf_op jit(solution)/shard_map/ppermute | solution.py:75
  19.4 37.5 %collective-permute-start.11 = (bf16[128,2048]{1,0:T(8,128)(2,1)}, bf16[128,2048]{1,0:T(8,128)(2,1)S(1)}, u32[]{:S(2)}, u32[]{:S(2)}) collective-permute-start(bf16[128,2048]{1,0:T(8,128)(2,1)} %own_ref.1), channel_id=1, source_target_pairs={{0,1},{1,0},{2,3},{3,2},{4,5},{5,4},{6,7},{7,6},{8,9},{9,8},{10,11... | collective-permute-start | bytes 1572872 | tf_op jit(solution)/shard_map/ppermute | solution.py:76
  28.9 34.2 %collective-permute-start.10 = (bf16[128,2048]{1,0:T(8,128)(2,1)S(1)}, bf16[128,2048]{1,0:T(8,128)(2,1)}, u32[]{:S(2)}, u32[]{:S(2)}) collective-permute-start(bf16[128,2048]{1,0:T(8,128)(2,1)S(1)} %collective-permute-done.9.own_ref), channel_id=1, source_target_pairs={{0,1},{1,0},{2,3},{3,2},{4,5},{5,4},{6,7},{7,6},{8,9},{9,8},{10,11... | collective-permute-start | bytes 1572872 | tf_op jit(solution)/shard_map/ppermute | solution.py:76
  28.9 37.6 %collective-permute-start.8 = (bf16[128,2048]{1,0:T(8,128)(2,1)S(1)}, bf16[128,2048]{1,0:T(8,128)(2,1)}, u32[]{:S(2)}, u32[]{:S(2)}) collective-permute-start(bf16[128,2048]{1,0:T(8,128)(2,1)S(1)} %collective-permute-done.1.own_ref), channel_id=1, source_target_pairs={{0,1},{1,0},{2,3},{3,2},{4,5},{5,4},{6,7},{7,6},{8,9},{9,8},{10,11... | collective-permute-start | bytes 1572872 | tf_op jit(solution)/shard_map/ppermute | solution.py:76
  40.8 28.9 %collective-permute-start.3 = (bf16[128,2048]{1,0:T(8,128)(2,1)S(1)}, bf16[128,2048]{1,0:T(8,128)(2,1)}, u32[]{:S(2)}, u32[]{:S(2)}) collective-permute-start(bf16[128,2048]{1,0:T(8,128)(2,1)S(1)} %add.6.own_ref), channel_id=1, source_target_pairs={{0,1},{1,0},{2,3},{3,2},{4,5},{5,4},{6,7},{7,6},{8,9},{9,8},{10,11... | collective-permute-start | bytes 1572872 | tf_op jit(solution)/shard_map/ppermute | solution.py:76
  40.9 3.9 %collective-permute-start.4 = (s32[4,128]{1,0:T(4,128)}, s32[4,128]{1,0:T(4,128)S(1)}, u32[]{:S(2)}, u32[]{:S(2)}) collective-permute-start(s32[4,128]{1,0:T(4,128)} %bitcast.14), channel_id=1, source_target_pairs={{0,2},{1,3},{2,0},{3,1},{4,6},{5,7},{6,4},{7,5},{8,10},{9,11},{10,... | collective-permute-start | bytes 6152 | tf_op jit(solution)/shard_map/ppermute | solution.py:75
  44.8 5.6 %collective-permute-start.5 = (s32[4,128]{1,0:T(4,128)}, s32[4,128]{1,0:T(4,128)S(1)}, u32[]{:S(2)}, u32[]{:S(2)}) collective-permute-start(s32[4,128]{1,0:T(4,128)} %bitcast.15), channel_id=1, source_target_pairs={{0,6},{1,7},{2,4},{3,5},{4,2},{5,3},{6,0},{7,1},{8,14},{9,15},{10,... | collective-permute-start | bytes 6152 | tf_op jit(solution)/shard_map/ppermute | solution.py:75
  50.3 4.7 %collective-permute-start.6 = (s32[4,128]{1,0:T(4,128)}, s32[4,128]{1,0:T(4,128)S(1)}, u32[]{:S(2)}, u32[]{:S(2)}) collective-permute-start(s32[4,128]{1,0:T(4,128)} %bitcast.16), channel_id=1, source_target_pairs={{0,4},{1,5},{2,6},{3,7},{4,0},{5,1},{6,2},{7,3},{8,12},{9,13},{10,... | collective-permute-start | bytes 6152 | tf_op jit(solution)/shard_map/ppermute | solution.py:75
  55.7 1.2 collective-permute-start.7
  56.9 1.6 %copy-start = (bf16[1,2048,512]{2,1,0:T(8,128)(2,1)S(1)}, bf16[1,2048,512]{2,1,0:T(8,128)(2,1)}, u32[]{:S(2)}) copy-start(bf16[1,2048,512]{2,1,0:T(8,128)(2,1)} %param.6) | copy-start | bytes 6291460
  58.5 1.6 %copy-start.2 = (bf16[1,2048,512]{2,1,0:T(8,128)(2,1)S(1)}, bf16[1,2048,512]{2,1,0:T(8,128)(2,1)}, u32[]{:S(2)}) copy-start(bf16[1,2048,512]{2,1,0:T(8,128)(2,1)} %param.7) | copy-start | bytes 6291460
  60.1 1.0 copy-start.5
  61.1 2.1 %copy-start.1 = (bf16[1,2048,512]{2,1,0:T(8,128)(2,1)S(1)}, bf16[1,2048,512]{2,1,0:T(8,128)(2,1)}, u32[]{:S(2)}) copy-start(bf16[1,2048,512]{2,1,0:T(8,128)(2,1)} %param.6) | copy-start | bytes 6291460
  61.1 2.2 %copy-start.3 = (bf16[1,2048,512]{2,1,0:T(8,128)(2,1)S(1)}, bf16[1,2048,512]{2,1,0:T(8,128)(2,1)}, u32[]{:S(2)}) copy-start(bf16[1,2048,512]{2,1,0:T(8,128)(2,1)} %param.7) | copy-start | bytes 6291460
  72.8 25.3 %copy-start.4 = (f32[512,512]{1,0:T(8,128)}, f32[512,512]{1,0:T(8,128)S(1)}, u32[]{:S(2)}) copy-start(f32[512,512]{1,0:T(8,128)S(1)} %shard_map.49.mine_ref) | copy-start | bytes 3145732
  72.8 25.3 %collective-permute-start.12 = (f32[512,512]{1,0:T(8,128)S(1)}, f32[512,512]{1,0:T(8,128)S(1)}, u32[]{:S(2)}, u32[]{:S(2)}) collective-permute-start(f32[512,512]{1,0:T(8,128)S(1)} %shard_map.49.mine_ref), channel_id=1, source_target_pairs={{0,8},{8,0},{1,9},{9,1},{2,10},{10,2},{3,11},{11,3},{4,12},{12,4},... | collective-permute-start | bytes 3145736 | tf_op jit(solution)/shard_map/ppermute | solution.py:218
  98.1 1.0 copy-start.6

commit v4 on v3

--- a/solution.py
+++ b/solution.py
@@ -13,12 +13,10 @@
 CHIPS_DENSE = 4
 
 
-def hidden_gram_kernel(me_ref, own_ref, other_ref, own_names_ref, other_names_ref, gate_ref, up_ref, *rest, slot):
-    gram_ref, hidden_ref = rest[-2:]
+def hidden_kernel(me_ref, own_ref, other_ref, own_names_ref, other_names_ref, gate_ref, up_ref, hidden_ref, *, at, top):
     hw = gate_ref.shape[1]
     width = 256
-    top = own_names_ref.shape[0] // CHIPS_DENSE
-    mine = slice(slot * top, (slot + 1) * top)
+    mine = slice(at * top, (at + 1) * top)
     named = jnp.concatenate([own_names_ref[mine, :], other_names_ref[mine, :]], axis=0) == me_ref[0]
     named = named.astype(jnp.float32).T
     member = jnp.concatenate(
@@ -27,75 +25,101 @@
     x = jnp.concatenate([own_ref[...], other_ref[...]], axis=0)
 
     def step(i, carry):
-        at = pl.ds(pl.multiple_of(i * width, width), width)
-        gate = jnp.dot(x, gate_ref[:, at], preferred_element_type=jnp.float32)
-        up = jnp.dot(x, up_ref[:, at], preferred_element_type=jnp.float32)
+        columns = pl.ds(pl.multiple_of(i * width, width), width)
+        gate = jnp.dot(x, gate_ref[:, columns], preferred_element_type=jnp.float32)
+        up = jnp.dot(x, up_ref[:, columns], preferred_element_type=jnp.float32)
         value = gate / (1.0 + jnp.exp(-gate)) * up
-        hidden_ref[:, at] = jnp.where(member > 0, value, 0.0).astype(jnp.bfloat16)
+        hidden_ref[:, columns] = jnp.where(member > 0, value, 0.0).astype(jnp.bfloat16)
         return carry
 
     lax.fori_loop(0, hw // width, step, 0)
-    h = hidden_ref[...]
-    gram = lax.dot_general(h, h, (((0,), (0,)), ((), ())), preferred_element_type=jnp.float32)
-    gram_ref[...] = gram if len(rest) == 2 else rest[0][...] + gram
-
-
-def hidden_gram(me, own, other, own_names, other_names, slot, gate_w, up_w, gram=None):
+
+
+def hidden_of(me, own, other, own_names, other_names, at, top, gate_w, up_w):
     rows, model = own.shape
     hw = gate_w.shape[1]
-    args = [me, own, other, own_names, other_names, gate_w, up_w]
-    in_specs = [pl.BlockSpec(memory_space=pltpu.SMEM)] + [pl.BlockSpec(memory_space=pltpu.VMEM)] * 6
-    aliases = {}
-    if gram is not None:
-        in_specs.append(pl.BlockSpec(memory_space=pltpu.VMEM))
-        args.append(gram)
-        aliases = {7: 0}
     return pl.pallas_call(
-        functools.partial(hidden_gram_kernel, slot=slot),
-        in_specs=in_specs,
+        functools.partial(hidden_kernel, at=at, top=top),
+        in_specs=[pl.BlockSpec(memory_space=pltpu.SMEM)] + [pl.BlockSpec(memory_space=pltpu.VMEM)] * 6,
+        out_specs=pl.BlockSpec(memory_space=pltpu.VMEM),
+        out_shape=jax.ShapeDtypeStruct((CORES * rows, hw), jnp.bfloat16),
+        compiler_params=pltpu.CompilerParams(vmem_limit_bytes=24 << 20),
+        cost_estimate=pl.CostEstimate(
+            flops=2 * CORES * rows * model * 2 * hw,
+            bytes_accessed=2 * (CORES * rows * model + 2 * model * hw) + 2 * CORES * rows * hw,
+            transcendentals=CORES * rows * hw,
+        ),
+        name="hidden",
+    )(me, own, other, own_names, other_names, gate_w, up_w)
+
+
+def gram_of(refs):
+    total = None
+    for ref in refs:
+        h = ref[...]
+        part = lax.dot_general(h, h, (((0,), (0,)), ((), ())), preferred_element_type=jnp.float32)
+        total = part if total is None else total + part
+    return total
+
+
+def gram_kernel(*refs):
+    refs[-1][...] = gram_of(refs[:-1])
+
+
+def partial_gram(hiddens):
+    rows, hw = hiddens[0].shape
+    return pl.pallas_call(
+        gram_kernel,
+        in_specs=[pl.BlockSpec(memory_space=pltpu.VMEM)] * len(hiddens),
         out_specs=pl.BlockSpec(memory_space=pltpu.VMEM),
         out_shape=jax.ShapeDtypeStruct((hw, hw), jnp.float32),
-        scratch_shapes=[pltpu.VMEM((CORES * rows, hw), jnp.bfloat16)],
-        input_output_aliases=aliases,
         compiler_params=pltpu.CompilerParams(vmem_limit_bytes=24 << 20),
         cost_estimate=pl.CostEstimate(
-            flops=2 * CORES * rows * model * 2 * hw + 2 * CORES * rows * hw * hw,
-            bytes_accessed=2 * (CORES * rows * model + 2 * model * hw) + 4 * hw * hw,
-            transcendentals=CORES * rows * hw,
+            flops=2 * len(hiddens) * rows * hw * hw,
+            bytes_accessed=2 * len(hiddens) * rows * hw + 4 * hw * hw,
+            transcendentals=0,
         ),
-    )(*args)
+        name="partial_gram",
+    )(*hiddens)
 
 
 def between_chips(pairs):
     return [(s * CORES + c, d * CORES + c) for s, d in pairs for c in range(CORES)]
 
 
-def gather_grams(tokens, routes, gate_w, up_w):
-    me = lax.axis_index("expert")
+def gathered(tokens, routes, gate_w, up_w):
+    me = lax.axis_index("expert").astype(jnp.int32).reshape(1)
+    data_ranks = lax.axis_size("dp")
+    top = routes.shape[1]
     move = lambda x, pairs: lax.ppermute(x, "expert", between_chips(pairs))
     swap = lambda x: lax.ppermute(x, "expert", [(e, e ^ 1) for e in range(CHIPS_DENSE * CORES)])
+    turn = lambda x, s: lax.ppermute(x, "dp", [(r, (r + s) % data_ranks) for r in range(data_ranks)])
     near = [(z, z ^ 1) for z in range(CHIPS_DENSE)]
     cross = [(z, z ^ 3) for z in range(CHIPS_DENSE)]
     two = [(z, z ^ 2) for z in range(CHIPS_DENSE)]
 
     names = routes.T
     first = move(tokens, near)
-    named = [names]
-    for pairs in [near, cross, two]:
-        named.append(move(names, pairs))
-    own_names = jnp.concatenate(named, axis=0)
-    other_names = swap(own_names)
     second = move(tokens, cross)
     far = move(tokens, [(0, 2), (3, 1)])
     onward = move(second, [(1, 0), (2, 3)])
-    third = far + onward
-
-    me = me.astype(jnp.int32).reshape(1)
-    gram = None
-    for slot, own in enumerate([tokens, first, second, third]):
+    moved = []
+    for pairs in [near, cross, two]:
+        moved.append(move(names, pairs))
+    moved = jnp.concatenate(moved, axis=0)
+    other_names = swap(names)
+    other_moved = swap(moved)
+
+    hiddens = []
+    for slot, own in enumerate([tokens, first, second, far + onward]):
         other = swap(own)
-        gram = hidden_gram(me, own, other, own_names, other_names, slot, gate_w, up_w, gram)
-    return gram
+        if slot == 0:
+            hidden = hidden_of(me, own, other, names, other_names, 0, top, gate_w, up_w)
+        else:
+            hidden = hidden_of(me, own, other, moved, other_moved, slot - 1, top, gate_w, up_w)
+        hiddens.append([hidden] + [turn(hidden, s) for s in range(1, data_ranks)])
+    early = partial_gram(sum(hiddens[:-1], []))
+    return early, hiddens[-1]
 
 
 def packed_grams(tokens, routes, gate_w, up_w, capacity):
@@ -124,16 +148,18 @@
     owners = lax.axis_size("expert")
     data_ranks = lax.axis_size("dp")
     experts = w_gate.shape[0] * owners
-    factor_width = w_gate.shape[2]
     tok_rows, top_count = routes.shape
     capacity = min(tok_rows, 2 * tok_rows * top_count // experts)
     gate_w, up_w = w_gate[0], w_up[0]
     if tok_rows * owners <= experts * capacity and owners == CHIPS_DENSE * CORES:
-        gram_local = gather_grams(tokens, routes, gate_w, up_w)
+        early, late = gathered(tokens, routes, gate_w, up_w)
     else:
-        gram_local = packed_grams(tokens, routes, gate_w, up_w, capacity)
+        gram = packed_grams(tokens, routes, gate_w, up_w, capacity)
+        early, late = gram, []
+        for s in range(1, data_ranks):
+            early = early + lax.ppermute(gram, "dp", [(r, (r + s) % data_ranks) for r in range(data_ranks)])
     rows_mean = data_ranks * tok_rows * top_count
-    return finish(gram_local, rows_mean, data_ranks, factor_width)
+    return factor_rows(early, late, rows_mean, data_ranks)[None]
 
 
 def over_lanes(column, width):
@@ -161,12 +187,16 @@
     )
 
 
-def factor_kernel(mine_ref, theirs_ref, out_ref, rest_ref, *, rows_mean):
-    size = mine_ref.shape[0]
+def factor_kernel(rank_ref, early_ref, *refs, rows_mean):
+    late_refs, (my_rows_ref, out_ref, rest_ref) = refs[:-3], refs[-3:]
+    size = early_ref.shape[0]
     block, panel = 128, 8
     row = lax.broadcasted_iota(jnp.int32, (size, size), 0)
     col = lax.broadcasted_iota(jnp.int32, (size, size), 1)
-    rest_ref[...] = (mine_ref[...] + theirs_ref[...]) / rows_mean + jnp.where(row == col, RIDGE, 0.0)
+    gram = early_ref[...]
+    if late_refs:
+        gram = gram + gram_of(late_refs)
+    rest_ref[...] = gram / rows_mean + jnp.where(row == col, RIDGE, 0.0)
     for base in range(0, size, block):
         width = size - base
         end = base + block
@@ -196,30 +226,22 @@
         if end < size:
             done = out_ref[base:end, end:]
             rest_ref[end:, end:] -= outer_sum(done, done)
-
-
-def factor_of(mine, theirs, rows_mean):
-    size = mine.shape[0]
+    count = my_rows_ref.shape[0]
+    my_rows_ref[...] = out_ref[pl.ds(pl.multiple_of(rank_ref[0] * count, count), count), :]
+
+
+def factor_rows(early, late, rows_mean, data_ranks):
+    size = early.shape[0]
+    rank = lax.axis_index("dp").astype(jnp.int32).reshape(1)
     return pl.pallas_call(
         functools.partial(factor_kernel, rows_mean=rows_mean),
-        in_specs=[pl.BlockSpec(memory_space=pltpu.VMEM)] * 2,
+        in_specs=[pl.BlockSpec(memory_space=pltpu.SMEM)] + [pl.BlockSpec(memory_space=pltpu.VMEM)] * (1 + len(late)),
         out_specs=pl.BlockSpec(memory_space=pltpu.VMEM),
-        out_shape=jax.ShapeDtypeStruct((size, size), jnp.float32),
-        scratch_shapes=[pltpu.VMEM((size, size), jnp.float32)],
+        out_shape=jax.ShapeDtypeStruct((size // data_ranks, size), jnp.float32),
+        scratch_shapes=[pltpu.VMEM((size, size), jnp.float32)] * 2,
+        compiler_params=pltpu.CompilerParams(vmem_limit_bytes=24 << 20),
         name="factor",
-    )(mine, theirs)
-
-
-def finish(gram_local, rows_mean, data_ranks, factor_width):
-    block_rows = factor_width // data_ranks
-    my_rank = lax.axis_index("dp")
-    theirs = jnp.zeros_like(gram_local)
-    for s in range(1, data_ranks):
-        moved = lax.ppermute(gram_local, "dp", [(r, (r + s) % data_ranks) for r in range(data_ranks)])
-        theirs = moved if s == 1 else theirs + moved
-    factor = factor_of(gram_local, theirs, rows_mean)
-    my_rows = lax.dynamic_slice_in_dim(factor, my_rank * block_rows, block_rows, 0)
-    return my_rows.reshape(1, block_rows, factor_width)
+    )(rank, early, *late)
 
 
 def solution(mesh):

time: 137 us -> 123 us (0.90)
  waiting for transfers between devices: 67.9 us -> 55.6 us
  starting transfers between devices: 13.4 us -> 18 us
  Pallas kernels: 46.7 us -> 44.1 us
  local copies, waits for them, and re-layouts: 7.23 us -> 4.91 us
    ppermute x13 -> x17, waiting for transfers between devices: 67.9 us -> 55.6 us  [the longest x7 41.3 us: gathered(): move = lambda x, pairs: lax.ppermute(x, 'expert', between_chips(pairs))]
    ppermute x13 -> x17, starting transfers between devices: 13.4 us -> 18 us  [the longest x7 12.9 us: gathered(): move = lambda x, pairs: lax.ppermute(x, 'expert', between_chips(pairs))]
    pallas_call x5 -> x6, Pallas kernels: 46.7 us -> 44.1 us  [the longest x1 34.2 us: factor_rows(): pl.pallas_call(functools.partial(factor_kernel, rows_mean=rows_mean), in_...]
    reshape x1 -> x0, local copies, waits for them, and re-layouts: 1.87 us -> none  [finish(): return my_rows.reshape(1, block_rows, factor_width)]
    unnamed x14 -> x12, local copies, waits for them, and re-layouts: 5.37 us -> 4.91 us
  transfers between devices with their start and end apart: 13 -> 17, of which waited for: 9 -> 11; matrix products, arithmetic and copies ran while one was open for 1% -> 0% of each run, Pallas kernels for 6% -> 8%
where the time goes in v4:
time: 123 us
  waiting for transfers between devices  55.6 us (45%)
  Pallas kernels  44.1 us (36%)
  starting transfers between devices  18 us (15%)
  local copies, waits for them, and re-layouts  4.91 us (4%)
    ppermute x7, waiting for transfers between devices, gathered(): move = lambda x, pairs: lax.ppermute(x, 'expert', between_chips(pairs))  41.3 us
    pallas_call x1, Pallas kernels, factor_rows(): pl.pallas_call(functools.partial(factor_kernel, rows_mean=rows_mean), in_...  34.2 us
    ppermute x4, waiting for transfers between devices, gathered(): lax.ppermute(x, 'dp', [(r, (r + s) % data_ranks) for r in range(data_rank...  12.9 us
    ppermute x7, starting transfers between devices, gathered(): move = lambda x, pairs: lax.ppermute(x, 'expert', between_chips(pairs))  12.9 us
    pallas_call x4, Pallas kernels, hidden_of(): pl.pallas_call(functools.partial(hidden_kernel, at=at, top=top), in_specs...  7.98 us
    unnamed x12, local copies, waits for them, and re-layouts  4.91 us
    ppermute x4, starting transfers between devices, gathered(): lax.ppermute(x, 'dp', [(r, (r + s) % data_ranks) for r in range(data_rank...  4.31 us
  transfers between devices with their start and end apart: 17, of which 11 were waited for; matrix products, arithmetic and copies ran while one was open for 0% of the time, Pallas kernels for 8%

profile of v4, /device:TPU:0, one launch (start us, length us, event | category | flops | bytes accessed | tf_op | source)
XLA Modules:
  0.0 122.9 jit_solution(9192948512919320907)
XLA Ops:
  0.0 5.1 %collective-permute-start.10 = (bf16[128,2048]{1,0:T(8,128)(2,1)}, bf16[128,2048]{1,0:T(8,128)(2,1)S(1)}, u32[]{:S(2)}, u32[]{:S(2)}) collective-permute-start(bf16[128,2048]{1,0:T(8,128)(2,1)} %own_ref.1), channel_id=1, source_target_pairs={{0,6},{1,7},{2,4},{3,5},{4,2},{5,3},{6,0},{7,1},{8,14},{9,15},{10,... | collective-permute-start | bytes 1572872 | tf_op jit(solution)/shard_map/ppermute | solution.py:94
  5.1 2.5 %collective-permute-start.13 = (bf16[128,2048]{1,0:T(8,128)(2,1)}, bf16[128,2048]{1,0:T(8,128)(2,1)S(1)}, u32[]{:S(2)}, u32[]{:S(2)}) collective-permute-start(bf16[128,2048]{1,0:T(8,128)(2,1)} %own_ref.1), channel_id=1, source_target_pairs={{0,4},{1,5},{6,2},{7,3},{8,12},{9,13},{14,10},{15,11},{16,20},{17,... | collective-permute-start | bytes 1572872 | tf_op jit(solution)/shard_map/ppermute | solution.py:94
  7.6 10.6 %collective-permute-done.10.own_ref = bf16[128,2048]{1,0:T(8,128)(2,1)S(1)} collective-permute-done((bf16[128,2048]{1,0:T(8,128)(2,1)}, bf16[128,2048]{1,0:T(8,128)(2,1)S(1)}, u32[]{:S(2)}, u32[]{:S(2)}) %collective-permute-start.10) | collective-permute-done | bytes 524320 | tf_op jit(solution)/shard_map/ppermute | solution.py:94
  19.5 9.4 %collective-permute-done.3.own_ref = bf16[128,2048]{1,0:T(8,128)(2,1)S(1)} collective-permute-done((bf16[128,2048]{1,0:T(8,128)(2,1)}, bf16[128,2048]{1,0:T(8,128)(2,1)S(1)}, u32[]{:S(2)}, u32[]{:S(2)}) %collective-permute-start.3) | collective-permute-done | bytes 524320 | tf_op jit(solution)/shard_map/ppermute | solution.py:94
  29.5 9.6 %collective-permute-done.13 = bf16[128,2048]{1,0:T(8,128)(2,1)S(1)} collective-permute-done((bf16[128,2048]{1,0:T(8,128)(2,1)}, bf16[128,2048]{1,0:T(8,128)(2,1)S(1)}, u32[]{:S(2)}, u32[]{:S(2)}) %collective-permute-start.13) | collective-permute-done | bytes 524320 | tf_op jit(solution)/shard_map/ppermute | solution.py:94
  39.1 1.6 %collective-permute-done.14 = bf16[128,2048]{1,0:T(8,128)(2,1)S(1)} collective-permute-done((bf16[128,2048]{1,0:T(8,128)(2,1)S(1)}, bf16[128,2048]{1,0:T(8,128)(2,1)S(1)}, u32[]{:S(2)}, u32[]{:S(2)}) %collective-permute-start.14) | collective-permute-done | bytes 524320 | tf_op jit(solution)/shard_map/ppermute | solution.py:94
  40.9 1.8 %collective-permute-start.7 = (s32[4,128]{1,0:T(4,128)}, s32[4,128]{1,0:T(4,128)S(1)}, u32[]{:S(2)}, u32[]{:S(2)}) collective-permute-start(s32[4,128]{1,0:T(4,128)} %bitcast.14), channel_id=1, source_target_pairs={{0,4},{1,5},{2,6},{3,7},{4,0},{5,1},{6,2},{7,3},{8,12},{9,13},{10,... | collective-permute-start | bytes 6152 | tf_op jit(solution)/shard_map/ppermute | solution.py:94
  42.6 3.0 %collective-permute-done.7 = s32[4,128]{1,0:T(4,128)S(1)} collective-permute-done((s32[4,128]{1,0:T(4,128)}, s32[4,128]{1,0:T(4,128)S(1)}, u32[]{:S(2)}, u32[]{:S(2)}) %collective-permute-start.7) | collective-permute-done | bytes 2080 | tf_op jit(solution)/shard_map/ppermute | solution.py:94
  45.7 2.3 %collective-permute-start.6 = (s32[4,128]{1,0:T(4,128)}, s32[4,128]{1,0:T(4,128)S(1)}, u32[]{:S(2)}, u32[]{:S(2)}) collective-permute-start(s32[4,128]{1,0:T(4,128)} %bitcast.15), channel_id=1, source_target_pairs={{0,6},{1,7},{2,4},{3,5},{4,2},{5,3},{6,0},{7,1},{8,14},{9,15},{10,... | collective-permute-start | bytes 6152 | tf_op jit(solution)/shard_map/ppermute | solution.py:94
  47.9 3.3 %collective-permute-done.6 = s32[4,128]{1,0:T(4,128)S(1)} collective-permute-done((s32[4,128]{1,0:T(4,128)}, s32[4,128]{1,0:T(4,128)S(1)}, u32[]{:S(2)}, u32[]{:S(2)}) %collective-permute-start.6) | collective-permute-done | bytes 2080 | tf_op jit(solution)/shard_map/ppermute | solution.py:94
  51.2 3.8 %collective-permute-done.5 = s32[4,128]{1,0:T(4,128)S(1)} collective-permute-done((s32[4,128]{1,0:T(4,128)}, s32[4,128]{1,0:T(4,128)S(1)}, u32[]{:S(2)}, u32[]{:S(2)}) %collective-permute-start.5) | collective-permute-done | bytes 2080 | tf_op jit(solution)/shard_map/ppermute | solution.py:94
  56.6 1.6 %copy-done = bf16[1,2048,512]{2,1,0:T(8,128)(2,1)S(1)} copy-done((bf16[1,2048,512]{2,1,0:T(8,128)(2,1)S(1)}, bf16[1,2048,512]{2,1,0:T(8,128)(2,1)}, u32[]{:S(2)}) %copy-start) | copy-done | bytes 2097176
  58.2 1.6 %copy-done.2 = bf16[1,2048,512]{2,1,0:T(8,128)(2,1)S(1)} copy-done((bf16[1,2048,512]{2,1,0:T(8,128)(2,1)S(1)}, bf16[1,2048,512]{2,1,0:T(8,128)(2,1)}, u32[]{:S(2)}) %copy-start.2) | copy-done | bytes 2097176
  61.5 1.7 %hidden.4.refs_0_ = bf16[256,512]{1,0:T(8,128)(2,1)S(1)} custom-call(s32[1]{0:T(128)} %bitcast.1.me_ref, bf16[128,2048]{1,0:T(8,128)(2,1)S(1)} %copy-done.4, bf16[128,2048]{1,0:T(8,128)(2,1)S(1)} %collective-permute-done.other_ref, s32[4,128]{1,0:T(4,128)S(1)} %bitcast.18, s32[4,128]{1,0:T(4,128)S(1)} %collective-permute-done.1.other_names_ref, ...), custom_call_target="tpu_custom_call" | custom-call | flops 1073741824 | bytes 5505024 | tf_op jit(solution)/shard_map/hidden/pallas_call | solution.py:41
  63.2 1.6 %collective-permute-start.2 = (bf16[256,512]{1,0:T(8,128)(2,1)S(1)}, bf16[256,512]{1,0:T(8,128)(2,1)}, u32[]{:S(2)}, u32[]{:S(2)}) collective-permute-start(bf16[256,512]{1,0:T(8,128)(2,1)S(1)} %hidden.4.refs_0_), channel_id=1, source_target_pairs={{0,8},{8,0},{1,9},{9,1},{2,10},{10,2},{3,11},{11,3},{4,12},{12,4},... | collective-permute-start | bytes 786440 | tf_op jit(solution)/shard_map/ppermute | solution.py:96
  64.8 2.8 %hidden.5.refs_2_ = bf16[256,512]{1,0:T(8,128)(2,1)S(1)} custom-call(s32[1]{0:T(128)} %bitcast.1.me_ref, bf16[128,2048]{1,0:T(8,128)(2,1)S(1)} %collective-permute-done.3.own_ref, bf16[128,2048]{1,0:T(8,128)(2,1)} %collective-permute-done.4.other_ref, s32[12,128]{1,0:T(8,128)S(1)} %pad_add_fusion.own_names_ref, ...), custom_call_target="tpu_custom_call" | custom-call | flops 1073741824 | bytes 5505024 | tf_op jit(solution)/shard_map/hidden/pallas_call | solution.py:41
  68.2 1.7 %hidden.6.refs_4_ = bf16[256,512]{1,0:T(8,128)(2,1)S(1)} custom-call(s32[1]{0:T(128)} %bitcast.1.me_ref, bf16[128,2048]{1,0:T(8,128)(2,1)S(1)} %collective-permute-done.10.own_ref, bf16[128,2048]{1,0:T(8,128)(2,1)S(1)} %collective-permute-done.11.other_ref, s32[12,128]{1,0:T(8,128)S(1)} %pad_add_fusion.own_names_ref, ...), custom_call_target="tpu_custom_call" | custom-call | flops 1073741824 | bytes 5505024 | tf_op jit(solution)/shard_map/hidden/pallas_call | solution.py:41
  70.0 1.6 %collective-permute-start.12 = (bf16[256,512]{1,0:T(8,128)(2,1)S(1)}, bf16[256,512]{1,0:T(8,128)(2,1)S(1)}, u32[]{:S(2)}, u32[]{:S(2)}) collective-permute-start(bf16[256,512]{1,0:T(8,128)(2,1)S(1)} %hidden.6.refs_4_), channel_id=1, source_target_pairs={{0,8},{8,0},{1,9},{9,1},{2,10},{10,2},{3,11},{11,3},{4,12},{12,4},... | collective-permute-start | bytes 786440 | tf_op jit(solution)/shard_map/ppermute | solution.py:96
  71.5 1.7 %hidden.7.refs_0_ = bf16[256,512]{1,0:T(8,128)(2,1)S(1)} custom-call(s32[1]{0:T(128)} %bitcast.1.me_ref, bf16[128,2048]{1,0:T(8,128)(2,1)S(1)} %add.3.own_ref, bf16[128,2048]{1,0:T(8,128)(2,1)S(1)} %collective-permute-done.15.other_ref, s32[12,128]{1,0:T(8,128)S(1)} %pad_add_fusion.own_names_ref, s32[12,128]{1,0:T(8,128)S(1)} %collective-permute-done.8.other_names_ref, ...), custom_call_target="tpu_custom_call" | custom-call | flops 1073741824 | bytes 5505024 | tf_op jit(solution)/shard_map/hidden/pallas_call | solution.py:41
  73.9 4.2 %collective-permute-done.9.refs_3_ = bf16[256,512]{1,0:T(8,128)(2,1)S(1)} collective-permute-done((bf16[256,512]{1,0:T(8,128)(2,1)S(1)}, bf16[256,512]{1,0:T(8,128)(2,1)S(1)}, u32[]{:S(2)}, u32[]{:S(2)}) %collective-permute-start.9) | collective-permute-done | bytes 262176 | tf_op jit(solution)/shard_map/ppermute | solution.py:96
  78.1 5.6 %collective-permute-done.12.refs_5_ = bf16[256,512]{1,0:T(8,128)(2,1)S(1)} collective-permute-done((bf16[256,512]{1,0:T(8,128)(2,1)S(1)}, bf16[256,512]{1,0:T(8,128)(2,1)S(1)}, u32[]{:S(2)}, u32[]{:S(2)}) %collective-permute-start.12) | collective-permute-done | bytes 262176 | tf_op jit(solution)/shard_map/ppermute | solution.py:96
  83.7 1.9 %partial_gram.1.early_ref = f32[512,512]{1,0:T(8,128)S(1)} custom-call(bf16[256,512]{1,0:T(8,128)(2,1)S(1)} %hidden.4.refs_0_, bf16[256,512]{1,0:T(8,128)(2,1)} %collective-permute-done.2.refs_1_, bf16[256,512]{1,0:T(8,128)(2,1)S(1)} %hidden.5.refs_2_, bf16[256,512]{1,0:T(8,128)(2,1)S(1)} %collective-permute-done.9.refs_3_, ...), custom_call_target="tpu_custom_call" | custom-call | flops 805306368 | bytes 2621440 | tf_op jit(solution)/shard_map/partial_gram/pallas_call | solution.py:71
  85.7 3.0 %collective-permute-done.16.refs_1_ = bf16[256,512]{1,0:T(8,128)(2,1)S(1)} collective-permute-done((bf16[256,512]{1,0:T(8,128)(2,1)S(1)}, bf16[256,512]{1,0:T(8,128)(2,1)S(1)}, u32[]{:S(2)}, u32[]{:S(2)}) %collective-permute-start.16) | collective-permute-done | bytes 262176 | tf_op jit(solution)/shard_map/ppermute | solution.py:96
  88.7 34.2 %factor.1 = f32[256,512]{1,0:T(8,128)} custom-call(s32[1]{0:T(128)} %bitcast.rank_ref, f32[512,512]{1,0:T(8,128)S(1)} %partial_gram.1.early_ref, bf16[256,512]{1,0:T(8,128)(2,1)S(1)} %hidden.7.refs_0_, bf16[256,512]{1,0:T(8,128)(2,1)S(1)} %collective-permute-done.16.refs_1_), custom_call_target="tpu_custom_call" | custom-call | tf_op jit(solution)/shard_map/factor/pallas_call | solution.py:236
  (30 shorter events, 6.6 us)
Async XLA Ops:
  0.0 18.2 %collective-permute-start.10 = (bf16[128,2048]{1,0:T(8,128)(2,1)}, bf16[128,2048]{1,0:T(8,128)(2,1)S(1)}, u32[]{:S(2)}, u32[]{:S(2)}) collective-permute-start(bf16[128,2048]{1,0:T(8,128)(2,1)} %own_ref.1), channel_id=1, source_target_pairs={{0,6},{1,7},{2,4},{3,5},{4,2},{5,3},{6,0},{7,1},{8,14},{9,15},{10,... | collective-permute-start | bytes 1572872 | tf_op jit(solution)/shard_map/ppermute | solution.py:94
  5.1 23.9 %collective-permute-start.3 = (bf16[128,2048]{1,0:T(8,128)(2,1)}, bf16[128,2048]{1,0:T(8,128)(2,1)S(1)}, u32[]{:S(2)}, u32[]{:S(2)}) collective-permute-start(bf16[128,2048]{1,0:T(8,128)(2,1)} %own_ref.1), channel_id=1, source_target_pairs={{0,2},{1,3},{2,0},{3,1},{4,6},{5,7},{6,4},{7,5},{8,10},{9,11},{10,... | collective-permute-start | bytes 1572872 | tf_op jit(solution)/shard_map/ppermute | solution.py:94
  5.1 34.0 %collective-permute-start.13 = (bf16[128,2048]{1,0:T(8,128)(2,1)}, bf16[128,2048]{1,0:T(8,128)(2,1)S(1)}, u32[]{:S(2)}, u32[]{:S(2)}) collective-permute-start(bf16[128,2048]{1,0:T(8,128)(2,1)} %own_ref.1), channel_id=1, source_target_pairs={{0,4},{1,5},{6,2},{7,3},{8,12},{9,13},{14,10},{15,11},{16,20},{17,... | collective-permute-start | bytes 1572872 | tf_op jit(solution)/shard_map/ppermute | solution.py:94
  18.2 22.5 %collective-permute-start.14 = (bf16[128,2048]{1,0:T(8,128)(2,1)S(1)}, bf16[128,2048]{1,0:T(8,128)(2,1)S(1)}, u32[]{:S(2)}, u32[]{:S(2)}) collective-permute-start(bf16[128,2048]{1,0:T(8,128)(2,1)S(1)} %collective-permute-done.10.own_ref), channel_id=1, source_target_pairs={{2,0},{3,1},{4,6},{5,7},{10,8},{11,9},{12,14},{13,15},{18,16},{19,... | collective-permute-start | bytes 1572872 | tf_op jit(solution)/shard_map/ppermute | solution.py:94
  19.4 37.1 %collective-permute-start = (bf16[128,2048]{1,0:T(8,128)(2,1)}, bf16[128,2048]{1,0:T(8,128)(2,1)S(1)}, u32[]{:S(2)}, u32[]{:S(2)}) collective-permute-start(bf16[128,2048]{1,0:T(8,128)(2,1)} %own_ref.1), channel_id=1, source_target_pairs={{0,1},{1,0},{2,3},{3,2},{4,5},{5,4},{6,7},{7,6},{8,9},{9,8},{10,11... | collective-permute-start | bytes 1572872 | tf_op jit(solution)/shard_map/ppermute | solution.py:95
  28.9 35.8 %collective-permute-start.4 = (bf16[128,2048]{1,0:T(8,128)(2,1)S(1)}, bf16[128,2048]{1,0:T(8,128)(2,1)}, u32[]{:S(2)}, u32[]{:S(2)}) collective-permute-start(bf16[128,2048]{1,0:T(8,128)(2,1)S(1)} %collective-permute-done.3.own_ref), channel_id=1, source_target_pairs={{0,1},{1,0},{2,3},{3,2},{4,5},{5,4},{6,7},{7,6},{8,9},{9,8},{10,11... | collective-permute-start | bytes 1572872 | tf_op jit(solution)/shard_map/ppermute | solution.py:95
  28.9 39.3 %collective-permute-start.11 = (bf16[128,2048]{1,0:T(8,128)(2,1)S(1)}, bf16[128,2048]{1,0:T(8,128)(2,1)S(1)}, u32[]{:S(2)}, u32[]{:S(2)}) collective-permute-start(bf16[128,2048]{1,0:T(8,128)(2,1)S(1)} %collective-permute-done.10.own_ref), channel_id=1, source_target_pairs={{0,1},{1,0},{2,3},{3,2},{4,5},{5,4},{6,7},{7,6},{8,9},{9,8},{10,11... | collective-permute-start | bytes 1572872 | tf_op jit(solution)/shard_map/ppermute | solution.py:95
  40.8 30.7 %collective-permute-start.15 = (bf16[128,2048]{1,0:T(8,128)(2,1)S(1)}, bf16[128,2048]{1,0:T(8,128)(2,1)S(1)}, u32[]{:S(2)}, u32[]{:S(2)}) collective-permute-start(bf16[128,2048]{1,0:T(8,128)(2,1)S(1)} %add.3.own_ref), channel_id=1, source_target_pairs={{0,1},{1,0},{2,3},{3,2},{4,5},{5,4},{6,7},{7,6},{8,9},{9,8},{10,11... | collective-permute-start | bytes 1572872 | tf_op jit(solution)/shard_map/ppermute | solution.py:95
  40.9 4.8 %collective-permute-start.7 = (s32[4,128]{1,0:T(4,128)}, s32[4,128]{1,0:T(4,128)S(1)}, u32[]{:S(2)}, u32[]{:S(2)}) collective-permute-start(s32[4,128]{1,0:T(4,128)} %bitcast.14), channel_id=1, source_target_pairs={{0,4},{1,5},{2,6},{3,7},{4,0},{5,1},{6,2},{7,3},{8,12},{9,13},{10,... | collective-permute-start | bytes 6152 | tf_op jit(solution)/shard_map/ppermute | solution.py:94
  45.7 5.6 %collective-permute-start.6 = (s32[4,128]{1,0:T(4,128)}, s32[4,128]{1,0:T(4,128)S(1)}, u32[]{:S(2)}, u32[]{:S(2)}) collective-permute-start(s32[4,128]{1,0:T(4,128)} %bitcast.15), channel_id=1, source_target_pairs={{0,6},{1,7},{2,4},{3,5},{4,2},{5,3},{6,0},{7,1},{8,14},{9,15},{10,... | collective-permute-start | bytes 6152 | tf_op jit(solution)/shard_map/ppermute | solution.py:94
  51.2 3.8 %collective-permute-start.5 = (s32[4,128]{1,0:T(4,128)}, s32[4,128]{1,0:T(4,128)S(1)}, u32[]{:S(2)}, u32[]{:S(2)}) collective-permute-start(s32[4,128]{1,0:T(4,128)} %bitcast.16), channel_id=1, source_target_pairs={{0,2},{1,3},{2,0},{3,1},{4,6},{5,7},{6,4},{7,5},{8,10},{9,11},{10,... | collective-permute-start | bytes 6152 | tf_op jit(solution)/shard_map/ppermute | solution.py:94
  55.0 1.4 %collective-permute-start.1 = (s32[4,128]{1,0:T(4,128)}, s32[4,128]{1,0:T(4,128)S(1)}, u32[]{:S(2)}, u32[]{:S(2)}) collective-permute-start(s32[4,128]{1,0:T(4,128)} %bitcast.17), channel_id=1, source_target_pairs={{0,1},{1,0},{2,3},{3,2},{4,5},{5,4},{6,7},{7,6},{8,9},{9,8},{10,11... | collective-permute-start | bytes 6152 | tf_op jit(solution)/shard_map/ppermute | solution.py:95
  56.4 8.4 %collective-permute-start.8 = (s32[12,128]{1,0:T(8,128)S(1)}, s32[12,128]{1,0:T(8,128)S(1)}, u32[]{:S(2)}, u32[]{:S(2)}) collective-permute-start(s32[12,128]{1,0:T(8,128)S(1)} %pad_add_fusion.own_names_ref), channel_id=1, source_target_pairs={{0,1},{1,0},{2,3},{3,2},{4,5},{5,4},{6,7},{7,6},{8,9},{9,8},{10,11... | collective-permute-start | bytes 18440 | tf_op jit(solution)/shard_map/ppermute | solution.py:95
  56.6 1.6 %copy-start = (bf16[1,2048,512]{2,1,0:T(8,128)(2,1)S(1)}, bf16[1,2048,512]{2,1,0:T(8,128)(2,1)}, u32[]{:S(2)}) copy-start(bf16[1,2048,512]{2,1,0:T(8,128)(2,1)} %param.6) | copy-start | bytes 6291460
  58.2 1.6 %copy-start.2 = (bf16[1,2048,512]{2,1,0:T(8,128)(2,1)S(1)}, bf16[1,2048,512]{2,1,0:T(8,128)(2,1)}, u32[]{:S(2)}) copy-start(bf16[1,2048,512]{2,1,0:T(8,128)(2,1)} %param.7) | copy-start | bytes 6291460
  59.8 1.0 copy-start.4
  60.8 0.7 copy-start.5
  61.5 3.3 %copy-start.1 = (bf16[1,2048,512]{2,1,0:T(8,128)(2,1)S(1)}, bf16[1,2048,512]{2,1,0:T(8,128)(2,1)}, u32[]{:S(2)}) copy-start(bf16[1,2048,512]{2,1,0:T(8,128)(2,1)} %param.6) | copy-start | bytes 6291460
  61.5 3.3 %copy-start.3 = (bf16[1,2048,512]{2,1,0:T(8,128)(2,1)S(1)}, bf16[1,2048,512]{2,1,0:T(8,128)(2,1)}, u32[]{:S(2)}) copy-start(bf16[1,2048,512]{2,1,0:T(8,128)(2,1)} %param.7) | copy-start | bytes 6291460
  63.2 10.6 %collective-permute-start.2 = (bf16[256,512]{1,0:T(8,128)(2,1)S(1)}, bf16[256,512]{1,0:T(8,128)(2,1)}, u32[]{:S(2)}, u32[]{:S(2)}) collective-permute-start(bf16[256,512]{1,0:T(8,128)(2,1)S(1)} %hidden.4.refs_0_), channel_id=1, source_target_pairs={{0,8},{8,0},{1,9},{9,1},{2,10},{10,2},{3,11},{11,3},{4,12},{12,4},... | collective-permute-start | bytes 786440 | tf_op jit(solution)/shard_map/ppermute | solution.py:96
  67.6 10.5 %collective-permute-start.9 = (bf16[256,512]{1,0:T(8,128)(2,1)S(1)}, bf16[256,512]{1,0:T(8,128)(2,1)S(1)}, u32[]{:S(2)}, u32[]{:S(2)}) collective-permute-start(bf16[256,512]{1,0:T(8,128)(2,1)S(1)} %hidden.5.refs_2_), channel_id=1, source_target_pairs={{0,8},{8,0},{1,9},{9,1},{2,10},{10,2},{3,11},{11,3},{4,12},{12,4},... | collective-permute-start | bytes 786440 | tf_op jit(solution)/shard_map/ppermute | solution.py:96
  70.0 13.8 %collective-permute-start.12 = (bf16[256,512]{1,0:T(8,128)(2,1)S(1)}, bf16[256,512]{1,0:T(8,128)(2,1)S(1)}, u32[]{:S(2)}, u32[]{:S(2)}) collective-permute-start(bf16[256,512]{1,0:T(8,128)(2,1)S(1)} %hidden.6.refs_4_), channel_id=1, source_target_pairs={{0,8},{8,0},{1,9},{9,1},{2,10},{10,2},{3,11},{11,3},{4,12},{12,4},... | collective-permute-start | bytes 786440 | tf_op jit(solution)/shard_map/ppermute | solution.py:96
  73.2 15.5 %collective-permute-start.16 = (bf16[256,512]{1,0:T(8,128)(2,1)S(1)}, bf16[256,512]{1,0:T(8,128)(2,1)S(1)}, u32[]{:S(2)}, u32[]{:S(2)}) collective-permute-start(bf16[256,512]{1,0:T(8,128)(2,1)S(1)} %hidden.7.refs_0_), channel_id=1, source_target_pairs={{0,8},{8,0},{1,9},{9,1},{2,10},{10,2},{3,11},{11,3},{4,12},{12,4},... | collective-permute-start | bytes 786440 | tf_op jit(solution)/shard_map/ppermute | solution.py:96

commit v5 on v4

--- a/solution.py
+++ b/solution.py
@@ -94,24 +94,23 @@
     move = lambda x, pairs: lax.ppermute(x, "expert", between_chips(pairs))
     swap = lambda x: lax.ppermute(x, "expert", [(e, e ^ 1) for e in range(CHIPS_DENSE * CORES)])
     turn = lambda x, s: lax.ppermute(x, "dp", [(r, (r + s) % data_ranks) for r in range(data_ranks)])
-    near = [(z, z ^ 1) for z in range(CHIPS_DENSE)]
-    cross = [(z, z ^ 3) for z in range(CHIPS_DENSE)]
-    two = [(z, z ^ 2) for z in range(CHIPS_DENSE)]
+    ring = lambda s: [(z, (z + s) % CHIPS_DENSE) for z in range(CHIPS_DENSE)]
 
     names = routes.T
-    first = move(tokens, near)
-    second = move(tokens, cross)
+    below = move(tokens, ring(1))
+    above = move(tokens, ring(-1))
     far = move(tokens, [(0, 2), (3, 1)])
-    onward = move(second, [(1, 0), (2, 3)])
+    on_up = move(below, [(2, 3)])
+    on_down = move(above, [(1, 0)])
     moved = []
-    for pairs in [near, cross, two]:
+    for pairs in [ring(1), ring(-1), ring(2)]:
         moved.append(move(names, pairs))
     moved = jnp.concatenate(moved, axis=0)
     other_names = swap(names)
     other_moved = swap(moved)
 
     hiddens = []
-    for slot, own in enumerate([tokens, first, second, far + onward]):
+    for slot, own in enumerate([tokens, below, above, far + on_up + on_down]):
         other = swap(own)
         if slot == 0:
             hidden = hidden_of(me, own, other, names, other_names, 0, top, gate_w, up_w)

time: 123 us -> 128 us (1.041)
  starting transfers between devices: 18 us -> 25.2 us
  waiting for transfers between devices: 55.6 us -> 52 us
  Pallas kernels: 44.1 us -> 47.5 us
  local copies, waits for them, and re-layouts: 4.91 us -> 2.64 us
    ppermute x7 -> x8, starting transfers between devices: 12.9 us -> 20.2 us  [gathered(): move = lambda x, pairs: lax.ppermute(x, 'expert', between_chips(pairs))]
    ppermute x4, waiting for transfers between devices: 12.9 us -> 9.56 us  [gathered(): lax.ppermute(x, 'dp', [(r, (r + s) % data_ranks) for r in range(data_rank...]
    pallas_call x4, Pallas kernels: 7.98 us -> 11.2 us  [hidden_of(): pl.pallas_call(functools.partial(hidden_kernel, at=at, top=top), in_specs...]
    unnamed x12 -> x8, local copies, waits for them, and re-layouts: 4.91 us -> 2.64 us
    ppermute x7 -> x8, waiting for transfers between devices: 41.3 us -> 41.3 us  [gathered(): move = lambda x, pairs: lax.ppermute(x, 'expert', between_chips(pairs))]
  transfers between devices with their start and end apart: 17 -> 18, of which waited for: 11 -> 11; matrix products, arithmetic and copies ran while one was open for 0% -> 0% of each run, Pallas kernels for 8% -> 10%
where the time goes in v5:
time: 128 us
  waiting for transfers between devices  52 us (41%)
  Pallas kernels  47.5 us (37%)
  starting transfers between devices  25.2 us (20%)
  local copies, waits for them, and re-layouts  2.64 us (2%)
    ppermute x8, waiting for transfers between devices, gathered(): move = lambda x, pairs: lax.ppermute(x, 'expert', between_chips(pairs))  41.3 us
    pallas_call x1, Pallas kernels, factor_rows(): pl.pallas_call(functools.partial(factor_kernel, rows_mean=rows_mean), in_...  34.2 us
    ppermute x8, starting transfers between devices, gathered(): move = lambda x, pairs: lax.ppermute(x, 'expert', between_chips(pairs))  20.2 us
    pallas_call x4, Pallas kernels, hidden_of(): pl.pallas_call(functools.partial(hidden_kernel, at=at, top=top), in_specs...  11.2 us
    ppermute x4, waiting for transfers between devices, gathered(): lax.ppermute(x, 'dp', [(r, (r + s) % data_ranks) for r in range(data_rank...  9.56 us
    ppermute x4, starting transfers between devices, gathered(): lax.ppermute(x, 'dp', [(r, (r + s) % data_ranks) for r in range(data_rank...  4.25 us
    unnamed x8, local copies, waits for them, and re-layouts  2.64 us
  transfers between devices with their start and end apart: 18, of which 11 were waited for; matrix products, arithmetic and copies ran while one was open for 0% of the time, Pallas kernels for 10%

profile of v5, /device:TPU:0, one launch (start us, length us, event | category | flops | bytes accessed | tf_op | source)
XLA Modules:
  0.0 127.7 jit_solution(6854545576844912239)
XLA Ops:
  0.0 3.1 %collective-permute-start.3 = (bf16[128,2048]{1,0:T(8,128)(2,1)}, bf16[128,2048]{1,0:T(8,128)(2,1)}, u32[]{:S(2)}, u32[]{:S(2)}) collective-permute-start(bf16[128,2048]{1,0:T(8,128)(2,1)} %own_ref.1), channel_id=1, source_target_pairs={{0,2},{1,3},{2,4},{3,5},{4,6},{5,7},{6,0},{7,1},{8,10},{9,11},{10,... | collective-permute-start | bytes 1572872 | tf_op jit(solution)/shard_map/ppermute | solution.py:94
  3.1 2.1 %collective-permute-start.10 = (bf16[128,2048]{1,0:T(8,128)(2,1)}, bf16[128,2048]{1,0:T(8,128)(2,1)}, u32[]{:S(2)}, u32[]{:S(2)}) collective-permute-start(bf16[128,2048]{1,0:T(8,128)(2,1)} %own_ref.1), channel_id=1, source_target_pairs={{0,6},{1,7},{2,0},{3,1},{4,2},{5,3},{6,4},{7,5},{8,14},{9,15},{10,... | collective-permute-start | bytes 1572872 | tf_op jit(solution)/shard_map/ppermute | solution.py:94
  5.1 2.9 %collective-permute-start.13 = (bf16[128,2048]{1,0:T(8,128)(2,1)}, bf16[128,2048]{1,0:T(8,128)(2,1)S(1)}, u32[]{:S(2)}, u32[]{:S(2)}) collective-permute-start(bf16[128,2048]{1,0:T(8,128)(2,1)} %own_ref.1), channel_id=1, source_target_pairs={{0,4},{1,5},{6,2},{7,3},{8,12},{9,13},{14,10},{15,11},{16,20},{17,... | collective-permute-start | bytes 1572872 | tf_op jit(solution)/shard_map/ppermute | solution.py:94
  8.0 10.2 %collective-permute-done.3.own_ref = bf16[128,2048]{1,0:T(8,128)(2,1)} collective-permute-done((bf16[128,2048]{1,0:T(8,128)(2,1)}, bf16[128,2048]{1,0:T(8,128)(2,1)}, u32[]{:S(2)}, u32[]{:S(2)}) %collective-permute-start.3) | collective-permute-done | bytes 524320 | tf_op jit(solution)/shard_map/ppermute | solution.py:94
  18.9 9.1 %collective-permute-done.10.own_ref = bf16[128,2048]{1,0:T(8,128)(2,1)} collective-permute-done((bf16[128,2048]{1,0:T(8,128)(2,1)}, bf16[128,2048]{1,0:T(8,128)(2,1)}, u32[]{:S(2)}, u32[]{:S(2)}) %collective-permute-start.10) | collective-permute-done | bytes 524320 | tf_op jit(solution)/shard_map/ppermute | solution.py:94
  28.0 1.3 %collective-permute-start.15 = (bf16[128,2048]{1,0:T(8,128)(2,1)}, bf16[128,2048]{1,0:T(8,128)(2,1)S(1)}, u32[]{:S(2)}, u32[]{:S(2)}) collective-permute-start(bf16[128,2048]{1,0:T(8,128)(2,1)} %collective-permute-done.10.own_ref), channel_id=1, source_target_pairs={{2,0},{3,1},{10,8},{11,9},{18,16},{19,17},{26,24},{27,25}} | collective-permute-start | bytes 1572872 | tf_op jit(solution)/shard_map/ppermute | solution.py:94
  29.9 7.2 %collective-permute-done.13 = bf16[128,2048]{1,0:T(8,128)(2,1)S(1)} collective-permute-done((bf16[128,2048]{1,0:T(8,128)(2,1)}, bf16[128,2048]{1,0:T(8,128)(2,1)S(1)}, u32[]{:S(2)}, u32[]{:S(2)}) %collective-permute-start.13) | collective-permute-done | bytes 524320 | tf_op jit(solution)/shard_map/ppermute | solution.py:94
  37.1 6.3 %collective-permute-done.15 = bf16[128,2048]{1,0:T(8,128)(2,1)S(1)} collective-permute-done((bf16[128,2048]{1,0:T(8,128)(2,1)}, bf16[128,2048]{1,0:T(8,128)(2,1)S(1)}, u32[]{:S(2)}, u32[]{:S(2)}) %collective-permute-start.15) | collective-permute-done | bytes 524320 | tf_op jit(solution)/shard_map/ppermute | solution.py:94
  43.6 5.5 %collective-permute-start.7 = (s32[4,128]{1,0:T(4,128)S(1)}, s32[4,128]{1,0:T(4,128)S(1)}, u32[]{:S(2)}, u32[]{:S(2)}) collective-permute-start(s32[4,128]{1,0:T(4,128)S(1)} %bitcast.14), channel_id=1, source_target_pairs={{0,4},{1,5},{2,6},{3,7},{4,0},{5,1},{6,2},{7,3},{8,12},{9,13},{10,... | collective-permute-start | bytes 6152 | tf_op jit(solution)/shard_map/ppermute | solution.py:94
  49.0 1.6 %collective-permute-done.7 = s32[4,128]{1,0:T(4,128)S(1)} collective-permute-done((s32[4,128]{1,0:T(4,128)S(1)}, s32[4,128]{1,0:T(4,128)S(1)}, u32[]{:S(2)}, u32[]{:S(2)}) %collective-permute-start.7) | collective-permute-done | bytes 2080 | tf_op jit(solution)/shard_map/ppermute | solution.py:94
  50.6 4.7 %collective-permute-start.6 = (s32[4,128]{1,0:T(4,128)S(1)}, s32[4,128]{1,0:T(4,128)S(1)}, u32[]{:S(2)}, u32[]{:S(2)}) collective-permute-start(s32[4,128]{1,0:T(4,128)S(1)} %bitcast.15), channel_id=1, source_target_pairs={{0,6},{1,7},{2,0},{3,1},{4,2},{5,3},{6,4},{7,5},{8,14},{9,15},{10,... | collective-permute-start | bytes 6152 | tf_op jit(solution)/shard_map/ppermute | solution.py:94
  55.3 1.3 %collective-permute-done.6 = s32[4,128]{1,0:T(4,128)S(1)} collective-permute-done((s32[4,128]{1,0:T(4,128)S(1)}, s32[4,128]{1,0:T(4,128)S(1)}, u32[]{:S(2)}, u32[]{:S(2)}) %collective-permute-start.6) | collective-permute-done | bytes 2080 | tf_op jit(solution)/shard_map/ppermute | solution.py:94
  56.7 5.6 %collective-permute-done.5 = s32[4,128]{1,0:T(4,128)S(1)} collective-permute-done((s32[4,128]{1,0:T(4,128)S(1)}, s32[4,128]{1,0:T(4,128)S(1)}, u32[]{:S(2)}, u32[]{:S(2)}) %collective-permute-start.5) | collective-permute-done | bytes 2080 | tf_op jit(solution)/shard_map/ppermute | solution.py:94
  63.6 1.6 %copy-done.1 = bf16[1,2048,512]{2,1,0:T(8,128)(2,1)S(1)} copy-done((bf16[1,2048,512]{2,1,0:T(8,128)(2,1)S(1)}, bf16[1,2048,512]{2,1,0:T(8,128)(2,1)}, u32[]{:S(2)}) %copy-start.1) | copy-done | bytes 2097176
  66.3 1.7 %hidden.4.refs_0_ = bf16[256,512]{1,0:T(8,128)(2,1)S(1)} custom-call(s32[1]{0:T(128)} %bitcast.1.me_ref, bf16[128,2048]{1,0:T(8,128)(2,1)S(1)} %copy-done.2, bf16[128,2048]{1,0:T(8,128)(2,1)S(1)} %collective-permute-done.other_ref, s32[4,128]{1,0:T(4,128)S(1)} %bitcast.18, s32[4,128]{1,0:T(4,128)S(1)} %collective-permute-done.1.other_names_ref, ...), custom_call_target="tpu_custom_call" | custom-call | flops 1073741824 | bytes 5505024 | tf_op jit(solution)/shard_map/hidden/pallas_call | solution.py:41
  68.0 1.6 %collective-permute-start.2 = (bf16[256,512]{1,0:T(8,128)(2,1)S(1)}, bf16[256,512]{1,0:T(8,128)(2,1)}, u32[]{:S(2)}, u32[]{:S(2)}) collective-permute-start(bf16[256,512]{1,0:T(8,128)(2,1)S(1)} %hidden.4.refs_0_), channel_id=1, source_target_pairs={{0,8},{8,0},{1,9},{9,1},{2,10},{10,2},{3,11},{11,3},{4,12},{12,4},... | collective-permute-start | bytes 786440 | tf_op jit(solution)/shard_map/ppermute | solution.py:96
  69.6 3.0 %hidden.5.refs_2_ = bf16[256,512]{1,0:T(8,128)(2,1)S(1)} custom-call(s32[1]{0:T(128)} %bitcast.1.me_ref, bf16[128,2048]{1,0:T(8,128)(2,1)} %collective-permute-done.3.own_ref, bf16[128,2048]{1,0:T(8,128)(2,1)} %collective-permute-done.4.other_ref, s32[12,128]{1,0:T(8,128)S(1)} %pad_add_fusion.own_names_ref, ...), custom_call_target="tpu_custom_call" | custom-call | flops 1073741824 | bytes 5505024 | tf_op jit(solution)/shard_map/hidden/pallas_call | solution.py:41
  73.1 3.7 %hidden.6.refs_4_ = bf16[256,512]{1,0:T(8,128)(2,1)} custom-call(s32[1]{0:T(128)} %bitcast.1.me_ref, bf16[128,2048]{1,0:T(8,128)(2,1)} %collective-permute-done.10.own_ref, bf16[128,2048]{1,0:T(8,128)(2,1)} %collective-permute-done.11.other_ref, s32[12,128]{1,0:T(8,128)S(1)} %pad_add_fusion.own_names_ref, ...), custom_call_target="tpu_custom_call" | custom-call | flops 1073741824 | bytes 5505024 | tf_op jit(solution)/shard_map/hidden/pallas_call | solution.py:41
  76.8 1.5 %collective-permute-start.12 = (bf16[256,512]{1,0:T(8,128)(2,1)}, bf16[256,512]{1,0:T(8,128)(2,1)}, u32[]{:S(2)}, u32[]{:S(2)}) collective-permute-start(bf16[256,512]{1,0:T(8,128)(2,1)} %hidden.6.refs_4_), channel_id=1, source_target_pairs={{0,8},{8,0},{1,9},{9,1},{2,10},{10,2},{3,11},{11,3},{4,12},{12,4},... | collective-permute-start | bytes 786440 | tf_op jit(solution)/shard_map/ppermute | solution.py:96
  78.3 2.8 %hidden.7.refs_0_ = bf16[256,512]{1,0:T(8,128)(2,1)S(1)} custom-call(s32[1]{0:T(128)} %bitcast.1.me_ref, bf16[128,2048]{1,0:T(8,128)(2,1)S(1)} %add_add_fusion.own_ref, bf16[128,2048]{1,0:T(8,128)(2,1)} %collective-permute-done.16.other_ref, s32[12,128]{1,0:T(8,128)S(1)} %pad_add_fusion.own_names_ref, s32[12,128]{1,0:T(8,128)S(1)} %collective-permute-done.8.other_names_ref, ...), custom_call_target="tpu_custom_call" | custom-call | flops 1073741824 | bytes 5505024 | tf_op jit(solution)/shard_map/hidden/pallas_call | solution.py:41
  83.0 5.6 %collective-permute-done.12.refs_5_ = bf16[256,512]{1,0:T(8,128)(2,1)} collective-permute-done((bf16[256,512]{1,0:T(8,128)(2,1)}, bf16[256,512]{1,0:T(8,128)(2,1)}, u32[]{:S(2)}, u32[]{:S(2)}) %collective-permute-start.12) | collective-permute-done | bytes 262176 | tf_op jit(solution)/shard_map/ppermute | solution.py:96
  88.6 2.2 %partial_gram.1.early_ref = f32[512,512]{1,0:T(8,128)S(1)} custom-call(bf16[256,512]{1,0:T(8,128)(2,1)S(1)} %hidden.4.refs_0_, bf16[256,512]{1,0:T(8,128)(2,1)} %collective-permute-done.2.refs_1_, bf16[256,512]{1,0:T(8,128)(2,1)S(1)} %hidden.5.refs_2_, bf16[256,512]{1,0:T(8,128)(2,1)} %collective-permute-done.9.refs_3_, bf16[256,512]{1,0:T(8,128)(2,1)} %hidden.6.refs_4_, ...), custom_call_target="tpu_custom_call" | custom-call | flops 805306368 | bytes 2621440 | tf_op jit(solution)/shard_map/partial_gram/pallas_call | solution.py:71
  90.8 2.7 %collective-permute-done.17.refs_1_ = bf16[256,512]{1,0:T(8,128)(2,1)S(1)} collective-permute-done((bf16[256,512]{1,0:T(8,128)(2,1)S(1)}, bf16[256,512]{1,0:T(8,128)(2,1)S(1)}, u32[]{:S(2)}, u32[]{:S(2)}) %collective-permute-start.17) | collective-permute-done | bytes 262176 | tf_op jit(solution)/shard_map/ppermute | solution.py:96
  93.5 34.2 %factor.1 = f32[256,512]{1,0:T(8,128)} custom-call(s32[1]{0:T(128)} %bitcast.rank_ref, f32[512,512]{1,0:T(8,128)S(1)} %partial_gram.1.early_ref, bf16[256,512]{1,0:T(8,128)(2,1)S(1)} %hidden.7.refs_0_, bf16[256,512]{1,0:T(8,128)(2,1)S(1)} %collective-permute-done.17.refs_1_), custom_call_target="tpu_custom_call" | custom-call | tf_op jit(solution)/shard_map/factor/pallas_call | solution.py:235
  (28 shorter events, 6.2 us)
Async XLA Ops:
  0.0 43.6 %copy-start.3 = (s32[128,4]{0,1:T(4,128)S(1)}, s32[128,4]{0,1:T(4,128)}, u32[]{:S(2)}) copy-start(s32[128,4]{0,1:T(4,128)} %param.5) | copy-start | bytes 6148
  0.0 63.6 %copy-start = (bf16[1,2048,512]{2,1,0:T(8,128)(2,1)S(1)}, bf16[1,2048,512]{2,1,0:T(8,128)(2,1)}, u32[]{:S(2)}) copy-start(bf16[1,2048,512]{2,1,0:T(8,128)(2,1)} %param.6) | copy-start | bytes 6291460
  0.0 18.2 %collective-permute-start.3 = (bf16[128,2048]{1,0:T(8,128)(2,1)}, bf16[128,2048]{1,0:T(8,128)(2,1)}, u32[]{:S(2)}, u32[]{:S(2)}) collective-permute-start(bf16[128,2048]{1,0:T(8,128)(2,1)} %own_ref.1), channel_id=1, source_target_pairs={{0,2},{1,3},{2,4},{3,5},{4,6},{5,7},{6,0},{7,1},{8,10},{9,11},{10,... | collective-permute-start | bytes 1572872 | tf_op jit(solution)/shard_map/ppermute | solution.py:94
  3.1 24.9 %collective-permute-start.10 = (bf16[128,2048]{1,0:T(8,128)(2,1)}, bf16[128,2048]{1,0:T(8,128)(2,1)}, u32[]{:S(2)}, u32[]{:S(2)}) collective-permute-start(bf16[128,2048]{1,0:T(8,128)(2,1)} %own_ref.1), channel_id=1, source_target_pairs={{0,6},{1,7},{2,0},{3,1},{4,2},{5,3},{6,4},{7,5},{8,14},{9,15},{10,... | collective-permute-start | bytes 1572872 | tf_op jit(solution)/shard_map/ppermute | solution.py:94
  5.1 31.9 %collective-permute-start.13 = (bf16[128,2048]{1,0:T(8,128)(2,1)}, bf16[128,2048]{1,0:T(8,128)(2,1)S(1)}, u32[]{:S(2)}, u32[]{:S(2)}) collective-permute-start(bf16[128,2048]{1,0:T(8,128)(2,1)} %own_ref.1), channel_id=1, source_target_pairs={{0,4},{1,5},{6,2},{7,3},{8,12},{9,13},{14,10},{15,11},{16,20},{17,... | collective-permute-start | bytes 1572872 | tf_op jit(solution)/shard_map/ppermute | solution.py:94
  18.2 18.9 %collective-permute-start.14 = (bf16[128,2048]{1,0:T(8,128)(2,1)}, bf16[128,2048]{1,0:T(8,128)(2,1)S(1)}, u32[]{:S(2)}, u32[]{:S(2)}) collective-permute-start(bf16[128,2048]{1,0:T(8,128)(2,1)} %collective-permute-done.3.own_ref), channel_id=1, source_target_pairs={{4,6},{5,7},{12,14},{13,15},{20,22},{21,23},{28,30},{29,31}} | collective-permute-start | bytes 1572872 | tf_op jit(solution)/shard_map/ppermute | solution.py:94
  28.0 15.4 %collective-permute-start.15 = (bf16[128,2048]{1,0:T(8,128)(2,1)}, bf16[128,2048]{1,0:T(8,128)(2,1)S(1)}, u32[]{:S(2)}, u32[]{:S(2)}) collective-permute-start(bf16[128,2048]{1,0:T(8,128)(2,1)} %collective-permute-done.10.own_ref), channel_id=1, source_target_pairs={{2,0},{3,1},{10,8},{11,9},{18,16},{19,17},{26,24},{27,25}} | collective-permute-start | bytes 1572872 | tf_op jit(solution)/shard_map/ppermute | solution.py:94
  29.3 34.3 %collective-permute-start = (bf16[128,2048]{1,0:T(8,128)(2,1)}, bf16[128,2048]{1,0:T(8,128)(2,1)S(1)}, u32[]{:S(2)}, u32[]{:S(2)}) collective-permute-start(bf16[128,2048]{1,0:T(8,128)(2,1)} %own_ref.1), channel_id=1, source_target_pairs={{0,1},{1,0},{2,3},{3,2},{4,5},{5,4},{6,7},{7,6},{8,9},{9,8},{10,11... | collective-permute-start | bytes 1572872 | tf_op jit(solution)/shard_map/ppermute | solution.py:95
  29.4 40.2 %collective-permute-start.4 = (bf16[128,2048]{1,0:T(8,128)(2,1)}, bf16[128,2048]{1,0:T(8,128)(2,1)}, u32[]{:S(2)}, u32[]{:S(2)}) collective-permute-start(bf16[128,2048]{1,0:T(8,128)(2,1)} %collective-permute-done.3.own_ref), channel_id=1, source_target_pairs={{0,1},{1,0},{2,3},{3,2},{4,5},{5,4},{6,7},{7,6},{8,9},{9,8},{10,11... | collective-permute-start | bytes 1572872 | tf_op jit(solution)/shard_map/ppermute | solution.py:95
  37.1 36.1 %collective-permute-start.11 = (bf16[128,2048]{1,0:T(8,128)(2,1)}, bf16[128,2048]{1,0:T(8,128)(2,1)}, u32[]{:S(2)}, u32[]{:S(2)}) collective-permute-start(bf16[128,2048]{1,0:T(8,128)(2,1)} %collective-permute-done.10.own_ref), channel_id=1, source_target_pairs={{0,1},{1,0},{2,3},{3,2},{4,5},{5,4},{6,7},{7,6},{8,9},{9,8},{10,11... | collective-permute-start | bytes 1572872 | tf_op jit(solution)/shard_map/ppermute | solution.py:95
  43.5 34.8 %collective-permute-start.16 = (bf16[128,2048]{1,0:T(8,128)(2,1)S(1)}, bf16[128,2048]{1,0:T(8,128)(2,1)}, u32[]{:S(2)}, u32[]{:S(2)}) collective-permute-start(bf16[128,2048]{1,0:T(8,128)(2,1)S(1)} %add_add_fusion.own_ref), channel_id=1, source_target_pairs={{0,1},{1,0},{2,3},{3,2},{4,5},{5,4},{6,7},{7,6},{8,9},{9,8},{10,11... | collective-permute-start | bytes 1572872 | tf_op jit(solution)/shard_map/ppermute | solution.py:95
  43.6 7.0 %collective-permute-start.7 = (s32[4,128]{1,0:T(4,128)S(1)}, s32[4,128]{1,0:T(4,128)S(1)}, u32[]{:S(2)}, u32[]{:S(2)}) collective-permute-start(s32[4,128]{1,0:T(4,128)S(1)} %bitcast.14), channel_id=1, source_target_pairs={{0,4},{1,5},{2,6},{3,7},{4,0},{5,1},{6,2},{7,3},{8,12},{9,13},{10,... | collective-permute-start | bytes 6152 | tf_op jit(solution)/shard_map/ppermute | solution.py:94
  50.6 6.0 %collective-permute-start.6 = (s32[4,128]{1,0:T(4,128)S(1)}, s32[4,128]{1,0:T(4,128)S(1)}, u32[]{:S(2)}, u32[]{:S(2)}) collective-permute-start(s32[4,128]{1,0:T(4,128)S(1)} %bitcast.15), channel_id=1, source_target_pairs={{0,6},{1,7},{2,0},{3,1},{4,2},{5,3},{6,4},{7,5},{8,14},{9,15},{10,... | collective-permute-start | bytes 6152 | tf_op jit(solution)/shard_map/ppermute | solution.py:94
  56.7 5.6 %collective-permute-start.5 = (s32[4,128]{1,0:T(4,128)S(1)}, s32[4,128]{1,0:T(4,128)S(1)}, u32[]{:S(2)}, u32[]{:S(2)}) collective-permute-start(s32[4,128]{1,0:T(4,128)S(1)} %bitcast.16), channel_id=1, source_target_pairs={{0,2},{1,3},{2,4},{3,5},{4,6},{5,7},{6,0},{7,1},{8,10},{9,11},{10,... | collective-permute-start | bytes 6152 | tf_op jit(solution)/shard_map/ppermute | solution.py:94
  62.3 1.2 collective-permute-start.1
  63.5 6.1 %collective-permute-start.8 = (s32[12,128]{1,0:T(8,128)S(1)}, s32[12,128]{1,0:T(8,128)S(1)}, u32[]{:S(2)}, u32[]{:S(2)}) collective-permute-start(s32[12,128]{1,0:T(8,128)S(1)} %pad_add_fusion.own_names_ref), channel_id=1, source_target_pairs={{0,1},{1,0},{2,3},{3,2},{4,5},{5,4},{6,7},{7,6},{8,9},{9,8},{10,11... | collective-permute-start | bytes 18440 | tf_op jit(solution)/shard_map/ppermute | solution.py:95
  63.6 1.6 %copy-start.1 = (bf16[1,2048,512]{2,1,0:T(8,128)(2,1)S(1)}, bf16[1,2048,512]{2,1,0:T(8,128)(2,1)}, u32[]{:S(2)}) copy-start(bf16[1,2048,512]{2,1,0:T(8,128)(2,1)} %param.7) | copy-start | bytes 6291460
  65.2 1.0 copy-start.2
  68.0 13.7 %collective-permute-start.2 = (bf16[256,512]{1,0:T(8,128)(2,1)S(1)}, bf16[256,512]{1,0:T(8,128)(2,1)}, u32[]{:S(2)}, u32[]{:S(2)}) collective-permute-start(bf16[256,512]{1,0:T(8,128)(2,1)S(1)} %hidden.4.refs_0_), channel_id=1, source_target_pairs={{0,8},{8,0},{1,9},{9,1},{2,10},{10,2},{3,11},{11,3},{4,12},{12,4},... | collective-permute-start | bytes 786440 | tf_op jit(solution)/shard_map/ppermute | solution.py:96
  72.5 10.4 %collective-permute-start.9 = (bf16[256,512]{1,0:T(8,128)(2,1)S(1)}, bf16[256,512]{1,0:T(8,128)(2,1)}, u32[]{:S(2)}, u32[]{:S(2)}) collective-permute-start(bf16[256,512]{1,0:T(8,128)(2,1)S(1)} %hidden.5.refs_2_), channel_id=1, source_target_pairs={{0,8},{8,0},{1,9},{9,1},{2,10},{10,2},{3,11},{11,3},{4,12},{12,4},... | collective-permute-start | bytes 786440 | tf_op jit(solution)/shard_map/ppermute | solution.py:96
  76.8 11.8 %collective-permute-start.12 = (bf16[256,512]{1,0:T(8,128)(2,1)}, bf16[256,512]{1,0:T(8,128)(2,1)}, u32[]{:S(2)}, u32[]{:S(2)}) collective-permute-start(bf16[256,512]{1,0:T(8,128)(2,1)} %hidden.6.refs_4_), channel_id=1, source_target_pairs={{0,8},{8,0},{1,9},{9,1},{2,10},{10,2},{3,11},{11,3},{4,12},{12,4},... | collective-permute-start | bytes 786440 | tf_op jit(solution)/shard_map/ppermute | solution.py:96
  81.1 12.4 %collective-permute-start.17 = (bf16[256,512]{1,0:T(8,128)(2,1)S(1)}, bf16[256,512]{1,0:T(8,128)(2,1)S(1)}, u32[]{:S(2)}, u32[]{:S(2)}) collective-permute-start(bf16[256,512]{1,0:T(8,128)(2,1)S(1)} %hidden.7.refs_0_), channel_id=1, source_target_pairs={{0,8},{8,0},{1,9},{9,1},{2,10},{10,2},{3,11},{11,3},{4,12},{12,4},... | collective-permute-start | bytes 786440 | tf_op jit(solution)/shard_map/ppermute | solution.py:96

commit v6 on v5

--- a/solution.py
+++ b/solution.py
@@ -13,16 +13,22 @@
 CHIPS_DENSE = 4
 
 
-def hidden_kernel(me_ref, own_ref, other_ref, own_names_ref, other_names_ref, gate_ref, up_ref, hidden_ref, *, at, top):
+def hidden_kernel(me_ref, own_names_ref, other_names_ref, gate_ref, up_ref, *refs, at, top, first):
+    pieces, hidden_ref = refs[:-1], refs[-1]
+    rows = hidden_ref.shape[0] // CORES
     hw = gate_ref.shape[1]
     width = 256
     mine = slice(at * top, (at + 1) * top)
     named = jnp.concatenate([own_names_ref[mine, :], other_names_ref[mine, :]], axis=0) == me_ref[0]
     named = named.astype(jnp.float32).T
     member = jnp.concatenate(
-        [jnp.max(named[:, c * top : (c + 1) * top], axis=1, keepdims=True) for c in range(CORES)], axis=0
-    )
-    x = jnp.concatenate([own_ref[...], other_ref[...]], axis=0)
+        [
+            jnp.max(named[first : first + rows, c * top : (c + 1) * top], axis=1, keepdims=True)
+            for c in range(CORES)
+        ],
+        axis=0,
+    )
+    x = jnp.concatenate([piece[...] for piece in pieces], axis=0)
 
     def step(i, carry):
         columns = pl.ds(pl.multiple_of(i * width, width), width)
@@ -35,22 +41,22 @@
     lax.fori_loop(0, hw // width, step, 0)
 
 
-def hidden_of(me, own, other, own_names, other_names, at, top, gate_w, up_w):
-    rows, model = own.shape
-    hw = gate_w.shape[1]
+def hidden_of(me, pieces, names, at, top, first, gate_w, up_w):
+    rows = sum(piece.shape[0] for piece in pieces)
+    model, hw = gate_w.shape
     return pl.pallas_call(
-        functools.partial(hidden_kernel, at=at, top=top),
-        in_specs=[pl.BlockSpec(memory_space=pltpu.SMEM)] + [pl.BlockSpec(memory_space=pltpu.VMEM)] * 6,
+        functools.partial(hidden_kernel, at=at, top=top, first=first),
+        in_specs=[pl.BlockSpec(memory_space=pltpu.SMEM)] + [pl.BlockSpec(memory_space=pltpu.VMEM)] * (4 + len(pieces)),
         out_specs=pl.BlockSpec(memory_space=pltpu.VMEM),
-        out_shape=jax.ShapeDtypeStruct((CORES * rows, hw), jnp.bfloat16),
+        out_shape=jax.ShapeDtypeStruct((rows, hw), jnp.bfloat16),
         compiler_params=pltpu.CompilerParams(vmem_limit_bytes=24 << 20),
         cost_estimate=pl.CostEstimate(
-            flops=2 * CORES * rows * model * 2 * hw,
-            bytes_accessed=2 * (CORES * rows * model + 2 * model * hw) + 2 * CORES * rows * hw,
-            transcendentals=CORES * rows * hw,
+            flops=2 * rows * model * 2 * hw,
+            bytes_accessed=2 * (rows * model + 2 * model * hw) + 2 * rows * hw,
+            transcendentals=rows * hw,
         ),
         name="hidden",
-    )(me, own, other, own_names, other_names, gate_w, up_w)
+    )(me, *names, gate_w, up_w, *pieces)
 
 
 def gram_of(refs):
@@ -67,7 +73,8 @@
 
 
 def partial_gram(hiddens):
-    rows, hw = hiddens[0].shape
+    rows = sum(hidden.shape[0] for hidden in hiddens)
+    hw = hiddens[0].shape[1]
     return pl.pallas_call(
         gram_kernel,
         in_specs=[pl.BlockSpec(memory_space=pltpu.VMEM)] * len(hiddens),
@@ -75,48 +82,109 @@
         out_shape=jax.ShapeDtypeStruct((hw, hw), jnp.float32),
         compiler_params=pltpu.CompilerParams(vmem_limit_bytes=24 << 20),
         cost_estimate=pl.CostEstimate(
-            flops=2 * len(hiddens) * rows * hw * hw,
-            bytes_accessed=2 * len(hiddens) * rows * hw + 4 * hw * hw,
+            flops=2 * rows * hw * hw,
+            bytes_accessed=2 * rows * hw + 4 * hw * hw,
             transcendentals=0,
         ),
         name="partial_gram",
     )(*hiddens)
 
 
+def pick_kernel(chip_ref, *refs, wanted):
+    sources, out_ref = refs[:-1], refs[-1]
+    rows = sources[0].shape[0]
+    parts = out_ref.shape[0] // rows
+    kinds = len(sources) // parts
+    for kind in range(kinds):
+        here = functools.reduce(lambda a, b: a | b, [chip_ref[0] == c for c, k in enumerate(wanted) if k == kind])
+
+        @pl.when(here)
+        def _():
+            for part in range(parts):
+                out_ref[part * rows : (part + 1) * rows, :] = sources[part * kinds + kind][...]
+
+
+def pick(chip, parts, wanted):
+    rows, model = parts[0][0].shape
+    return pl.pallas_call(
+        functools.partial(pick_kernel, wanted=wanted),
+        in_specs=[pl.BlockSpec(memory_space=pltpu.SMEM)]
+        + [pl.BlockSpec(memory_space=pltpu.VMEM)] * sum(len(part) for part in parts),
+        out_specs=pl.BlockSpec(memory_space=pltpu.VMEM),
+        out_shape=jax.ShapeDtypeStruct((len(parts) * rows, model), parts[0][0].dtype),
+        compiler_params=pltpu.CompilerParams(vmem_limit_bytes=8 << 20),
+        cost_estimate=pl.CostEstimate(
+            flops=0, bytes_accessed=4 * len(parts) * rows * model, transcendentals=0
+        ),
+        name="pick",
+    )(chip.reshape(1), *sum(parts, []))
+
+
 def between_chips(pairs):
     return [(s * CORES + c, d * CORES + c) for s, d in pairs for c in range(CORES)]
 
 
 def gathered(tokens, routes, gate_w, up_w):
     me = lax.axis_index("expert").astype(jnp.int32).reshape(1)
+    chip = lax.axis_index("expert") // CORES
     data_ranks = lax.axis_size("dp")
-    top = routes.shape[1]
-    move = lambda x, pairs: lax.ppermute(x, "expert", between_chips(pairs))
-    swap = lambda x: lax.ppermute(x, "expert", [(e, e ^ 1) for e in range(CHIPS_DENSE * CORES)])
-    turn = lambda x, s: lax.ppermute(x, "dp", [(r, (r + s) % data_ranks) for r in range(data_ranks)])
-    ring = lambda s: [(z, (z + s) % CHIPS_DENSE) for z in range(CHIPS_DENSE)]
+    rows, top = routes.shape
+    half = rows // 2
+    swap_pairs = [(e, e ^ 1) for e in range(CHIPS_DENSE * CORES)]
+
+    def move(x, pairs):
+        return lax.ppermute(x, "expert", between_chips(pairs))
+
+    def swap(x):
+        return lax.ppermute(x, "expert", swap_pairs)
+
+    def turns(x):
+        shifts = [[(r, (r + s) % data_ranks) for r in range(data_ranks)] for s in range(1, data_ranks)]
+        return [x] + [lax.ppermute(x, "dp", pairs) for pairs in shifts]
+
+    up, down = [(0, 1), (1, 2), (2, 3)], [(3, 2), (2, 1), (1, 0)]
+    halves = []
+    for h in range(2):
+        ups, downs = [], []
+        x = y = tokens[h * half : (h + 1) * half]
+        for hop in range(3):
+            x = move(x, up[hop:])
+            y = move(y, down[hop:])
+            ups.append(x)
+            downs.append(y)
+        halves.append((ups, downs))
+    near = pick(chip, [[u[0], d[0]] for u, d in halves], (1, 0, 0, 0))
+    middle = pick(chip, [[u[1], d[0], d[1]] for u, d in halves], (2, 1, 1, 0))
+    last = [pick(chip, [[u[2], u[1], d[1], d[2]]], (3, 2, 1, 0)) for u, d in halves]
 
     names = routes.T
-    below = move(tokens, ring(1))
-    above = move(tokens, ring(-1))
-    far = move(tokens, [(0, 2), (3, 1)])
-    on_up = move(below, [(2, 3)])
-    on_down = move(above, [(1, 0)])
-    moved = []
-    for pairs in [ring(1), ring(-1), ring(2)]:
-        moved.append(move(names, pairs))
-    moved = jnp.concatenate(moved, axis=0)
-    other_names = swap(names)
-    other_moved = swap(moved)
-
+    by_one, by_two, by_three = (
+        move(names, [(z, (z + s) % CHIPS_DENSE) for z in range(CHIPS_DENSE)]) for s in (1, 2, 3)
+    )
+    ends = (chip == 0) | (chip == 3)
+    moved = jnp.concatenate(
+        [
+            jnp.where(chip == 0, by_three, by_one),
+            jnp.where(ends, by_two, by_three),
+            jnp.where(chip == 0, by_one, jnp.where(chip == 3, by_three, by_two)),
+        ],
+        axis=0,
+    )
+    own_names = (names, swap(names))
+    moved_names = (moved, swap(moved))
+
+    blocks = [
+        (tokens, own_names, 0, 0),
+        (near, moved_names, 0, 0),
+        (middle, moved_names, 1, 0),
+        (last[0], moved_names, 2, 0),
+        (last[1], moved_names, 2, half),
+    ]
     hiddens = []
-    for slot, own in enumerate([tokens, below, above, far + on_up + on_down]):
-        other = swap(own)
-        if slot == 0:
-            hidden = hidden_of(me, own, other, names, other_names, 0, top, gate_w, up_w)
-        else:
-            hidden = hidden_of(me, own, other, moved, other_moved, slot - 1, top, gate_w, up_w)
-        hiddens.append([hidden] + [turn(hidden, s) for s in range(1, data_ranks)])
+    for own, who, at, first in blocks:
+        pieces = (own, swap(own))
+        hidden = hidden_of(me, pieces, who, at, top, first, gate_w, up_w)
+        hiddens.append(turns(hidden))
     early = partial_gram(sum(hiddens[:-1], []))
     return early, hiddens[-1]
 

time: 128 us -> 121 us (0.945)
  the two profiles are of different devices: /device:TPU:0 before, /device:TPU:24 now
where the time goes in v6:
time: 121 us; the launch traced here: 120 us
  Pallas kernels  51.5 us (43%)
  starting transfers between devices  35.4 us (29%)
  waiting for transfers between devices  27.4 us (23%)
  local copies, waits for them, and re-layouts  5.28 us (4%)
    pallas_call x1, Pallas kernels, factor_rows(): pl.pallas_call(functools.partial(factor_kernel, rows_mean=rows_mean), in_...  34.2 us
    ppermute x15, starting transfers between devices, move(): return lax.ppermute(x, 'expert', between_chips(pairs))  28.4 us
    ppermute x15, waiting for transfers between devices, move(): return lax.ppermute(x, 'expert', between_chips(pairs))  18.1 us
    pallas_call x5, Pallas kernels, hidden_of(): pl.pallas_call(functools.partial(hidden_kernel, at=at, top=top, first=fir...  10.3 us
    ppermute x5, waiting for transfers between devices, turns(): return [x] + [lax.ppermute(x, 'dp', pairs) for pairs in shifts]  9.32 us
    ppermute x5, starting transfers between devices, turns(): return [x] + [lax.ppermute(x, 'dp', pairs) for pairs in shifts]  5.87 us
    pallas_call x4, Pallas kernels, pick(): pl.pallas_call(functools.partial(pick_kernel, wanted=wanted), in_specs=[p...  4.51 us
    unnamed x14, local copies, waits for them, and re-layouts  4.2 us
  transfers between devices with their start and end apart: 27, of which 6 were waited for; matrix products, arithmetic and copies ran while one was open for 0% of the time, Pallas kernels for 14%

profile of v6, /device:TPU:24, one launch (start us, length us, event | category | flops | bytes accessed | tf_op | source)
XLA Modules:
  0.0 119.9 jit_solution(17410756017567153481)
XLA Ops:
  1.1 2.5 %collective-permute-start.10 = (bf16[64,2048]{1,0:T(8,128)(2,1)S(1)}, bf16[64,2048]{1,0:T(8,128)(2,1)S(1)}, u32[]{:S(2)}, u32[]{:S(2)}) collective-permute-start(bf16[64,2048]{1,0:T(8,128)(2,1)S(1)} %get-tuple-element.5), channel_id=1, source_target_pairs={{6,4},{7,5},{4,2},{5,3},{2,0},{3,1},{14,12},{15,13},{12,10},{13,11... | collective-permute-start | bytes 786440 | tf_op jit(solution)/shard_map/ppermute | solution.py:136
  3.6 1.3 %collective-permute-start.9 = (bf16[64,2048]{1,0:T(8,128)(2,1)S(1)}, bf16[64,2048]{1,0:T(8,128)(2,1)}, u32[]{:S(2)}, u32[]{:S(2)}) collective-permute-start(bf16[64,2048]{1,0:T(8,128)(2,1)S(1)} %get-tuple-element.5), channel_id=1, source_target_pairs={{0,2},{1,3},{2,4},{3,5},{4,6},{5,7},{8,10},{9,11},{10,12},{11,13},... | collective-permute-start | bytes 786440 | tf_op jit(solution)/shard_map/ppermute | solution.py:136
  4.9 2.7 %collective-permute-start.3 = (s32[4,128]{1,0:T(4,128)}, s32[4,128]{1,0:T(4,128)S(1)}, u32[]{:S(2)}, u32[]{:S(2)}) collective-permute-start(s32[4,128]{1,0:T(4,128)} %bitcast.17), channel_id=1, source_target_pairs={{0,6},{1,7},{2,0},{3,1},{4,2},{5,3},{6,4},{7,5},{8,14},{9,15},{10,... | collective-permute-start | bytes 6152 | tf_op jit(solution)/shard_map/ppermute | solution.py:136
  7.6 3.0 %collective-permute-start.8 = (bf16[64,2048]{1,0:T(8,128)(2,1)S(1)}, bf16[64,2048]{1,0:T(8,128)(2,1)}, u32[]{:S(2)}, u32[]{:S(2)}) collective-permute-start(bf16[64,2048]{1,0:T(8,128)(2,1)S(1)} %get-tuple-element.6), channel_id=1, source_target_pairs={{6,4},{7,5},{4,2},{5,3},{2,0},{3,1},{14,12},{15,13},{12,10},{13,11... | collective-permute-start | bytes 786440 | tf_op jit(solution)/shard_map/ppermute | solution.py:136
  13.0 2.3 %collective-permute-start.4 = (s32[4,128]{1,0:T(4,128)}, s32[4,128]{1,0:T(4,128)S(1)}, u32[]{:S(2)}, u32[]{:S(2)}) collective-permute-start(s32[4,128]{1,0:T(4,128)} %bitcast.18), channel_id=1, source_target_pairs={{0,2},{1,3},{2,4},{3,5},{4,6},{5,7},{6,0},{7,1},{8,10},{9,11},{10,... | collective-permute-start | bytes 6152 | tf_op jit(solution)/shard_map/ppermute | solution.py:136
  15.3 4.3 %collective-permute-done.4 = s32[4,128]{1,0:T(4,128)S(1)} collective-permute-done((s32[4,128]{1,0:T(4,128)}, s32[4,128]{1,0:T(4,128)S(1)}, u32[]{:S(2)}, u32[]{:S(2)}) %collective-permute-start.4) | collective-permute-done | bytes 2080 | tf_op jit(solution)/shard_map/ppermute | solution.py:136
  19.6 1.4 %collective-permute-start.16 = (bf16[64,2048]{1,0:T(8,128)(2,1)S(1)}, bf16[64,2048]{1,0:T(8,128)(2,1)}, u32[]{:S(2)}, u32[]{:S(2)}) collective-permute-start(bf16[64,2048]{1,0:T(8,128)(2,1)S(1)} %collective-permute-done.10.refs_3_.refs_4_), channel_id=1, source_target_pairs={{4,2},{5,3},{2,0},{3,1},{12,10},{13,11},{10,8},{11,9},{20,18},{21,... | collective-permute-start | bytes 786440 | tf_op jit(solution)/shard_map/ppermute | solution.py:136
  21.7 1.3 %collective-permute-start.15 = (bf16[64,2048]{1,0:T(8,128)(2,1)}, bf16[64,2048]{1,0:T(8,128)(2,1)}, u32[]{:S(2)}, u32[]{:S(2)}) collective-permute-start(bf16[64,2048]{1,0:T(8,128)(2,1)} %collective-permute-done.9.refs_2_), channel_id=1, source_target_pairs={{2,4},{3,5},{4,6},{5,7},{10,12},{11,13},{12,14},{13,15},{18,20},{1... | collective-permute-start | bytes 786440 | tf_op jit(solution)/shard_map/ppermute | solution.py:136
  23.7 1.3 %collective-permute-start.13 = (bf16[64,2048]{1,0:T(8,128)(2,1)}, bf16[64,2048]{1,0:T(8,128)(2,1)}, u32[]{:S(2)}, u32[]{:S(2)}) collective-permute-start(bf16[64,2048]{1,0:T(8,128)(2,1)} %collective-permute-done.7.refs_0_), channel_id=1, source_target_pairs={{2,4},{3,5},{4,6},{5,7},{10,12},{11,13},{12,14},{13,15},{18,20},{1... | collective-permute-start | bytes 786440 | tf_op jit(solution)/shard_map/ppermute | solution.py:136
  25.0 1.4 %collective-permute-start.24 = (bf16[64,2048]{1,0:T(8,128)(2,1)}, bf16[64,2048]{1,0:T(8,128)(2,1)}, u32[]{:S(2)}, u32[]{:S(2)}) collective-permute-start(bf16[64,2048]{1,0:T(8,128)(2,1)} %collective-permute-done.16.refs_5_.refs_2_), channel_id=1, source_target_pairs={{2,0},{3,1},{10,8},{11,9},{18,16},{19,17},{26,24},{27,25}} | collective-permute-start | bytes 786440 | tf_op jit(solution)/shard_map/ppermute | solution.py:136
  28.5 4.8 %collective-permute-done.15.refs_3_.refs_1_ = bf16[64,2048]{1,0:T(8,128)(2,1)} collective-permute-done((bf16[64,2048]{1,0:T(8,128)(2,1)}, bf16[64,2048]{1,0:T(8,128)(2,1)}, u32[]{:S(2)}, u32[]{:S(2)}) %collective-permute-start.15) | collective-permute-done | bytes 262176 | tf_op jit(solution)/shard_map/ppermute | solution.py:136
  33.3 6.0 %collective-permute-start.5 = (s32[4,128]{1,0:T(4,128)S(1)}, s32[4,128]{1,0:T(4,128)S(1)}, u32[]{:S(2)}, u32[]{:S(2)}) collective-permute-start(s32[4,128]{1,0:T(4,128)S(1)} %bitcast.19), channel_id=1, source_target_pairs={{0,4},{1,5},{2,6},{3,7},{4,0},{5,1},{6,2},{7,3},{8,12},{9,13},{10,... | collective-permute-start | bytes 6152 | tf_op jit(solution)/shard_map/ppermute | solution.py:136
  44.1 1.3 %collective-permute-start.19 = (bf16[64,2048]{1,0:T(8,128)(2,1)}, bf16[64,2048]{1,0:T(8,128)(2,1)S(1)}, u32[]{:S(2)}, u32[]{:S(2)}) collective-permute-start(bf16[64,2048]{1,0:T(8,128)(2,1)} %collective-permute-done.13.refs_0_.refs_1_), channel_id=1, source_target_pairs={{4,6},{5,7},{12,14},{13,15},{20,22},{21,23},{28,30},{29,31}} | collective-permute-start | bytes 786440 | tf_op jit(solution)/shard_map/ppermute | solution.py:136
  45.4 7.9 %collective-permute-done.23.refs_0_ = bf16[64,2048]{1,0:T(8,128)(2,1)S(1)} collective-permute-done((bf16[64,2048]{1,0:T(8,128)(2,1)}, bf16[64,2048]{1,0:T(8,128)(2,1)S(1)}, u32[]{:S(2)}, u32[]{:S(2)}) %collective-permute-start.23) | collective-permute-done | bytes 262176 | tf_op jit(solution)/shard_map/ppermute | solution.py:136
  53.4 1.6 %copy-done.1 = bf16[1,2048,512]{2,1,0:T(8,128)(2,1)S(1)} copy-done((bf16[1,2048,512]{2,1,0:T(8,128)(2,1)S(1)}, bf16[1,2048,512]{2,1,0:T(8,128)(2,1)}, u32[]{:S(2)}) %copy-start.1) | copy-done | bytes 2097176
  55.0 3.5 %hidden.5.refs_0_ = bf16[256,512]{1,0:T(8,128)(2,1)} custom-call(s32[1]{0:T(128)} %bitcast.1.me_ref, s32[4,128]{1,0:T(4,128)S(1)} %bitcast.21, s32[4,128]{1,0:T(4,128)S(1)} %collective-permute-done.other_names_ref, bf16[2048,512]{1,0:T(8,128)(2,1)S(1)} %bitcast.7, bf16[2048,512]{1,0:T(8,128)(2,1)S(1)} %bitcast.12, bf16[128,2048]{1,0:T(8,128)(2,1)S(1)} %copy-done.2, ...), custom_call_target="tpu_custom_call" | custom-call | flops 1073741824 | bytes 5505024 | tf_op jit(solution)/shard_map/hidden/pallas_call | solution.py:47
  59.7 1.6 %collective-permute-start.2 = (bf16[256,512]{1,0:T(8,128)(2,1)}, bf16[256,512]{1,0:T(8,128)(2,1)}, u32[]{:S(2)}, u32[]{:S(2)}) collective-permute-start(bf16[256,512]{1,0:T(8,128)(2,1)} %hidden.5.refs_0_), channel_id=1, source_target_pairs={{0,8},{8,0},{1,9},{9,1},{2,10},{10,2},{3,11},{11,3},{4,12},{12,4},... | collective-permute-start | bytes 786440 | tf_op jit(solution)/shard_map/ppermute | solution.py:143
  62.8 2.8 %hidden.6.refs_2_ = bf16[256,512]{1,0:T(8,128)(2,1)S(1)} custom-call(s32[1]{0:T(128)} %bitcast.1.me_ref, s32[12,128]{1,0:T(8,128)S(1)} %pad_add_fusion.own_names_ref, s32[12,128]{1,0:T(8,128)S(1)} %collective-permute-done.6.other_names_ref, bf16[2048,512]{1,0:T(8,128)(2,1)S(1)} %bitcast.8, bf16[2048,512]{1,0:T(8,128)(2,1)S(1)} %bitcast.13, ...), custom_call_target="tpu_custom_call" | custom-call | flops 1073741824 | bytes 5505024 | tf_op jit(solution)/shard_map/hidden/pallas_call | solution.py:47
  66.2 1.7 %hidden.7.refs_4_ = bf16[256,512]{1,0:T(8,128)(2,1)S(1)} custom-call(s32[1]{0:T(128)} %bitcast.1.me_ref, s32[12,128]{1,0:T(8,128)S(1)} %pad_add_fusion.own_names_ref, s32[12,128]{1,0:T(8,128)S(1)} %collective-permute-done.6.other_names_ref, bf16[2048,512]{1,0:T(8,128)(2,1)S(1)} %bitcast.9, bf16[2048,512]{1,0:T(8,128)(2,1)S(1)} %bitcast.14, ...), custom_call_target="tpu_custom_call" | custom-call | flops 1073741824 | bytes 5505024 | tf_op jit(solution)/shard_map/hidden/pallas_call | solution.py:47
  67.9 1.6 %collective-permute-start.18 = (bf16[256,512]{1,0:T(8,128)(2,1)S(1)}, bf16[256,512]{1,0:T(8,128)(2,1)}, u32[]{:S(2)}, u32[]{:S(2)}) collective-permute-start(bf16[256,512]{1,0:T(8,128)(2,1)S(1)} %hidden.7.refs_4_), channel_id=1, source_target_pairs={{0,8},{8,0},{1,9},{9,1},{2,10},{10,2},{3,11},{11,3},{4,12},{12,4},... | collective-permute-start | bytes 786440 | tf_op jit(solution)/shard_map/ppermute | solution.py:143
  72.4 1.6 %collective-permute-start.26 = (bf16[128,512]{1,0:T(8,128)(2,1)S(1)}, bf16[128,512]{1,0:T(8,128)(2,1)S(1)}, u32[]{:S(2)}, u32[]{:S(2)}) collective-permute-start(bf16[128,512]{1,0:T(8,128)(2,1)S(1)} %hidden.9.refs_0_), channel_id=1, source_target_pairs={{0,8},{8,0},{1,9},{9,1},{2,10},{10,2},{3,11},{11,3},{4,12},{12,4},... | collective-permute-start | bytes 393224 | tf_op jit(solution)/shard_map/ppermute | solution.py:143
  75.0 8.3 %collective-permute-done.22.refs_7_ = bf16[128,512]{1,0:T(8,128)(2,1)S(1)} collective-permute-done((bf16[128,512]{1,0:T(8,128)(2,1)S(1)}, bf16[128,512]{1,0:T(8,128)(2,1)S(1)}, u32[]{:S(2)}, u32[]{:S(2)}) %collective-permute-start.22) | collective-permute-done | bytes 131104 | tf_op jit(solution)/shard_map/ppermute | solution.py:143
  83.3 2.5 %partial_gram.1.early_ref = f32[512,512]{1,0:T(8,128)S(1)} custom-call(bf16[256,512]{1,0:T(8,128)(2,1)} %hidden.5.refs_0_, bf16[256,512]{1,0:T(8,128)(2,1)} %collective-permute-done.2.refs_1_, bf16[256,512]{1,0:T(8,128)(2,1)S(1)} %hidden.6.refs_2_, bf16[256,512]{1,0:T(8,128)(2,1)} %collective-permute-done.12.refs_3_, bf16[256,512]{1,0:T(8,128)(2,1)S(1)} %hidden.7.refs_4_, ...), custom_call_target="tpu_custom_call" | custom-call | flops 939524096 | bytes 2883584 | tf_op jit(solution)/shard_map/partial_gram/pallas_call | solution.py:78
  85.8 34.2 %factor.1 = f32[256,512]{1,0:T(8,128)} custom-call(s32[1]{0:T(128)} %bitcast.rank_ref, f32[512,512]{1,0:T(8,128)S(1)} %partial_gram.1.early_ref, bf16[128,512]{1,0:T(8,128)(2,1)S(1)} %hidden.9.refs_0_, bf16[128,512]{1,0:T(8,128)(2,1)S(1)} %collective-permute-done.26.refs_1_), custom_call_target="tpu_custom_call" | custom-call | tf_op jit(solution)/shard_map/factor/pallas_call | solution.py:303
  (58 shorter events, 18.9 us)
Async XLA Ops:
  1.1 18.5 %collective-permute-start.10 = (bf16[64,2048]{1,0:T(8,128)(2,1)S(1)}, bf16[64,2048]{1,0:T(8,128)(2,1)S(1)}, u32[]{:S(2)}, u32[]{:S(2)}) collective-permute-start(bf16[64,2048]{1,0:T(8,128)(2,1)S(1)} %get-tuple-element.5), channel_id=1, source_target_pairs={{6,4},{7,5},{4,2},{5,3},{2,0},{3,1},{14,12},{15,13},{12,10},{13,11... | collective-permute-start | bytes 786440 | tf_op jit(solution)/shard_map/ppermute | solution.py:136
  3.6 18.0 %collective-permute-start.9 = (bf16[64,2048]{1,0:T(8,128)(2,1)S(1)}, bf16[64,2048]{1,0:T(8,128)(2,1)}, u32[]{:S(2)}, u32[]{:S(2)}) collective-permute-start(bf16[64,2048]{1,0:T(8,128)(2,1)S(1)} %get-tuple-element.5), channel_id=1, source_target_pairs={{0,2},{1,3},{2,4},{3,5},{4,6},{5,7},{8,10},{9,11},{10,12},{11,13},... | collective-permute-start | bytes 786440 | tf_op jit(solution)/shard_map/ppermute | solution.py:136
  4.9 8.1 %collective-permute-start.3 = (s32[4,128]{1,0:T(4,128)}, s32[4,128]{1,0:T(4,128)S(1)}, u32[]{:S(2)}, u32[]{:S(2)}) collective-permute-start(s32[4,128]{1,0:T(4,128)} %bitcast.17), channel_id=1, source_target_pairs={{0,6},{1,7},{2,0},{3,1},{4,2},{5,3},{6,4},{7,5},{8,14},{9,15},{10,... | collective-permute-start | bytes 6152 | tf_op jit(solution)/shard_map/ppermute | solution.py:136
  7.6 15.3 %collective-permute-start.8 = (bf16[64,2048]{1,0:T(8,128)(2,1)S(1)}, bf16[64,2048]{1,0:T(8,128)(2,1)}, u32[]{:S(2)}, u32[]{:S(2)}) collective-permute-start(bf16[64,2048]{1,0:T(8,128)(2,1)S(1)} %get-tuple-element.6), channel_id=1, source_target_pairs={{6,4},{7,5},{4,2},{5,3},{2,0},{3,1},{14,12},{15,13},{12,10},{13,11... | collective-permute-start | bytes 786440 | tf_op jit(solution)/shard_map/ppermute | solution.py:136
  10.7 13.0 %collective-permute-start.7 = (bf16[64,2048]{1,0:T(8,128)(2,1)S(1)}, bf16[64,2048]{1,0:T(8,128)(2,1)}, u32[]{:S(2)}, u32[]{:S(2)}) collective-permute-start(bf16[64,2048]{1,0:T(8,128)(2,1)S(1)} %get-tuple-element.6), channel_id=1, source_target_pairs={{0,2},{1,3},{2,4},{3,5},{4,6},{5,7},{8,10},{9,11},{10,12},{11,13},... | collective-permute-start | bytes 786440 | tf_op jit(solution)/shard_map/ppermute | solution.py:136
  19.6 23.8 %collective-permute-start.1 = (bf16[128,2048]{1,0:T(8,128)(2,1)}, bf16[128,2048]{1,0:T(8,128)(2,1)}, u32[]{:S(2)}, u32[]{:S(2)}) collective-permute-start(bf16[128,2048]{1,0:T(8,128)(2,1)} %refs_0_.1), channel_id=1, source_target_pairs={{0,1},{1,0},{2,3},{3,2},{4,5},{5,4},{6,7},{7,6},{8,9},{9,8},{10,11... | collective-permute-start | bytes 1572872 | tf_op jit(solution)/shard_map/ppermute | solution.py:139
  21.7 11.6 %collective-permute-start.15 = (bf16[64,2048]{1,0:T(8,128)(2,1)}, bf16[64,2048]{1,0:T(8,128)(2,1)}, u32[]{:S(2)}, u32[]{:S(2)}) collective-permute-start(bf16[64,2048]{1,0:T(8,128)(2,1)} %collective-permute-done.9.refs_2_), channel_id=1, source_target_pairs={{2,4},{3,5},{4,6},{5,7},{10,12},{11,13},{12,14},{13,15},{18,20},{1... | collective-permute-start | bytes 786440 | tf_op jit(solution)/shard_map/ppermute | solution.py:136
  23.0 10.3 %collective-permute-start.14 = (bf16[64,2048]{1,0:T(8,128)(2,1)}, bf16[64,2048]{1,0:T(8,128)(2,1)S(1)}, u32[]{:S(2)}, u32[]{:S(2)}) collective-permute-start(bf16[64,2048]{1,0:T(8,128)(2,1)} %collective-permute-done.8.refs_1_), channel_id=1, source_target_pairs={{4,2},{5,3},{2,0},{3,1},{12,10},{13,11},{10,8},{11,9},{20,18},{21,... | collective-permute-start | bytes 786440 | tf_op jit(solution)/shard_map/ppermute | solution.py:136
  23.7 15.7 %collective-permute-start.13 = (bf16[64,2048]{1,0:T(8,128)(2,1)}, bf16[64,2048]{1,0:T(8,128)(2,1)}, u32[]{:S(2)}, u32[]{:S(2)}) collective-permute-start(bf16[64,2048]{1,0:T(8,128)(2,1)} %collective-permute-done.7.refs_0_), channel_id=1, source_target_pairs={{2,4},{3,5},{4,6},{5,7},{10,12},{11,13},{12,14},{13,15},{18,20},{1... | collective-permute-start | bytes 786440 | tf_op jit(solution)/shard_map/ppermute | solution.py:136
  25.0 19.1 %collective-permute-start.24 = (bf16[64,2048]{1,0:T(8,128)(2,1)}, bf16[64,2048]{1,0:T(8,128)(2,1)}, u32[]{:S(2)}, u32[]{:S(2)}) collective-permute-start(bf16[64,2048]{1,0:T(8,128)(2,1)} %collective-permute-done.16.refs_5_.refs_2_), channel_id=1, source_target_pairs={{2,0},{3,1},{10,8},{11,9},{18,16},{19,17},{26,24},{27,25}} | collective-permute-start | bytes 786440 | tf_op jit(solution)/shard_map/ppermute | solution.py:136
  33.3 29.5 %collective-permute-start.11 = (bf16[128,2048]{1,0:T(8,128)(2,1)S(1)}, bf16[128,2048]{1,0:T(8,128)(2,1)}, u32[]{:S(2)}, u32[]{:S(2)}) collective-permute-start(bf16[128,2048]{1,0:T(8,128)(2,1)S(1)} %pick.4.refs_0_), channel_id=1, source_target_pairs={{0,1},{1,0},{2,3},{3,2},{4,5},{5,4},{6,7},{7,6},{8,9},{9,8},{10,11... | collective-permute-start | bytes 1572872 | tf_op jit(solution)/shard_map/ppermute | solution.py:139
  33.3 8.4 %collective-permute-start.5 = (s32[4,128]{1,0:T(4,128)S(1)}, s32[4,128]{1,0:T(4,128)S(1)}, u32[]{:S(2)}, u32[]{:S(2)}) collective-permute-start(s32[4,128]{1,0:T(4,128)S(1)} %bitcast.19), channel_id=1, source_target_pairs={{0,4},{1,5},{2,6},{3,7},{4,0},{5,1},{6,2},{7,3},{8,12},{9,13},{10,... | collective-permute-start | bytes 6152 | tf_op jit(solution)/shard_map/ppermute | solution.py:136
  41.7 24.5 %collective-permute-start.17 = (bf16[128,2048]{1,0:T(8,128)(2,1)S(1)}, bf16[128,2048]{1,0:T(8,128)(2,1)S(1)}, u32[]{:S(2)}, u32[]{:S(2)}) collective-permute-start(bf16[128,2048]{1,0:T(8,128)(2,1)S(1)} %pick.5.refs_0_), channel_id=1, source_target_pairs={{0,1},{1,0},{2,3},{3,2},{4,5},{5,4},{6,7},{7,6},{8,9},{9,8},{10,11... | collective-permute-start | bytes 1572872 | tf_op jit(solution)/shard_map/ppermute | solution.py:139
  42.1 11.3 %collective-permute-start.23 = (bf16[64,2048]{1,0:T(8,128)(2,1)}, bf16[64,2048]{1,0:T(8,128)(2,1)S(1)}, u32[]{:S(2)}, u32[]{:S(2)}) collective-permute-start(bf16[64,2048]{1,0:T(8,128)(2,1)} %collective-permute-done.15.refs_3_.refs_1_), channel_id=1, source_target_pairs={{4,6},{5,7},{12,14},{13,15},{20,22},{21,23},{28,30},{29,31}} | collective-permute-start | bytes 786440 | tf_op jit(solution)/shard_map/ppermute | solution.py:136
  43.4 16.2 %collective-permute-start.20 = (bf16[64,2048]{1,0:T(8,128)(2,1)S(1)}, bf16[64,2048]{1,0:T(8,128)(2,1)S(1)}, u32[]{:S(2)}, u32[]{:S(2)}) collective-permute-start(bf16[64,2048]{1,0:T(8,128)(2,1)S(1)} %collective-permute-done.14.refs_2_), channel_id=1, source_target_pairs={{2,0},{3,1},{10,8},{11,9},{18,16},{19,17},{26,24},{27,25}} | collective-permute-start | bytes 786440 | tf_op jit(solution)/shard_map/ppermute | solution.py:136
  44.1 17.1 %collective-permute-start.19 = (bf16[64,2048]{1,0:T(8,128)(2,1)}, bf16[64,2048]{1,0:T(8,128)(2,1)S(1)}, u32[]{:S(2)}, u32[]{:S(2)}) collective-permute-start(bf16[64,2048]{1,0:T(8,128)(2,1)} %collective-permute-done.13.refs_0_.refs_1_), channel_id=1, source_target_pairs={{4,6},{5,7},{12,14},{13,15},{20,22},{21,23},{28,30},{29,31}} | collective-permute-start | bytes 786440 | tf_op jit(solution)/shard_map/ppermute | solution.py:136
  53.4 9.1 %collective-permute-start.6 = (s32[12,128]{1,0:T(8,128)S(1)}, s32[12,128]{1,0:T(8,128)S(1)}, u32[]{:S(2)}, u32[]{:S(2)}) collective-permute-start(s32[12,128]{1,0:T(8,128)S(1)} %pad_add_fusion.own_names_ref), channel_id=1, source_target_pairs={{0,1},{1,0},{2,3},{3,2},{4,5},{5,4},{6,7},{7,6},{8,9},{9,8},{10,11... | collective-permute-start | bytes 18440 | tf_op jit(solution)/shard_map/ppermute | solution.py:139
  59.7 14.3 %collective-permute-start.2 = (bf16[256,512]{1,0:T(8,128)(2,1)}, bf16[256,512]{1,0:T(8,128)(2,1)}, u32[]{:S(2)}, u32[]{:S(2)}) collective-permute-start(bf16[256,512]{1,0:T(8,128)(2,1)} %hidden.5.refs_0_), channel_id=1, source_target_pairs={{0,8},{8,0},{1,9},{9,1},{2,10},{10,2},{3,11},{11,3},{4,12},{12,4},... | collective-permute-start | bytes 786440 | tf_op jit(solution)/shard_map/ppermute | solution.py:143
  61.2 10.0 %collective-permute-start.25 = (bf16[64,2048]{1,0:T(8,128)(2,1)S(1)}, bf16[64,2048]{1,0:T(8,128)(2,1)S(1)}, u32[]{:S(2)}, u32[]{:S(2)}) collective-permute-start(bf16[64,2048]{1,0:T(8,128)(2,1)S(1)} %pick.7.refs_0_), channel_id=1, source_target_pairs={{0,1},{1,0},{2,3},{3,2},{4,5},{5,4},{6,7},{7,6},{8,9},{9,8},{10,11... | collective-permute-start | bytes 786440 | tf_op jit(solution)/shard_map/ppermute | solution.py:139
  62.4 7.1 %collective-permute-start.21 = (bf16[64,2048]{1,0:T(8,128)(2,1)S(1)}, bf16[64,2048]{1,0:T(8,128)(2,1)S(1)}, u32[]{:S(2)}, u32[]{:S(2)}) collective-permute-start(bf16[64,2048]{1,0:T(8,128)(2,1)S(1)} %pick.6.refs_0_), channel_id=1, source_target_pairs={{0,1},{1,0},{2,3},{3,2},{4,5},{5,4},{6,7},{7,6},{8,9},{9,8},{10,11... | collective-permute-start | bytes 786440 | tf_op jit(solution)/shard_map/ppermute | solution.py:139
  65.6 9.3 %collective-permute-start.12 = (bf16[256,512]{1,0:T(8,128)(2,1)S(1)}, bf16[256,512]{1,0:T(8,128)(2,1)}, u32[]{:S(2)}, u32[]{:S(2)}) collective-permute-start(bf16[256,512]{1,0:T(8,128)(2,1)S(1)} %hidden.6.refs_2_), channel_id=1, source_target_pairs={{0,8},{8,0},{1,9},{9,1},{2,10},{10,2},{3,11},{11,3},{4,12},{12,4},... | collective-permute-start | bytes 786440 | tf_op jit(solution)/shard_map/ppermute | solution.py:143
  67.9 15.3 %collective-permute-start.18 = (bf16[256,512]{1,0:T(8,128)(2,1)S(1)}, bf16[256,512]{1,0:T(8,128)(2,1)}, u32[]{:S(2)}, u32[]{:S(2)}) collective-permute-start(bf16[256,512]{1,0:T(8,128)(2,1)S(1)} %hidden.7.refs_4_), channel_id=1, source_target_pairs={{0,8},{8,0},{1,9},{9,1},{2,10},{10,2},{3,11},{11,3},{4,12},{12,4},... | collective-permute-start | bytes 786440 | tf_op jit(solution)/shard_map/ppermute | solution.py:143
  70.7 12.6 %collective-permute-start.22 = (bf16[128,512]{1,0:T(8,128)(2,1)S(1)}, bf16[128,512]{1,0:T(8,128)(2,1)S(1)}, u32[]{:S(2)}, u32[]{:S(2)}) collective-permute-start(bf16[128,512]{1,0:T(8,128)(2,1)S(1)} %hidden.8.refs_6_), channel_id=1, source_target_pairs={{0,8},{8,0},{1,9},{9,1},{2,10},{10,2},{3,11},{11,3},{4,12},{12,4},... | collective-permute-start | bytes 393224 | tf_op jit(solution)/shard_map/ppermute | solution.py:143
  72.4 13.3 %collective-permute-start.26 = (bf16[128,512]{1,0:T(8,128)(2,1)S(1)}, bf16[128,512]{1,0:T(8,128)(2,1)S(1)}, u32[]{:S(2)}, u32[]{:S(2)}) collective-permute-start(bf16[128,512]{1,0:T(8,128)(2,1)S(1)} %hidden.9.refs_0_), channel_id=1, source_target_pairs={{0,8},{8,0},{1,9},{9,1},{2,10},{10,2},{3,11},{11,3},{4,12},{12,4},... | collective-permute-start | bytes 393224 | tf_op jit(solution)/shard_map/ppermute | solution.py:143
  (10 other events, 156.8 us)

commit v7 on v5

--- a/solution.py
+++ b/solution.py
@@ -99,9 +99,8 @@
     names = routes.T
     below = move(tokens, ring(1))
     above = move(tokens, ring(-1))
-    far = move(tokens, [(0, 2), (3, 1)])
-    on_up = move(below, [(2, 3)])
-    on_down = move(above, [(1, 0)])
+    on_up = move(below, [(1, 2), (2, 3)])
+    on_down = move(above, [(2, 1), (1, 0)])
     moved = []
     for pairs in [ring(1), ring(-1), ring(2)]:
         moved.append(move(names, pairs))
@@ -110,7 +109,7 @@
     other_moved = swap(moved)
 
     hiddens = []
-    for slot, own in enumerate([tokens, below, above, far + on_up + on_down]):
+    for slot, own in enumerate([tokens, below, above, on_up + on_down]):
         other = swap(own)
         if slot == 0:
             hidden = hidden_of(me, own, other, names, other_names, 0, top, gate_w, up_w)

time: 128 us -> 125 us (0.977)
  starting transfers between devices: 25.2 us -> 20.2 us
  waiting for transfers between devices: 52 us -> 55.5 us
  Pallas kernels: 47.5 us -> 44.1 us
  local copies, waits for them, and re-layouts: 2.64 us -> 4.91 us
    ppermute x8 -> x7, starting transfers between devices: 20.2 us -> 15 us  [gathered(): move = lambda x, pairs: lax.ppermute(x, 'expert', between_chips(pairs))]
    ppermute x4, waiting for transfers between devices: 9.56 us -> 12.9 us  [gathered(): lax.ppermute(x, 'dp', [(r, (r + s) % data_ranks) for r in range(data_rank...]
    pallas_call x4, Pallas kernels: 11.2 us -> 7.98 us  [hidden_of(): pl.pallas_call(functools.partial(hidden_kernel, at=at, top=top), in_specs...]
    unnamed x8 -> x12, local copies, waits for them, and re-layouts: 2.64 us -> 4.91 us
    ppermute x8 -> x7, waiting for transfers between devices: 41.3 us -> 41.2 us  [gathered(): move = lambda x, pairs: lax.ppermute(x, 'expert', between_chips(pairs))]
  transfers between devices with their start and end apart: 18 -> 17, of which waited for: 11 -> 10; matrix products, arithmetic and copies ran while one was open for 0% -> 0% of each run, Pallas kernels for 10% -> 8%
where the time goes in v7:
time: 125 us
  waiting for transfers between devices  55.5 us (44%)
  Pallas kernels  44.1 us (35%)
  starting transfers between devices  20.2 us (16%)
  local copies, waits for them, and re-layouts  4.91 us (4%)
    ppermute x7, waiting for transfers between devices, gathered(): move = lambda x, pairs: lax.ppermute(x, 'expert', between_chips(pairs))  41.2 us
    pallas_call x1, Pallas kernels, factor_rows(): pl.pallas_call(functools.partial(factor_kernel, rows_mean=rows_mean), in_...  34.2 us
    ppermute x7, starting transfers between devices, gathered(): move = lambda x, pairs: lax.ppermute(x, 'expert', between_chips(pairs))  15 us
    ppermute x4, waiting for transfers between devices, gathered(): lax.ppermute(x, 'dp', [(r, (r + s) % data_ranks) for r in range(data_rank...  12.9 us
    pallas_call x4, Pallas kernels, hidden_of(): pl.pallas_call(functools.partial(hidden_kernel, at=at, top=top), in_specs...  7.98 us
    unnamed x12, local copies, waits for them, and re-layouts  4.91 us
    ppermute x4, starting transfers between devices, gathered(): lax.ppermute(x, 'dp', [(r, (r + s) % data_ranks) for r in range(data_rank...  4.31 us
  transfers between devices with their start and end apart: 17, of which 10 were waited for; matrix products, arithmetic and copies ran while one was open for 0% of the time, Pallas kernels for 8%

profile of v7, /device:TPU:0, one launch (start us, length us, event | category | flops | bytes accessed | tf_op | source)
XLA Modules:
  0.0 125.0 jit_solution(5585906319485454294)
XLA Ops:
  0.0 5.1 %collective-permute-start.10 = (bf16[128,2048]{1,0:T(8,128)(2,1)}, bf16[128,2048]{1,0:T(8,128)(2,1)S(1)}, u32[]{:S(2)}, u32[]{:S(2)}) collective-permute-start(bf16[128,2048]{1,0:T(8,128)(2,1)} %own_ref.1), channel_id=1, source_target_pairs={{0,6},{1,7},{2,0},{3,1},{4,2},{5,3},{6,4},{7,5},{8,14},{9,15},{10,... | collective-permute-start | bytes 1572872 | tf_op jit(solution)/shard_map/ppermute | solution.py:94
  5.1 12.6 %collective-permute-done.10.own_ref = bf16[128,2048]{1,0:T(8,128)(2,1)S(1)} collective-permute-done((bf16[128,2048]{1,0:T(8,128)(2,1)}, bf16[128,2048]{1,0:T(8,128)(2,1)S(1)}, u32[]{:S(2)}, u32[]{:S(2)}) %collective-permute-start.10) | collective-permute-done | bytes 524320 | tf_op jit(solution)/shard_map/ppermute | solution.py:94
  17.7 1.3 %collective-permute-start.14 = (bf16[128,2048]{1,0:T(8,128)(2,1)S(1)}, bf16[128,2048]{1,0:T(8,128)(2,1)S(1)}, u32[]{:S(2)}, u32[]{:S(2)}) collective-permute-start(bf16[128,2048]{1,0:T(8,128)(2,1)S(1)} %collective-permute-done.10.own_ref), channel_id=1, source_target_pairs={{4,2},{5,3},{2,0},{3,1},{12,10},{13,11},{10,8},{11,9},{20,18},{21,... | collective-permute-start | bytes 1572872 | tf_op jit(solution)/shard_map/ppermute | solution.py:94
  19.0 9.7 %collective-permute-done.3.own_ref = bf16[128,2048]{1,0:T(8,128)(2,1)S(1)} collective-permute-done((bf16[128,2048]{1,0:T(8,128)(2,1)}, bf16[128,2048]{1,0:T(8,128)(2,1)S(1)}, u32[]{:S(2)}, u32[]{:S(2)}) %collective-permute-start.3) | collective-permute-done | bytes 524320 | tf_op jit(solution)/shard_map/ppermute | solution.py:94
  30.1 9.8 %collective-permute-done.14 = bf16[128,2048]{1,0:T(8,128)(2,1)S(1)} collective-permute-done((bf16[128,2048]{1,0:T(8,128)(2,1)S(1)}, bf16[128,2048]{1,0:T(8,128)(2,1)S(1)}, u32[]{:S(2)}, u32[]{:S(2)}) %collective-permute-start.14) | collective-permute-done | bytes 524320 | tf_op jit(solution)/shard_map/ppermute | solution.py:94
  40.1 4.3 %collective-permute-start.7 = (s32[4,128]{1,0:T(4,128)}, s32[4,128]{1,0:T(4,128)S(1)}, u32[]{:S(2)}, u32[]{:S(2)}) collective-permute-start(s32[4,128]{1,0:T(4,128)} %bitcast.14), channel_id=1, source_target_pairs={{0,4},{1,5},{2,6},{3,7},{4,0},{5,1},{6,2},{7,3},{8,12},{9,13},{10,... | collective-permute-start | bytes 6152 | tf_op jit(solution)/shard_map/ppermute | solution.py:94
  44.3 1.8 %collective-permute-done.7 = s32[4,128]{1,0:T(4,128)S(1)} collective-permute-done((s32[4,128]{1,0:T(4,128)}, s32[4,128]{1,0:T(4,128)S(1)}, u32[]{:S(2)}, u32[]{:S(2)}) %collective-permute-start.7) | collective-permute-done | bytes 2080 | tf_op jit(solution)/shard_map/ppermute | solution.py:94
  46.1 3.6 %collective-permute-start.6 = (s32[4,128]{1,0:T(4,128)}, s32[4,128]{1,0:T(4,128)S(1)}, u32[]{:S(2)}, u32[]{:S(2)}) collective-permute-start(s32[4,128]{1,0:T(4,128)} %bitcast.15), channel_id=1, source_target_pairs={{0,6},{1,7},{2,0},{3,1},{4,2},{5,3},{6,4},{7,5},{8,14},{9,15},{10,... | collective-permute-start | bytes 6152 | tf_op jit(solution)/shard_map/ppermute | solution.py:94
  49.7 1.5 %collective-permute-done.6 = s32[4,128]{1,0:T(4,128)S(1)} collective-permute-done((s32[4,128]{1,0:T(4,128)}, s32[4,128]{1,0:T(4,128)S(1)}, u32[]{:S(2)}, u32[]{:S(2)}) %collective-permute-start.6) | collective-permute-done | bytes 2080 | tf_op jit(solution)/shard_map/ppermute | solution.py:94
  51.4 5.7 %collective-permute-done.5 = s32[4,128]{1,0:T(4,128)S(1)} collective-permute-done((s32[4,128]{1,0:T(4,128)}, s32[4,128]{1,0:T(4,128)S(1)}, u32[]{:S(2)}, u32[]{:S(2)}) %collective-permute-start.5) | collective-permute-done | bytes 2080 | tf_op jit(solution)/shard_map/ppermute | solution.py:94
  57.1 1.4 %collective-permute-done.1.other_names_ref = s32[4,128]{1,0:T(4,128)S(1)} collective-permute-done((s32[4,128]{1,0:T(4,128)}, s32[4,128]{1,0:T(4,128)S(1)}, u32[]{:S(2)}, u32[]{:S(2)}) %collective-permute-start.1) | collective-permute-done | bytes 2080 | tf_op jit(solution)/shard_map/ppermute | solution.py:95
  58.7 1.6 %copy-done = bf16[1,2048,512]{2,1,0:T(8,128)(2,1)S(1)} copy-done((bf16[1,2048,512]{2,1,0:T(8,128)(2,1)S(1)}, bf16[1,2048,512]{2,1,0:T(8,128)(2,1)}, u32[]{:S(2)}) %copy-start) | copy-done | bytes 2097176
  60.2 1.6 %copy-done.2 = bf16[1,2048,512]{2,1,0:T(8,128)(2,1)S(1)} copy-done((bf16[1,2048,512]{2,1,0:T(8,128)(2,1)S(1)}, bf16[1,2048,512]{2,1,0:T(8,128)(2,1)}, u32[]{:S(2)}) %copy-start.2) | copy-done | bytes 2097176
  63.6 1.7 %hidden.4.refs_0_ = bf16[256,512]{1,0:T(8,128)(2,1)S(1)} custom-call(s32[1]{0:T(128)} %bitcast.1.me_ref, bf16[128,2048]{1,0:T(8,128)(2,1)S(1)} %copy-done.4, bf16[128,2048]{1,0:T(8,128)(2,1)S(1)} %collective-permute-done.other_ref, s32[4,128]{1,0:T(4,128)S(1)} %bitcast.18, s32[4,128]{1,0:T(4,128)S(1)} %collective-permute-done.1.other_names_ref, ...), custom_call_target="tpu_custom_call" | custom-call | flops 1073741824 | bytes 5505024 | tf_op jit(solution)/shard_map/hidden/pallas_call | solution.py:41
  65.3 1.6 %collective-permute-start.2 = (bf16[256,512]{1,0:T(8,128)(2,1)S(1)}, bf16[256,512]{1,0:T(8,128)(2,1)}, u32[]{:S(2)}, u32[]{:S(2)}) collective-permute-start(bf16[256,512]{1,0:T(8,128)(2,1)S(1)} %hidden.4.refs_0_), channel_id=1, source_target_pairs={{0,8},{8,0},{1,9},{9,1},{2,10},{10,2},{3,11},{11,3},{4,12},{12,4},... | collective-permute-start | bytes 786440 | tf_op jit(solution)/shard_map/ppermute | solution.py:96
  66.9 2.8 %hidden.6.refs_4_ = bf16[256,512]{1,0:T(8,128)(2,1)S(1)} custom-call(s32[1]{0:T(128)} %bitcast.1.me_ref, bf16[128,2048]{1,0:T(8,128)(2,1)S(1)} %collective-permute-done.10.own_ref, bf16[128,2048]{1,0:T(8,128)(2,1)} %collective-permute-done.11.other_ref, s32[12,128]{1,0:T(8,128)S(1)} %pad_add_fusion.own_names_ref, ...), custom_call_target="tpu_custom_call" | custom-call | flops 1073741824 | bytes 5505024 | tf_op jit(solution)/shard_map/hidden/pallas_call | solution.py:41
  70.3 1.7 %hidden.5.refs_2_ = bf16[256,512]{1,0:T(8,128)(2,1)S(1)} custom-call(s32[1]{0:T(128)} %bitcast.1.me_ref, bf16[128,2048]{1,0:T(8,128)(2,1)S(1)} %collective-permute-done.3.own_ref, bf16[128,2048]{1,0:T(8,128)(2,1)S(1)} %collective-permute-done.4.other_ref, s32[12,128]{1,0:T(8,128)S(1)} %pad_add_fusion.own_names_ref, ...), custom_call_target="tpu_custom_call" | custom-call | flops 1073741824 | bytes 5505024 | tf_op jit(solution)/shard_map/hidden/pallas_call | solution.py:41
  72.0 1.6 %collective-permute-start.9 = (bf16[256,512]{1,0:T(8,128)(2,1)S(1)}, bf16[256,512]{1,0:T(8,128)(2,1)S(1)}, u32[]{:S(2)}, u32[]{:S(2)}) collective-permute-start(bf16[256,512]{1,0:T(8,128)(2,1)S(1)} %hidden.5.refs_2_), channel_id=1, source_target_pairs={{0,8},{8,0},{1,9},{9,1},{2,10},{10,2},{3,11},{11,3},{4,12},{12,4},... | collective-permute-start | bytes 786440 | tf_op jit(solution)/shard_map/ppermute | solution.py:96
  73.6 1.7 %hidden.7.refs_0_ = bf16[256,512]{1,0:T(8,128)(2,1)S(1)} custom-call(s32[1]{0:T(128)} %bitcast.1.me_ref, bf16[128,2048]{1,0:T(8,128)(2,1)S(1)} %add.3.own_ref, bf16[128,2048]{1,0:T(8,128)(2,1)S(1)} %collective-permute-done.15.other_ref, s32[12,128]{1,0:T(8,128)S(1)} %pad_add_fusion.own_names_ref, s32[12,128]{1,0:T(8,128)S(1)} %collective-permute-done.8.other_names_ref, ...), custom_call_target="tpu_custom_call" | custom-call | flops 1073741824 | bytes 5505024 | tf_op jit(solution)/shard_map/hidden/pallas_call | solution.py:41
  75.9 4.2 %collective-permute-done.12.refs_5_ = bf16[256,512]{1,0:T(8,128)(2,1)S(1)} collective-permute-done((bf16[256,512]{1,0:T(8,128)(2,1)S(1)}, bf16[256,512]{1,0:T(8,128)(2,1)S(1)}, u32[]{:S(2)}, u32[]{:S(2)}) %collective-permute-start.12) | collective-permute-done | bytes 262176 | tf_op jit(solution)/shard_map/ppermute | solution.py:96
  80.2 5.6 %collective-permute-done.9.refs_3_ = bf16[256,512]{1,0:T(8,128)(2,1)S(1)} collective-permute-done((bf16[256,512]{1,0:T(8,128)(2,1)S(1)}, bf16[256,512]{1,0:T(8,128)(2,1)S(1)}, u32[]{:S(2)}, u32[]{:S(2)}) %collective-permute-start.9) | collective-permute-done | bytes 262176 | tf_op jit(solution)/shard_map/ppermute | solution.py:96
  85.8 2.0 %partial_gram.1.early_ref = f32[512,512]{1,0:T(8,128)S(1)} custom-call(bf16[256,512]{1,0:T(8,128)(2,1)S(1)} %hidden.4.refs_0_, bf16[256,512]{1,0:T(8,128)(2,1)} %collective-permute-done.2.refs_1_, bf16[256,512]{1,0:T(8,128)(2,1)S(1)} %hidden.5.refs_2_, bf16[256,512]{1,0:T(8,128)(2,1)S(1)} %collective-permute-done.9.refs_3_, ...), custom_call_target="tpu_custom_call" | custom-call | flops 805306368 | bytes 2621440 | tf_op jit(solution)/shard_map/partial_gram/pallas_call | solution.py:71
  87.7 3.0 %collective-permute-done.16.refs_1_ = bf16[256,512]{1,0:T(8,128)(2,1)S(1)} collective-permute-done((bf16[256,512]{1,0:T(8,128)(2,1)S(1)}, bf16[256,512]{1,0:T(8,128)(2,1)S(1)}, u32[]{:S(2)}, u32[]{:S(2)}) %collective-permute-start.16) | collective-permute-done | bytes 262176 | tf_op jit(solution)/shard_map/ppermute | solution.py:96
  90.8 34.2 %factor.1 = f32[256,512]{1,0:T(8,128)} custom-call(s32[1]{0:T(128)} %bitcast.rank_ref, f32[512,512]{1,0:T(8,128)S(1)} %partial_gram.1.early_ref, bf16[256,512]{1,0:T(8,128)(2,1)S(1)} %hidden.7.refs_0_, bf16[256,512]{1,0:T(8,128)(2,1)S(1)} %collective-permute-done.16.refs_1_), custom_call_target="tpu_custom_call" | custom-call | tf_op jit(solution)/shard_map/factor/pallas_call | solution.py:234
  (30 shorter events, 4.8 us)
Async XLA Ops:
  0.0 17.7 %collective-permute-start.10 = (bf16[128,2048]{1,0:T(8,128)(2,1)}, bf16[128,2048]{1,0:T(8,128)(2,1)S(1)}, u32[]{:S(2)}, u32[]{:S(2)}) collective-permute-start(bf16[128,2048]{1,0:T(8,128)(2,1)} %own_ref.1), channel_id=1, source_target_pairs={{0,6},{1,7},{2,0},{3,1},{4,2},{5,3},{6,4},{7,5},{8,14},{9,15},{10,... | collective-permute-start | bytes 1572872 | tf_op jit(solution)/shard_map/ppermute | solution.py:94
  5.1 23.7 %collective-permute-start.3 = (bf16[128,2048]{1,0:T(8,128)(2,1)}, bf16[128,2048]{1,0:T(8,128)(2,1)S(1)}, u32[]{:S(2)}, u32[]{:S(2)}) collective-permute-start(bf16[128,2048]{1,0:T(8,128)(2,1)} %own_ref.1), channel_id=1, source_target_pairs={{0,2},{1,3},{2,4},{3,5},{4,6},{5,7},{6,0},{7,1},{8,10},{9,11},{10,... | collective-permute-start | bytes 1572872 | tf_op jit(solution)/shard_map/ppermute | solution.py:94
  17.7 22.2 %collective-permute-start.14 = (bf16[128,2048]{1,0:T(8,128)(2,1)S(1)}, bf16[128,2048]{1,0:T(8,128)(2,1)S(1)}, u32[]{:S(2)}, u32[]{:S(2)}) collective-permute-start(bf16[128,2048]{1,0:T(8,128)(2,1)S(1)} %collective-permute-done.10.own_ref), channel_id=1, source_target_pairs={{4,2},{5,3},{2,0},{3,1},{12,10},{13,11},{10,8},{11,9},{20,18},{21,... | collective-permute-start | bytes 1572872 | tf_op jit(solution)/shard_map/ppermute | solution.py:94
  28.7 11.1 %collective-permute-start.13 = (bf16[128,2048]{1,0:T(8,128)(2,1)S(1)}, bf16[128,2048]{1,0:T(8,128)(2,1)S(1)}, u32[]{:S(2)}, u32[]{:S(2)}) collective-permute-start(bf16[128,2048]{1,0:T(8,128)(2,1)S(1)} %collective-permute-done.3.own_ref), channel_id=1, source_target_pairs={{2,4},{3,5},{4,6},{5,7},{10,12},{11,13},{12,14},{13,15},{18,20},{1... | collective-permute-start | bytes 1572872 | tf_op jit(solution)/shard_map/ppermute | solution.py:94
  29.4 29.2 %collective-permute-start = (bf16[128,2048]{1,0:T(8,128)(2,1)}, bf16[128,2048]{1,0:T(8,128)(2,1)S(1)}, u32[]{:S(2)}, u32[]{:S(2)}) collective-permute-start(bf16[128,2048]{1,0:T(8,128)(2,1)} %own_ref.1), channel_id=1, source_target_pairs={{0,1},{1,0},{2,3},{3,2},{4,5},{5,4},{6,7},{7,6},{8,9},{9,8},{10,11... | collective-permute-start | bytes 1572872 | tf_op jit(solution)/shard_map/ppermute | solution.py:95
  29.5 37.4 %collective-permute-start.11 = (bf16[128,2048]{1,0:T(8,128)(2,1)S(1)}, bf16[128,2048]{1,0:T(8,128)(2,1)}, u32[]{:S(2)}, u32[]{:S(2)}) collective-permute-start(bf16[128,2048]{1,0:T(8,128)(2,1)S(1)} %collective-permute-done.10.own_ref), channel_id=1, source_target_pairs={{0,1},{1,0},{2,3},{3,2},{4,5},{5,4},{6,7},{7,6},{8,9},{9,8},{10,11... | collective-permute-start | bytes 1572872 | tf_op jit(solution)/shard_map/ppermute | solution.py:95
  30.0 40.3 %collective-permute-start.4 = (bf16[128,2048]{1,0:T(8,128)(2,1)S(1)}, bf16[128,2048]{1,0:T(8,128)(2,1)S(1)}, u32[]{:S(2)}, u32[]{:S(2)}) collective-permute-start(bf16[128,2048]{1,0:T(8,128)(2,1)S(1)} %collective-permute-done.3.own_ref), channel_id=1, source_target_pairs={{0,1},{1,0},{2,3},{3,2},{4,5},{5,4},{6,7},{7,6},{8,9},{9,8},{10,11... | collective-permute-start | bytes 1572872 | tf_op jit(solution)/shard_map/ppermute | solution.py:95
  40.0 33.6 %collective-permute-start.15 = (bf16[128,2048]{1,0:T(8,128)(2,1)S(1)}, bf16[128,2048]{1,0:T(8,128)(2,1)S(1)}, u32[]{:S(2)}, u32[]{:S(2)}) collective-permute-start(bf16[128,2048]{1,0:T(8,128)(2,1)S(1)} %add.3.own_ref), channel_id=1, source_target_pairs={{0,1},{1,0},{2,3},{3,2},{4,5},{5,4},{6,7},{7,6},{8,9},{9,8},{10,11... | collective-permute-start | bytes 1572872 | tf_op jit(solution)/shard_map/ppermute | solution.py:95
  40.1 6.0 %collective-permute-start.7 = (s32[4,128]{1,0:T(4,128)}, s32[4,128]{1,0:T(4,128)S(1)}, u32[]{:S(2)}, u32[]{:S(2)}) collective-permute-start(s32[4,128]{1,0:T(4,128)} %bitcast.14), channel_id=1, source_target_pairs={{0,4},{1,5},{2,6},{3,7},{4,0},{5,1},{6,2},{7,3},{8,12},{9,13},{10,... | collective-permute-start | bytes 6152 | tf_op jit(solution)/shard_map/ppermute | solution.py:94
  46.1 5.1 %collective-permute-start.6 = (s32[4,128]{1,0:T(4,128)}, s32[4,128]{1,0:T(4,128)S(1)}, u32[]{:S(2)}, u32[]{:S(2)}) collective-permute-start(s32[4,128]{1,0:T(4,128)} %bitcast.15), channel_id=1, source_target_pairs={{0,6},{1,7},{2,0},{3,1},{4,2},{5,3},{6,4},{7,5},{8,14},{9,15},{10,... | collective-permute-start | bytes 6152 | tf_op jit(solution)/shard_map/ppermute | solution.py:94
  51.3 5.8 %collective-permute-start.5 = (s32[4,128]{1,0:T(4,128)}, s32[4,128]{1,0:T(4,128)S(1)}, u32[]{:S(2)}, u32[]{:S(2)}) collective-permute-start(s32[4,128]{1,0:T(4,128)} %bitcast.16), channel_id=1, source_target_pairs={{0,2},{1,3},{2,4},{3,5},{4,6},{5,7},{6,0},{7,1},{8,10},{9,11},{10,... | collective-permute-start | bytes 6152 | tf_op jit(solution)/shard_map/ppermute | solution.py:94
  57.1 1.4 %collective-permute-start.1 = (s32[4,128]{1,0:T(4,128)}, s32[4,128]{1,0:T(4,128)S(1)}, u32[]{:S(2)}, u32[]{:S(2)}) collective-permute-start(s32[4,128]{1,0:T(4,128)} %bitcast.17), channel_id=1, source_target_pairs={{0,1},{1,0},{2,3},{3,2},{4,5},{5,4},{6,7},{7,6},{8,9},{9,8},{10,11... | collective-permute-start | bytes 6152 | tf_op jit(solution)/shard_map/ppermute | solution.py:95
  58.5 8.4 %collective-permute-start.8 = (s32[12,128]{1,0:T(8,128)S(1)}, s32[12,128]{1,0:T(8,128)S(1)}, u32[]{:S(2)}, u32[]{:S(2)}) collective-permute-start(s32[12,128]{1,0:T(8,128)S(1)} %pad_add_fusion.own_names_ref), channel_id=1, source_target_pairs={{0,1},{1,0},{2,3},{3,2},{4,5},{5,4},{6,7},{7,6},{8,9},{9,8},{10,11... | collective-permute-start | bytes 18440 | tf_op jit(solution)/shard_map/ppermute | solution.py:95
  58.7 1.6 %copy-start = (bf16[1,2048,512]{2,1,0:T(8,128)(2,1)S(1)}, bf16[1,2048,512]{2,1,0:T(8,128)(2,1)}, u32[]{:S(2)}) copy-start(bf16[1,2048,512]{2,1,0:T(8,128)(2,1)} %param.6) | copy-start | bytes 6291460
  60.2 1.6 %copy-start.2 = (bf16[1,2048,512]{2,1,0:T(8,128)(2,1)S(1)}, bf16[1,2048,512]{2,1,0:T(8,128)(2,1)}, u32[]{:S(2)}) copy-start(bf16[1,2048,512]{2,1,0:T(8,128)(2,1)} %param.7) | copy-start | bytes 6291460
  61.8 1.0 copy-start.4
  62.9 0.7 copy-start.5
  63.6 3.3 %copy-start.1 = (bf16[1,2048,512]{2,1,0:T(8,128)(2,1)S(1)}, bf16[1,2048,512]{2,1,0:T(8,128)(2,1)}, u32[]{:S(2)}) copy-start(bf16[1,2048,512]{2,1,0:T(8,128)(2,1)} %param.6) | copy-start | bytes 6291460
  63.6 3.3 %copy-start.3 = (bf16[1,2048,512]{2,1,0:T(8,128)(2,1)S(1)}, bf16[1,2048,512]{2,1,0:T(8,128)(2,1)}, u32[]{:S(2)}) copy-start(bf16[1,2048,512]{2,1,0:T(8,128)(2,1)} %param.7) | copy-start | bytes 6291460
  65.3 10.6 %collective-permute-start.2 = (bf16[256,512]{1,0:T(8,128)(2,1)S(1)}, bf16[256,512]{1,0:T(8,128)(2,1)}, u32[]{:S(2)}, u32[]{:S(2)}) collective-permute-start(bf16[256,512]{1,0:T(8,128)(2,1)S(1)} %hidden.4.refs_0_), channel_id=1, source_target_pairs={{0,8},{8,0},{1,9},{9,1},{2,10},{10,2},{3,11},{11,3},{4,12},{12,4},... | collective-permute-start | bytes 786440 | tf_op jit(solution)/shard_map/ppermute | solution.py:96
  69.7 10.5 %collective-permute-start.12 = (bf16[256,512]{1,0:T(8,128)(2,1)S(1)}, bf16[256,512]{1,0:T(8,128)(2,1)S(1)}, u32[]{:S(2)}, u32[]{:S(2)}) collective-permute-start(bf16[256,512]{1,0:T(8,128)(2,1)S(1)} %hidden.6.refs_4_), channel_id=1, source_target_pairs={{0,8},{8,0},{1,9},{9,1},{2,10},{10,2},{3,11},{11,3},{4,12},{12,4},... | collective-permute-start | bytes 786440 | tf_op jit(solution)/shard_map/ppermute | solution.py:96
  72.0 13.8 %collective-permute-start.9 = (bf16[256,512]{1,0:T(8,128)(2,1)S(1)}, bf16[256,512]{1,0:T(8,128)(2,1)S(1)}, u32[]{:S(2)}, u32[]{:S(2)}) collective-permute-start(bf16[256,512]{1,0:T(8,128)(2,1)S(1)} %hidden.5.refs_2_), channel_id=1, source_target_pairs={{0,8},{8,0},{1,9},{9,1},{2,10},{10,2},{3,11},{11,3},{4,12},{12,4},... | collective-permute-start | bytes 786440 | tf_op jit(solution)/shard_map/ppermute | solution.py:96
  75.3 15.5 %collective-permute-start.16 = (bf16[256,512]{1,0:T(8,128)(2,1)S(1)}, bf16[256,512]{1,0:T(8,128)(2,1)S(1)}, u32[]{:S(2)}, u32[]{:S(2)}) collective-permute-start(bf16[256,512]{1,0:T(8,128)(2,1)S(1)} %hidden.7.refs_0_), channel_id=1, source_target_pairs={{0,8},{8,0},{1,9},{9,1},{2,10},{10,2},{3,11},{11,3},{4,12},{12,4},... | collective-permute-start | bytes 786440 | tf_op jit(solution)/shard_map/ppermute | solution.py:96

commit v8 on v7

--- a/solution.py
+++ b/solution.py
@@ -164,31 +164,66 @@
     return jnp.concatenate([column] * (width // column.shape[1]), axis=1)
 
 
-def factor_panel(x, columns, sublane):
-    rows, width = x.shape
-    factor = jnp.zeros_like(x)
-    for k in range(rows):
-        scale = lax.rsqrt(jnp.broadcast_to(columns[k][k : k + 1, :], columns[k].shape))
-        lower = columns[k] * scale
-        upper = jnp.broadcast_to(x[k : k + 1, :], x.shape) * over_lanes(scale, width)
-        factor = jnp.where(sublane == k, upper, factor)
-        for j in range(k + 1, rows):
-            columns[j] = columns[j] - lower * jnp.broadcast_to(lower[j : j + 1, :], lower.shape)
-        if k + 1 < rows:
-            x = x - over_lanes(lower, width) * upper
-    return factor
-
-
-def outer_sum(a, b):
-    return lax.dot_general(
-        a, b, (((0,), (0,)), ((), ())), precision=lax.Precision.HIGHEST, preferred_element_type=jnp.float32
-    )
+def row_of(x, k):
+    return jnp.broadcast_to(x[k : k + 1, :], x.shape)
+
+
+def lane_of(x, at):
+    return jnp.take_along_axis(x, jnp.full(x.shape, at, jnp.int32), axis=1, mode="promise_in_bounds")
+
+
+PRODUCTS = ((0, 0), (0, 1), (1, 0), (0, 2), (2, 0), (1, 1))
+
+
+def three_parts(x):
+    high = x.astype(jnp.bfloat16).astype(jnp.float32)
+    rest = x - high
+    middle = rest.astype(jnp.bfloat16).astype(jnp.float32)
+    return high, middle, rest - middle
+
+
+def outer_of_few(a, b):
+    left, right = three_parts(a), three_parts(b)
+    left = jnp.concatenate([left[i] for i, _ in PRODUCTS], axis=0)
+    right = jnp.concatenate([right[j] for _, j in PRODUCTS], axis=0).astype(jnp.bfloat16)
+    return jnp.dot(left.T.astype(jnp.bfloat16), right, preferred_element_type=jnp.float32)
+
+
+def outer_of_many(a, b):
+    left, right = three_parts(a.T), three_parts(b)
+    left = jnp.concatenate([left[i].astype(jnp.bfloat16) for i, _ in PRODUCTS], axis=1)
+    right = jnp.concatenate([right[j].astype(jnp.bfloat16) for _, j in PRODUCTS], axis=0)
+    return jnp.dot(left, right, preferred_element_type=jnp.float32)
+
+
+def factor_panel(rows, columns, sublane):
+    group, width = rows[0].shape
+    count = len(rows)
+    done = []
+    for s in range(count):
+        factor = jnp.zeros_like(rows[s])
+        for k in range(group):
+            pivot = columns[s][s][k]
+            scale = lax.rsqrt(row_of(pivot, k))
+            lower = {t: columns[t][s][k] * scale for t in range(s, count)}
+            upper = row_of(rows[s], k) * over_lanes(scale, width)
+            factor = jnp.where(sublane == k, upper, factor)
+            for u in range(s, count):
+                for j in range(k + 1 if u == s else 0, group):
+                    entry = row_of(lower[u], j)
+                    for t in range(u, count):
+                        columns[t][u][j] = columns[t][u][j] - lower[t] * entry
+            for t in range(s if k + 1 < group else s + 1, count):
+                rows[t] = rows[t] - over_lanes(lower[t], width) * upper
+        done.append(factor)
+    return done
 
 
 def factor_kernel(rank_ref, early_ref, *refs, rows_mean):
     late_refs, (my_rows_ref, out_ref, rest_ref) = refs[:-3], refs[-3:]
     size = early_ref.shape[0]
-    block, panel = 128, 8
+    block, group, groups = 128, 8, 4
+    panel = group * groups
     row = lax.broadcasted_iota(jnp.int32, (size, size), 0)
     col = lax.broadcasted_iota(jnp.int32, (size, size), 1)
     gram = early_ref[...]
@@ -200,30 +235,30 @@
         end = base + block
         if base:
             out_ref[base:end, :base] = jnp.zeros((block, base), jnp.float32)
-        sublane = lax.broadcasted_iota(jnp.int32, (panel, width), 0)
-        lane = lax.broadcasted_iota(jnp.int32, (panel, width), 1)
+        sublane = lax.broadcasted_iota(jnp.int32, (group, width), 0)
+        lane = lax.broadcasted_iota(jnp.int32, (group, width), 1)
+        panel_lane = lax.broadcasted_iota(jnp.int32, (panel, block), 1)
 
         def step(p, carry):
             first = panel * p
-            rows = pl.ds(pl.multiple_of(base + first, panel), panel)
-            x = rest_ref[rows, base:]
-            corner = x[:, :block]
+            at = [pl.ds(pl.multiple_of(base + first + group * t, group), group) for t in range(groups)]
+            rows = [rest_ref[at[t], base:] for t in range(groups)]
             columns = [
-                jnp.take_along_axis(
-                    corner, jnp.full(corner.shape, first + j, jnp.int32), axis=1, mode="promise_in_bounds"
-                )
-                for j in range(panel)
+                [[lane_of(rows[t][:, :block], first + group * u + j) for j in range(group)] for u in range(t + 1)]
+                for t in range(groups)
             ]
-            factor = factor_panel(x, columns, sublane)
-            out_ref[rows, base:] = jnp.where(lane >= sublane + first, factor, 0.0)
-            below = jnp.where(lane[:, :block] >= first + panel, factor[:, :block], 0.0)
-            rest_ref[base:end, base:] -= outer_sum(below, factor)
+            done = factor_panel(rows, columns, sublane)
+            for t in range(groups):
+                out_ref[at[t], base:] = jnp.where(lane >= sublane + first + group * t, done[t], 0.0)
+            done = jnp.concatenate(done, axis=0)
+            below = jnp.where(panel_lane >= first + panel, done[:, :block], 0.0)
+            rest_ref[base:end, base:] -= outer_of_few(below, done)
             return carry
 
         lax.fori_loop(0, block // panel, step, 0)
-        if end < size:
-            done = out_ref[base:end, end:]
-            rest_ref[end:, end:] -= outer_sum(done, done)
+        for to in range(end, size, block):
+            right = out_ref[base:end, to:]
+            rest_ref[to : to + block, to:] -= outer_of_many(right[:, :block], right)
     count = my_rows_ref.shape[0]
     my_rows_ref[...] = out_ref[pl.ds(pl.multiple_of(rank_ref[0] * count, count), count), :]
 

time: 125 us -> 107 us (0.86)
  Pallas kernels: 44.1 us -> 25.7 us
    pallas_call x1, Pallas kernels: 34.2 us -> 15.8 us  [factor_rows(): pl.pallas_call(functools.partial(factor_kernel, rows_mean=rows_mean), in_...]
  transfers between devices with their start and end apart: 17 -> 17, of which waited for: 10 -> 10; matrix products, arithmetic and copies ran while one was open for 0% -> 0% of each run, Pallas kernels for 8% -> 9%
where the time goes in v8:
time: 107 us
  waiting for transfers between devices  55.5 us (52%)
  Pallas kernels  25.7 us (24%)
  starting transfers between devices  20.2 us (19%)
  local copies, waits for them, and re-layouts  4.91 us (5%)
    ppermute x7, waiting for transfers between devices, gathered(): move = lambda x, pairs: lax.ppermute(x, 'expert', between_chips(pairs))  41.2 us
    pallas_call x1, Pallas kernels, factor_rows(): pl.pallas_call(functools.partial(factor_kernel, rows_mean=rows_mean), in_...  15.8 us
    ppermute x7, starting transfers between devices, gathered(): move = lambda x, pairs: lax.ppermute(x, 'expert', between_chips(pairs))  15 us
    ppermute x4, waiting for transfers between devices, gathered(): lax.ppermute(x, 'dp', [(r, (r + s) % data_ranks) for r in range(data_rank...  12.9 us
    pallas_call x4, Pallas kernels, hidden_of(): pl.pallas_call(functools.partial(hidden_kernel, at=at, top=top), in_specs...  7.98 us
    unnamed x12, local copies, waits for them, and re-layouts  4.91 us
    ppermute x4, starting transfers between devices, gathered(): lax.ppermute(x, 'dp', [(r, (r + s) % data_ranks) for r in range(data_rank...  4.31 us
  transfers between devices with their start and end apart: 17, of which 10 were waited for; matrix products, arithmetic and copies ran while one was open for 0% of the time, Pallas kernels for 9%

profile of v8, /device:TPU:0, one launch (start us, length us, event | category | flops | bytes accessed | tf_op | source)
XLA Modules:
  0.0 106.5 jit_solution(11120327422243291583)
XLA Ops:
  0.0 5.1 %collective-permute-start.10 = (bf16[128,2048]{1,0:T(8,128)(2,1)}, bf16[128,2048]{1,0:T(8,128)(2,1)S(1)}, u32[]{:S(2)}, u32[]{:S(2)}) collective-permute-start(bf16[128,2048]{1,0:T(8,128)(2,1)} %own_ref.1), channel_id=1, source_target_pairs={{0,6},{1,7},{2,0},{3,1},{4,2},{5,3},{6,4},{7,5},{8,14},{9,15},{10,... | collective-permute-start | bytes 1572872 | tf_op jit(solution)/shard_map/ppermute | solution.py:94
  5.1 12.6 %collective-permute-done.10.own_ref = bf16[128,2048]{1,0:T(8,128)(2,1)S(1)} collective-permute-done((bf16[128,2048]{1,0:T(8,128)(2,1)}, bf16[128,2048]{1,0:T(8,128)(2,1)S(1)}, u32[]{:S(2)}, u32[]{:S(2)}) %collective-permute-start.10) | collective-permute-done | bytes 524320 | tf_op jit(solution)/shard_map/ppermute | solution.py:94
  17.7 1.3 %collective-permute-start.14 = (bf16[128,2048]{1,0:T(8,128)(2,1)S(1)}, bf16[128,2048]{1,0:T(8,128)(2,1)S(1)}, u32[]{:S(2)}, u32[]{:S(2)}) collective-permute-start(bf16[128,2048]{1,0:T(8,128)(2,1)S(1)} %collective-permute-done.10.own_ref), channel_id=1, source_target_pairs={{4,2},{5,3},{2,0},{3,1},{12,10},{13,11},{10,8},{11,9},{20,18},{21,... | collective-permute-start | bytes 1572872 | tf_op jit(solution)/shard_map/ppermute | solution.py:94
  19.0 9.7 %collective-permute-done.3.own_ref = bf16[128,2048]{1,0:T(8,128)(2,1)S(1)} collective-permute-done((bf16[128,2048]{1,0:T(8,128)(2,1)}, bf16[128,2048]{1,0:T(8,128)(2,1)S(1)}, u32[]{:S(2)}, u32[]{:S(2)}) %collective-permute-start.3) | collective-permute-done | bytes 524320 | tf_op jit(solution)/shard_map/ppermute | solution.py:94
  30.1 9.8 %collective-permute-done.14 = bf16[128,2048]{1,0:T(8,128)(2,1)S(1)} collective-permute-done((bf16[128,2048]{1,0:T(8,128)(2,1)S(1)}, bf16[128,2048]{1,0:T(8,128)(2,1)S(1)}, u32[]{:S(2)}, u32[]{:S(2)}) %collective-permute-start.14) | collective-permute-done | bytes 524320 | tf_op jit(solution)/shard_map/ppermute | solution.py:94
  40.1 4.3 %collective-permute-start.7 = (s32[4,128]{1,0:T(4,128)}, s32[4,128]{1,0:T(4,128)S(1)}, u32[]{:S(2)}, u32[]{:S(2)}) collective-permute-start(s32[4,128]{1,0:T(4,128)} %bitcast.14), channel_id=1, source_target_pairs={{0,4},{1,5},{2,6},{3,7},{4,0},{5,1},{6,2},{7,3},{8,12},{9,13},{10,... | collective-permute-start | bytes 6152 | tf_op jit(solution)/shard_map/ppermute | solution.py:94
  44.3 1.8 %collective-permute-done.7 = s32[4,128]{1,0:T(4,128)S(1)} collective-permute-done((s32[4,128]{1,0:T(4,128)}, s32[4,128]{1,0:T(4,128)S(1)}, u32[]{:S(2)}, u32[]{:S(2)}) %collective-permute-start.7) | collective-permute-done | bytes 2080 | tf_op jit(solution)/shard_map/ppermute | solution.py:94
  46.1 3.6 %collective-permute-start.6 = (s32[4,128]{1,0:T(4,128)}, s32[4,128]{1,0:T(4,128)S(1)}, u32[]{:S(2)}, u32[]{:S(2)}) collective-permute-start(s32[4,128]{1,0:T(4,128)} %bitcast.15), channel_id=1, source_target_pairs={{0,6},{1,7},{2,0},{3,1},{4,2},{5,3},{6,4},{7,5},{8,14},{9,15},{10,... | collective-permute-start | bytes 6152 | tf_op jit(solution)/shard_map/ppermute | solution.py:94
  49.7 1.5 %collective-permute-done.6 = s32[4,128]{1,0:T(4,128)S(1)} collective-permute-done((s32[4,128]{1,0:T(4,128)}, s32[4,128]{1,0:T(4,128)S(1)}, u32[]{:S(2)}, u32[]{:S(2)}) %collective-permute-start.6) | collective-permute-done | bytes 2080 | tf_op jit(solution)/shard_map/ppermute | solution.py:94
  51.4 5.7 %collective-permute-done.5 = s32[4,128]{1,0:T(4,128)S(1)} collective-permute-done((s32[4,128]{1,0:T(4,128)}, s32[4,128]{1,0:T(4,128)S(1)}, u32[]{:S(2)}, u32[]{:S(2)}) %collective-permute-start.5) | collective-permute-done | bytes 2080 | tf_op jit(solution)/shard_map/ppermute | solution.py:94
  57.1 1.4 %collective-permute-done.1.other_names_ref = s32[4,128]{1,0:T(4,128)S(1)} collective-permute-done((s32[4,128]{1,0:T(4,128)}, s32[4,128]{1,0:T(4,128)S(1)}, u32[]{:S(2)}, u32[]{:S(2)}) %collective-permute-start.1) | collective-permute-done | bytes 2080 | tf_op jit(solution)/shard_map/ppermute | solution.py:95
  58.7 1.6 %copy-done = bf16[1,2048,512]{2,1,0:T(8,128)(2,1)S(1)} copy-done((bf16[1,2048,512]{2,1,0:T(8,128)(2,1)S(1)}, bf16[1,2048,512]{2,1,0:T(8,128)(2,1)}, u32[]{:S(2)}) %copy-start) | copy-done | bytes 2097176
  60.2 1.6 %copy-done.2 = bf16[1,2048,512]{2,1,0:T(8,128)(2,1)S(1)} copy-done((bf16[1,2048,512]{2,1,0:T(8,128)(2,1)S(1)}, bf16[1,2048,512]{2,1,0:T(8,128)(2,1)}, u32[]{:S(2)}) %copy-start.2) | copy-done | bytes 2097176
  63.6 1.7 %hidden.4.refs_0_ = bf16[256,512]{1,0:T(8,128)(2,1)S(1)} custom-call(s32[1]{0:T(128)} %bitcast.1.me_ref, bf16[128,2048]{1,0:T(8,128)(2,1)S(1)} %copy-done.4, bf16[128,2048]{1,0:T(8,128)(2,1)S(1)} %collective-permute-done.other_ref, s32[4,128]{1,0:T(4,128)S(1)} %bitcast.18, s32[4,128]{1,0:T(4,128)S(1)} %collective-permute-done.1.other_names_ref, ...), custom_call_target="tpu_custom_call" | custom-call | flops 1073741824 | bytes 5505024 | tf_op jit(solution)/shard_map/hidden/pallas_call | solution.py:41
  65.3 1.6 %collective-permute-start.2 = (bf16[256,512]{1,0:T(8,128)(2,1)S(1)}, bf16[256,512]{1,0:T(8,128)(2,1)}, u32[]{:S(2)}, u32[]{:S(2)}) collective-permute-start(bf16[256,512]{1,0:T(8,128)(2,1)S(1)} %hidden.4.refs_0_), channel_id=1, source_target_pairs={{0,8},{8,0},{1,9},{9,1},{2,10},{10,2},{3,11},{11,3},{4,12},{12,4},... | collective-permute-start | bytes 786440 | tf_op jit(solution)/shard_map/ppermute | solution.py:96
  66.9 2.8 %hidden.6.refs_4_ = bf16[256,512]{1,0:T(8,128)(2,1)S(1)} custom-call(s32[1]{0:T(128)} %bitcast.1.me_ref, bf16[128,2048]{1,0:T(8,128)(2,1)S(1)} %collective-permute-done.10.own_ref, bf16[128,2048]{1,0:T(8,128)(2,1)} %collective-permute-done.11.other_ref, s32[12,128]{1,0:T(8,128)S(1)} %pad_add_fusion.own_names_ref, ...), custom_call_target="tpu_custom_call" | custom-call | flops 1073741824 | bytes 5505024 | tf_op jit(solution)/shard_map/hidden/pallas_call | solution.py:41
  70.3 1.7 %hidden.5.refs_2_ = bf16[256,512]{1,0:T(8,128)(2,1)S(1)} custom-call(s32[1]{0:T(128)} %bitcast.1.me_ref, bf16[128,2048]{1,0:T(8,128)(2,1)S(1)} %collective-permute-done.3.own_ref, bf16[128,2048]{1,0:T(8,128)(2,1)S(1)} %collective-permute-done.4.other_ref, s32[12,128]{1,0:T(8,128)S(1)} %pad_add_fusion.own_names_ref, ...), custom_call_target="tpu_custom_call" | custom-call | flops 1073741824 | bytes 5505024 | tf_op jit(solution)/shard_map/hidden/pallas_call | solution.py:41
  72.0 1.6 %collective-permute-start.9 = (bf16[256,512]{1,0:T(8,128)(2,1)S(1)}, bf16[256,512]{1,0:T(8,128)(2,1)S(1)}, u32[]{:S(2)}, u32[]{:S(2)}) collective-permute-start(bf16[256,512]{1,0:T(8,128)(2,1)S(1)} %hidden.5.refs_2_), channel_id=1, source_target_pairs={{0,8},{8,0},{1,9},{9,1},{2,10},{10,2},{3,11},{11,3},{4,12},{12,4},... | collective-permute-start | bytes 786440 | tf_op jit(solution)/shard_map/ppermute | solution.py:96
  73.6 1.7 %hidden.7.refs_0_ = bf16[256,512]{1,0:T(8,128)(2,1)S(1)} custom-call(s32[1]{0:T(128)} %bitcast.1.me_ref, bf16[128,2048]{1,0:T(8,128)(2,1)S(1)} %add.3.own_ref, bf16[128,2048]{1,0:T(8,128)(2,1)S(1)} %collective-permute-done.15.other_ref, s32[12,128]{1,0:T(8,128)S(1)} %pad_add_fusion.own_names_ref, s32[12,128]{1,0:T(8,128)S(1)} %collective-permute-done.8.other_names_ref, ...), custom_call_target="tpu_custom_call" | custom-call | flops 1073741824 | bytes 5505024 | tf_op jit(solution)/shard_map/hidden/pallas_call | solution.py:41
  75.9 4.2 %collective-permute-done.12.refs_5_ = bf16[256,512]{1,0:T(8,128)(2,1)S(1)} collective-permute-done((bf16[256,512]{1,0:T(8,128)(2,1)S(1)}, bf16[256,512]{1,0:T(8,128)(2,1)S(1)}, u32[]{:S(2)}, u32[]{:S(2)}) %collective-permute-start.12) | collective-permute-done | bytes 262176 | tf_op jit(solution)/shard_map/ppermute | solution.py:96
  80.2 5.6 %collective-permute-done.9.refs_3_ = bf16[256,512]{1,0:T(8,128)(2,1)S(1)} collective-permute-done((bf16[256,512]{1,0:T(8,128)(2,1)S(1)}, bf16[256,512]{1,0:T(8,128)(2,1)S(1)}, u32[]{:S(2)}, u32[]{:S(2)}) %collective-permute-start.9) | collective-permute-done | bytes 262176 | tf_op jit(solution)/shard_map/ppermute | solution.py:96
  85.8 2.0 %partial_gram.1.early_ref = f32[512,512]{1,0:T(8,128)S(1)} custom-call(bf16[256,512]{1,0:T(8,128)(2,1)S(1)} %hidden.4.refs_0_, bf16[256,512]{1,0:T(8,128)(2,1)} %collective-permute-done.2.refs_1_, bf16[256,512]{1,0:T(8,128)(2,1)S(1)} %hidden.5.refs_2_, bf16[256,512]{1,0:T(8,128)(2,1)S(1)} %collective-permute-done.9.refs_3_, ...), custom_call_target="tpu_custom_call" | custom-call | flops 805306368 | bytes 2621440 | tf_op jit(solution)/shard_map/partial_gram/pallas_call | solution.py:71
  87.7 3.0 %collective-permute-done.16.refs_1_ = bf16[256,512]{1,0:T(8,128)(2,1)S(1)} collective-permute-done((bf16[256,512]{1,0:T(8,128)(2,1)S(1)}, bf16[256,512]{1,0:T(8,128)(2,1)S(1)}, u32[]{:S(2)}, u32[]{:S(2)}) %collective-permute-start.16) | collective-permute-done | bytes 262176 | tf_op jit(solution)/shard_map/ppermute | solution.py:96
  90.8 15.8 %factor.1 = f32[256,512]{1,0:T(8,128)} custom-call(s32[1]{0:T(128)} %bitcast.rank_ref, f32[512,512]{1,0:T(8,128)S(1)} %partial_gram.1.early_ref, bf16[256,512]{1,0:T(8,128)(2,1)S(1)} %hidden.7.refs_0_, bf16[256,512]{1,0:T(8,128)(2,1)S(1)} %collective-permute-done.16.refs_1_), custom_call_target="tpu_custom_call" | custom-call | tf_op jit(solution)/shard_map/factor/pallas_call | solution.py:269
  (30 shorter events, 4.8 us)
Async XLA Ops:
  0.0 17.7 %collective-permute-start.10 = (bf16[128,2048]{1,0:T(8,128)(2,1)}, bf16[128,2048]{1,0:T(8,128)(2,1)S(1)}, u32[]{:S(2)}, u32[]{:S(2)}) collective-permute-start(bf16[128,2048]{1,0:T(8,128)(2,1)} %own_ref.1), channel_id=1, source_target_pairs={{0,6},{1,7},{2,0},{3,1},{4,2},{5,3},{6,4},{7,5},{8,14},{9,15},{10,... | collective-permute-start | bytes 1572872 | tf_op jit(solution)/shard_map/ppermute | solution.py:94
  5.1 23.7 %collective-permute-start.3 = (bf16[128,2048]{1,0:T(8,128)(2,1)}, bf16[128,2048]{1,0:T(8,128)(2,1)S(1)}, u32[]{:S(2)}, u32[]{:S(2)}) collective-permute-start(bf16[128,2048]{1,0:T(8,128)(2,1)} %own_ref.1), channel_id=1, source_target_pairs={{0,2},{1,3},{2,4},{3,5},{4,6},{5,7},{6,0},{7,1},{8,10},{9,11},{10,... | collective-permute-start | bytes 1572872 | tf_op jit(solution)/shard_map/ppermute | solution.py:94
  17.7 22.2 %collective-permute-start.14 = (bf16[128,2048]{1,0:T(8,128)(2,1)S(1)}, bf16[128,2048]{1,0:T(8,128)(2,1)S(1)}, u32[]{:S(2)}, u32[]{:S(2)}) collective-permute-start(bf16[128,2048]{1,0:T(8,128)(2,1)S(1)} %collective-permute-done.10.own_ref), channel_id=1, source_target_pairs={{4,2},{5,3},{2,0},{3,1},{12,10},{13,11},{10,8},{11,9},{20,18},{21,... | collective-permute-start | bytes 1572872 | tf_op jit(solution)/shard_map/ppermute | solution.py:94
  28.7 11.1 %collective-permute-start.13 = (bf16[128,2048]{1,0:T(8,128)(2,1)S(1)}, bf16[128,2048]{1,0:T(8,128)(2,1)S(1)}, u32[]{:S(2)}, u32[]{:S(2)}) collective-permute-start(bf16[128,2048]{1,0:T(8,128)(2,1)S(1)} %collective-permute-done.3.own_ref), channel_id=1, source_target_pairs={{2,4},{3,5},{4,6},{5,7},{10,12},{11,13},{12,14},{13,15},{18,20},{1... | collective-permute-start | bytes 1572872 | tf_op jit(solution)/shard_map/ppermute | solution.py:94
  29.4 29.2 %collective-permute-start = (bf16[128,2048]{1,0:T(8,128)(2,1)}, bf16[128,2048]{1,0:T(8,128)(2,1)S(1)}, u32[]{:S(2)}, u32[]{:S(2)}) collective-permute-start(bf16[128,2048]{1,0:T(8,128)(2,1)} %own_ref.1), channel_id=1, source_target_pairs={{0,1},{1,0},{2,3},{3,2},{4,5},{5,4},{6,7},{7,6},{8,9},{9,8},{10,11... | collective-permute-start | bytes 1572872 | tf_op jit(solution)/shard_map/ppermute | solution.py:95
  29.5 37.4 %collective-permute-start.11 = (bf16[128,2048]{1,0:T(8,128)(2,1)S(1)}, bf16[128,2048]{1,0:T(8,128)(2,1)}, u32[]{:S(2)}, u32[]{:S(2)}) collective-permute-start(bf16[128,2048]{1,0:T(8,128)(2,1)S(1)} %collective-permute-done.10.own_ref), channel_id=1, source_target_pairs={{0,1},{1,0},{2,3},{3,2},{4,5},{5,4},{6,7},{7,6},{8,9},{9,8},{10,11... | collective-permute-start | bytes 1572872 | tf_op jit(solution)/shard_map/ppermute | solution.py:95
  30.0 40.3 %collective-permute-start.4 = (bf16[128,2048]{1,0:T(8,128)(2,1)S(1)}, bf16[128,2048]{1,0:T(8,128)(2,1)S(1)}, u32[]{:S(2)}, u32[]{:S(2)}) collective-permute-start(bf16[128,2048]{1,0:T(8,128)(2,1)S(1)} %collective-permute-done.3.own_ref), channel_id=1, source_target_pairs={{0,1},{1,0},{2,3},{3,2},{4,5},{5,4},{6,7},{7,6},{8,9},{9,8},{10,11... | collective-permute-start | bytes 1572872 | tf_op jit(solution)/shard_map/ppermute | solution.py:95
  40.0 33.6 %collective-permute-start.15 = (bf16[128,2048]{1,0:T(8,128)(2,1)S(1)}, bf16[128,2048]{1,0:T(8,128)(2,1)S(1)}, u32[]{:S(2)}, u32[]{:S(2)}) collective-permute-start(bf16[128,2048]{1,0:T(8,128)(2,1)S(1)} %add.3.own_ref), channel_id=1, source_target_pairs={{0,1},{1,0},{2,3},{3,2},{4,5},{5,4},{6,7},{7,6},{8,9},{9,8},{10,11... | collective-permute-start | bytes 1572872 | tf_op jit(solution)/shard_map/ppermute | solution.py:95
  40.1 6.0 %collective-permute-start.7 = (s32[4,128]{1,0:T(4,128)}, s32[4,128]{1,0:T(4,128)S(1)}, u32[]{:S(2)}, u32[]{:S(2)}) collective-permute-start(s32[4,128]{1,0:T(4,128)} %bitcast.14), channel_id=1, source_target_pairs={{0,4},{1,5},{2,6},{3,7},{4,0},{5,1},{6,2},{7,3},{8,12},{9,13},{10,... | collective-permute-start | bytes 6152 | tf_op jit(solution)/shard_map/ppermute | solution.py:94
  46.1 5.1 %collective-permute-start.6 = (s32[4,128]{1,0:T(4,128)}, s32[4,128]{1,0:T(4,128)S(1)}, u32[]{:S(2)}, u32[]{:S(2)}) collective-permute-start(s32[4,128]{1,0:T(4,128)} %bitcast.15), channel_id=1, source_target_pairs={{0,6},{1,7},{2,0},{3,1},{4,2},{5,3},{6,4},{7,5},{8,14},{9,15},{10,... | collective-permute-start | bytes 6152 | tf_op jit(solution)/shard_map/ppermute | solution.py:94
  51.3 5.8 %collective-permute-start.5 = (s32[4,128]{1,0:T(4,128)}, s32[4,128]{1,0:T(4,128)S(1)}, u32[]{:S(2)}, u32[]{:S(2)}) collective-permute-start(s32[4,128]{1,0:T(4,128)} %bitcast.16), channel_id=1, source_target_pairs={{0,2},{1,3},{2,4},{3,5},{4,6},{5,7},{6,0},{7,1},{8,10},{9,11},{10,... | collective-permute-start | bytes 6152 | tf_op jit(solution)/shard_map/ppermute | solution.py:94
  57.1 1.4 %collective-permute-start.1 = (s32[4,128]{1,0:T(4,128)}, s32[4,128]{1,0:T(4,128)S(1)}, u32[]{:S(2)}, u32[]{:S(2)}) collective-permute-start(s32[4,128]{1,0:T(4,128)} %bitcast.17), channel_id=1, source_target_pairs={{0,1},{1,0},{2,3},{3,2},{4,5},{5,4},{6,7},{7,6},{8,9},{9,8},{10,11... | collective-permute-start | bytes 6152 | tf_op jit(solution)/shard_map/ppermute | solution.py:95
  58.5 8.4 %collective-permute-start.8 = (s32[12,128]{1,0:T(8,128)S(1)}, s32[12,128]{1,0:T(8,128)S(1)}, u32[]{:S(2)}, u32[]{:S(2)}) collective-permute-start(s32[12,128]{1,0:T(8,128)S(1)} %pad_add_fusion.own_names_ref), channel_id=1, source_target_pairs={{0,1},{1,0},{2,3},{3,2},{4,5},{5,4},{6,7},{7,6},{8,9},{9,8},{10,11... | collective-permute-start | bytes 18440 | tf_op jit(solution)/shard_map/ppermute | solution.py:95
  58.7 1.6 %copy-start = (bf16[1,2048,512]{2,1,0:T(8,128)(2,1)S(1)}, bf16[1,2048,512]{2,1,0:T(8,128)(2,1)}, u32[]{:S(2)}) copy-start(bf16[1,2048,512]{2,1,0:T(8,128)(2,1)} %param.6) | copy-start | bytes 6291460
  60.2 1.6 %copy-start.2 = (bf16[1,2048,512]{2,1,0:T(8,128)(2,1)S(1)}, bf16[1,2048,512]{2,1,0:T(8,128)(2,1)}, u32[]{:S(2)}) copy-start(bf16[1,2048,512]{2,1,0:T(8,128)(2,1)} %param.7) | copy-start | bytes 6291460
  61.8 1.0 copy-start.4
  62.9 0.7 copy-start.5
  63.6 3.3 %copy-start.1 = (bf16[1,2048,512]{2,1,0:T(8,128)(2,1)S(1)}, bf16[1,2048,512]{2,1,0:T(8,128)(2,1)}, u32[]{:S(2)}) copy-start(bf16[1,2048,512]{2,1,0:T(8,128)(2,1)} %param.6) | copy-start | bytes 6291460
  63.6 3.3 %copy-start.3 = (bf16[1,2048,512]{2,1,0:T(8,128)(2,1)S(1)}, bf16[1,2048,512]{2,1,0:T(8,128)(2,1)}, u32[]{:S(2)}) copy-start(bf16[1,2048,512]{2,1,0:T(8,128)(2,1)} %param.7) | copy-start | bytes 6291460
  65.3 10.6 %collective-permute-start.2 = (bf16[256,512]{1,0:T(8,128)(2,1)S(1)}, bf16[256,512]{1,0:T(8,128)(2,1)}, u32[]{:S(2)}, u32[]{:S(2)}) collective-permute-start(bf16[256,512]{1,0:T(8,128)(2,1)S(1)} %hidden.4.refs_0_), channel_id=1, source_target_pairs={{0,8},{8,0},{1,9},{9,1},{2,10},{10,2},{3,11},{11,3},{4,12},{12,4},... | collective-permute-start | bytes 786440 | tf_op jit(solution)/shard_map/ppermute | solution.py:96
  69.7 10.5 %collective-permute-start.12 = (bf16[256,512]{1,0:T(8,128)(2,1)S(1)}, bf16[256,512]{1,0:T(8,128)(2,1)S(1)}, u32[]{:S(2)}, u32[]{:S(2)}) collective-permute-start(bf16[256,512]{1,0:T(8,128)(2,1)S(1)} %hidden.6.refs_4_), channel_id=1, source_target_pairs={{0,8},{8,0},{1,9},{9,1},{2,10},{10,2},{3,11},{11,3},{4,12},{12,4},... | collective-permute-start | bytes 786440 | tf_op jit(solution)/shard_map/ppermute | solution.py:96
  72.0 13.8 %collective-permute-start.9 = (bf16[256,512]{1,0:T(8,128)(2,1)S(1)}, bf16[256,512]{1,0:T(8,128)(2,1)S(1)}, u32[]{:S(2)}, u32[]{:S(2)}) collective-permute-start(bf16[256,512]{1,0:T(8,128)(2,1)S(1)} %hidden.5.refs_2_), channel_id=1, source_target_pairs={{0,8},{8,0},{1,9},{9,1},{2,10},{10,2},{3,11},{11,3},{4,12},{12,4},... | collective-permute-start | bytes 786440 | tf_op jit(solution)/shard_map/ppermute | solution.py:96
  75.3 15.5 %collective-permute-start.16 = (bf16[256,512]{1,0:T(8,128)(2,1)S(1)}, bf16[256,512]{1,0:T(8,128)(2,1)S(1)}, u32[]{:S(2)}, u32[]{:S(2)}) collective-permute-start(bf16[256,512]{1,0:T(8,128)(2,1)S(1)} %hidden.7.refs_0_), channel_id=1, source_target_pairs={{0,8},{8,0},{1,9},{9,1},{2,10},{10,2},{3,11},{11,3},{4,12},{12,4},... | collective-permute-start | bytes 786440 | tf_op jit(solution)/shard_map/ppermute | solution.py:96
